TPU v7x, 32 devices: a whole 2x2x4 slice. The times are simulated.
32 devices in a mesh: dp: 16 (over z, y, core), ctx: 2 (over x).
Axes of the slice: x: 2, y: 2, z: 4, core: 2. Of those that a mesh axis runs over, the one named last changes fastest.
Arguments:
- tokens: bfloat16 [32, 1024, 1024], P('dp', 'ctx'), may hold values from -6 to 6
- segments: int32 [32, 1024], P('dp'), may hold values from 0 to 7, never falling along the last dimension, each value on 1 to 512 neighbouring positions
- cotangent: float32 [32, 1024, 1024], P('dp', 'ctx'), may hold values from -6 to 6
- w_q: bfloat16 [1024, 1024], P(('dp', 'ctx')), may hold values from -0.1875 to 0.1875
- w_k: bfloat16 [1024, 512], P(('dp', 'ctx')), may hold values from -0.1875 to 0.1875
- w_v: bfloat16 [1024, 512], P(('dp', 'ctx')), may hold values from -0.1875 to 0.1875
- w_o: bfloat16 [1024, 1024], P(('dp', 'ctx')), may hold values from -0.75 to 0.75
- w_gate: bfloat16 [1024, 4608], P(('dp', 'ctx')), may hold values from -0.1875 to 0.1875
- w_up: bfloat16 [1024, 4608], P(('dp', 'ctx')), may hold values from -0.1875 to 0.1875
- w_down: bfloat16 [4608, 1024], P(('dp', 'ctx')), may hold values from -0.09375 to 0.09375
- g_attn: float32 [1024], replicated, may hold values from 0.5 to 1.5
- g_q: float32 [64], replicated, may hold values from 0.5 to 1.5
- g_k: float32 [64], replicated, may hold values from 0.5 to 1.5
- g_ffn: float32 [1024], replicated, may hold values from 0.5 to 1.5
Outputs:
- output: bfloat16 [32, 1024, 1024], P('dp', 'ctx')
- input_grad: float32 [32, 1024, 1024], P('dp', 'ctx')
- grad_w_q: float32 [1024, 1024], P(('dp', 'ctx'))
- grad_w_k: float32 [1024, 512], P(('dp', 'ctx'))
- grad_w_v: float32 [1024, 512], P(('dp', 'ctx'))
- grad_w_o: float32 [1024, 1024], P(('dp', 'ctx'))
- grad_w_gate: float32 [1024, 4608], P(('dp', 'ctx'))
- grad_w_up: float32 [1024, 4608], P(('dp', 'ctx'))
- grad_w_down: float32 [4608, 1024], P(('dp', 'ctx'))
- grad_g_attn: float32 [1024], replicated
- grad_g_q: float32 [64], replicated
- grad_g_k: float32 [64], replicated
- grad_g_ffn: float32 [1024], replicated
Inputs may be any that keep to these rules, and one draw needn't show every extreme that they name: `segments`: segment numbers never fall along a sequence; each document has 1 to 512 tokens, and some document has exactly 512.
All inputs are finite; a program needn't handle non-finite values.
Results may differ from a plain program's by a relative error of at most 0.018.
Values may be sent and summed in bfloat16 or wider, within the bound.
A program may use at most 216 MiB of HBM per device.

v0:
```python
import jax
import jax.numpy as jnp
from jax import lax
from jax.sharding import PartitionSpec as P

epsilon = 1e-05
rope_base = 1000000.0


def doc_positions(seg_ids):
    token_index = jnp.arange(seg_ids.shape[0], dtype=jnp.int32)
    new_doc = jnp.concatenate([jnp.ones((1,), dtype=jnp.bool_), seg_ids[1:] != seg_ids[:-1]])
    doc_start = lax.cummax(jnp.where(new_doc, token_index, jnp.zeros_like(token_index)), axis=0)
    return token_index - doc_start


def rope_tables(positions, head_size):
    frequency = rope_base ** (-jnp.arange(0, head_size, 2, dtype=jnp.float32) / head_size)
    angles = positions.astype(jnp.float32)[:, None] * frequency[None, :]
    angles = jnp.concatenate([angles, angles], axis=-1)
    return (jnp.cos(angles), jnp.sin(angles))


def turn_half(field):
    half_dim = field.shape[-1] // 2
    return jnp.concatenate([-field[..., half_dim:], field[..., :half_dim]], axis=-1)


def unturn_half(field):
    half_dim = field.shape[-1] // 2
    return jnp.concatenate([field[..., half_dim:], -field[..., :half_dim]], axis=-1)


def scale_rows(field):
    return lax.rsqrt(jnp.mean(field * field, axis=-1, keepdims=True) + epsilon)


def norm_back(field, inverse, gain, incoming):
    scaled = incoming * gain
    shared = jnp.mean(field * scaled, axis=-1, keepdims=True)
    result = inverse * scaled - field * inverse**3 * shared
    gain_grad = jnp.sum((field * inverse * incoming).reshape(-1, field.shape[-1]), axis=0)
    return (result, gain_grad)


def forward(tok_block, seg_ids, weights, gain_set):
    w_q, w_k, w_v, w_o, w_gate, w_up, w_down = weights
    g_attn, g_q, g_k, g_ffn = gain_set
    tok_rows = tok_block.shape[0]
    seq_length = seg_ids.shape[0]
    head_size = g_q.shape[0]
    kv_width = w_k.shape[1]
    kv_heads = kv_width // head_size
    q_heads = w_q.shape[1] // head_size
    group_size = q_heads // kv_heads
    score_scale = head_size ** (-0.5)
    row_start = lax.axis_index("ctx") * tok_rows
    cos_table, sin_table = rope_tables(doc_positions(seg_ids), head_size)
    cos_rows = lax.dynamic_slice_in_dim(cos_table, row_start, tok_rows, 0)[:, None, :]
    sin_rows = lax.dynamic_slice_in_dim(sin_table, row_start, tok_rows, 0)[:, None, :]
    seg_rows = lax.dynamic_slice_in_dim(seg_ids, row_start, tok_rows, 0)
    x_float = tok_block.astype(jnp.float32)
    inv_one = scale_rows(x_float)
    normed = (x_float * inv_one * g_attn).astype(jnp.bfloat16)
    q_raw = jnp.dot(normed, w_q, preferred_element_type=jnp.float32).reshape(
        tok_rows, q_heads, head_size
    )
    k_raw = jnp.dot(normed, w_k, preferred_element_type=jnp.float32).reshape(
        tok_rows, kv_heads, head_size
    )
    v_raw = jnp.dot(normed, w_v, preferred_element_type=jnp.float32)
    inv_q = scale_rows(q_raw)
    inv_k = scale_rows(k_raw)
    q_normed = q_raw * inv_q * g_q
    k_normed = k_raw * inv_k * g_k
    queries = (q_normed * cos_rows + turn_half(q_normed) * sin_rows).astype(jnp.bfloat16)
    key_part = (k_normed * cos_rows + turn_half(k_normed) * sin_rows).astype(jnp.bfloat16)
    all_keys, all_values = (
        lax.all_gather(key_part.reshape(tok_rows, kv_width), "ctx", axis=0, tiled=True),
        lax.all_gather(v_raw.astype(jnp.bfloat16), "ctx", axis=0, tiled=True),
    )
    all_keys = all_keys.reshape(seq_length, kv_heads, head_size)
    all_values = all_values.reshape(seq_length, kv_heads, head_size)
    grouped = queries.reshape(tok_rows, kv_heads, group_size, head_size)
    scores = (
        jnp.einsum("qkgd,tkd->kgqt", grouped, all_keys, preferred_element_type=jnp.float32)
        * score_scale
    )
    query_pos = row_start + jnp.arange(tok_rows, dtype=jnp.int32)
    key_pos = jnp.arange(seq_length, dtype=jnp.int32)
    live_mask = (key_pos[None, :] <= query_pos[:, None]) & (seg_rows[:, None] == seg_ids[None, :])
    scores = jnp.where(live_mask, scores, -1000000000.0)
    row_top = jnp.max(scores, axis=-1, keepdims=True)
    log_total = row_top + jnp.log(jnp.sum(jnp.exp(scores - row_top), axis=-1, keepdims=True))
    attn_probs = jnp.exp(scores - log_total)
    probs_low = attn_probs.astype(jnp.bfloat16)
    attended = jnp.einsum(
        "kgqt,tkd->qkgd", probs_low, all_values, preferred_element_type=jnp.float32
    )
    attended = attended.reshape(tok_rows, q_heads * head_size).astype(jnp.bfloat16)
    hidden = x_float + jnp.dot(attended, w_o, preferred_element_type=jnp.float32)
    inv_two = scale_rows(hidden)
    normed_two = (hidden * inv_two * g_ffn).astype(jnp.bfloat16)
    gate_out = jnp.dot(normed_two, w_gate, preferred_element_type=jnp.float32)
    up_out = jnp.dot(normed_two, w_up, preferred_element_type=jnp.float32)
    hidden_act = (jax.nn.silu(gate_out) * up_out).astype(jnp.bfloat16)
    block_out = hidden + jnp.dot(hidden_act, w_down, preferred_element_type=jnp.float32)
    kept_state = {
        "x_float": x_float,
        "inv_one": inv_one,
        "normed": normed,
        "q_raw": q_raw,
        "k_raw": k_raw,
        "inv_q": inv_q,
        "inv_k": inv_k,
        "cos_rows": cos_rows,
        "sin_rows": sin_rows,
        "grouped": grouped,
        "all_keys": all_keys,
        "all_values": all_values,
        "attn_probs": attn_probs,
        "probs_low": probs_low,
        "attended": attended,
        "hidden": hidden,
        "inv_two": inv_two,
        "normed_two": normed_two,
        "gate_out": gate_out,
        "up_out": up_out,
        "hidden_act": hidden_act,
    }
    return (block_out, kept_state)


def backward(tok_block, seg_ids, grad_block, weights, gain_set):
    block_out, kept = forward(tok_block, seg_ids, weights, gain_set)
    w_q, w_k, w_v, w_o, w_gate, w_up, w_down = weights
    g_attn, g_q, g_k, g_ffn = gain_set
    tok_rows = tok_block.shape[0]
    seq_length = seg_ids.shape[0]
    head_size = g_q.shape[0]
    kv_width = w_k.shape[1]
    score_scale = head_size ** (-0.5)
    grad_low = grad_block.astype(jnp.bfloat16)
    d_act = jnp.einsum("td,fd->tf", grad_low, w_down, preferred_element_type=jnp.float32)
    gate_out = kept["gate_out"]
    sigmoid_g = jax.nn.sigmoid(gate_out)
    d_gate = (d_act * kept["up_out"] * sigmoid_g * (1.0 + gate_out * (1.0 - sigmoid_g))).astype(
        jnp.bfloat16
    )
    d_up = (d_act * gate_out * sigmoid_g).astype(jnp.bfloat16)
    d_normed_two = jnp.einsum(
        "tf,df->td", d_gate, w_gate, preferred_element_type=jnp.float32
    ) + jnp.einsum("tf,df->td", d_up, w_up, preferred_element_type=jnp.float32)
    back_two, grad_gffn = norm_back(kept["hidden"], kept["inv_two"], g_ffn, d_normed_two)
    d_hidden = grad_block + back_two
    d_hidden_low = d_hidden.astype(jnp.bfloat16)
    grouped = kept["grouped"]
    d_attended = jnp.einsum(
        "td,ed->te", d_hidden_low, w_o, preferred_element_type=jnp.float32
    ).astype(jnp.bfloat16)
    d_attended = d_attended.reshape(grouped.shape)
    attn_probs = kept["attn_probs"]
    d_probs = jnp.einsum(
        "qkgd,tkd->kgqt", d_attended, kept["all_values"], preferred_element_type=jnp.float32
    )
    row_delta = jnp.sum(attn_probs * d_probs, axis=-1, keepdims=True)
    d_scores = (attn_probs * (d_probs - row_delta)).astype(jnp.bfloat16)
    d_queries = (
        jnp.einsum("kgqt,tkd->qkgd", d_scores, kept["all_keys"], preferred_element_type=jnp.float32)
        * score_scale
    )
    d_keys_all = (
        jnp.einsum("kgqt,qkgd->tkd", d_scores, grouped, preferred_element_type=jnp.float32)
        * score_scale
    )
    d_values_all = jnp.einsum(
        "kgqt,qkgd->tkd", kept["probs_low"], d_attended, preferred_element_type=jnp.float32
    )
    d_keys, d_values = (
        lax.psum_scatter(
            d_keys_all.reshape(seq_length, kv_width).astype(jnp.bfloat16),
            "ctx",
            scatter_dimension=0,
            tiled=True,
        ).astype(jnp.float32),
        lax.psum_scatter(
            d_values_all.reshape(seq_length, kv_width).astype(jnp.bfloat16),
            "ctx",
            scatter_dimension=0,
            tiled=True,
        ).astype(jnp.float32),
    )
    cos_rows = kept["cos_rows"]
    sin_rows = kept["sin_rows"]
    d_queries = d_queries.reshape(kept["q_raw"].shape)
    d_keys = d_keys.reshape(kept["k_raw"].shape)
    dq_normed = d_queries * cos_rows + unturn_half(d_queries * sin_rows)
    dk_normed = d_keys * cos_rows + unturn_half(d_keys * sin_rows)
    dq_raw, grad_gq = norm_back(kept["q_raw"], kept["inv_q"], g_q, dq_normed)
    dk_raw, grad_gk = norm_back(kept["k_raw"], kept["inv_k"], g_k, dk_normed)
    dq_low = dq_raw.reshape(tok_rows, -1).astype(jnp.bfloat16)
    dk_low = dk_raw.reshape(tok_rows, kv_width).astype(jnp.bfloat16)
    dv_low = d_values.astype(jnp.bfloat16)
    d_normed = (
        jnp.einsum("te,ce->tc", dq_low, w_q, preferred_element_type=jnp.float32)
        + jnp.einsum("te,ce->tc", dk_low, w_k, preferred_element_type=jnp.float32)
        + jnp.einsum("te,ce->tc", dv_low, w_v, preferred_element_type=jnp.float32)
    )
    back_one, grad_gattn = norm_back(kept["x_float"], kept["inv_one"], g_attn, d_normed)
    grad_in = d_hidden + back_one
    operand_set = (
        kept["normed"],
        dq_low,
        dk_low,
        dv_low,
        kept["attended"],
        d_hidden_low,
        kept["normed_two"],
        d_gate,
        d_up,
        kept["hidden_act"],
        grad_low,
    )
    gain_grad_set = (grad_gattn, grad_gq, grad_gk, grad_gffn)
    return (grad_in, operand_set, gain_grad_set)


def per_device(
    tokens, segments, cotangent, w_q, w_k, w_v, w_o, w_gate, w_up, w_down, g_attn, g_q, g_k, g_ffn
):
    gain_set = (g_attn, g_q, g_k, g_ffn)
    dp_count = lax.axis_size("dp")

    def fetch_forward():
        return (
            lax.all_gather(w_q, ("dp", "ctx"), axis=0, tiled=True),
            lax.all_gather(w_k, ("dp", "ctx"), axis=0, tiled=True),
            lax.all_gather(w_v, ("dp", "ctx"), axis=0, tiled=True),
            lax.all_gather(w_o, ("dp", "ctx"), axis=0, tiled=True),
            lax.all_gather(w_gate, ("dp", "ctx"), axis=0, tiled=True),
            lax.all_gather(w_up, ("dp", "ctx"), axis=0, tiled=True),
            lax.all_gather(w_down, ("dp", "ctx"), axis=0, tiled=True),
        )

    def fetch_backward():
        return (
            lax.all_gather(w_q, ("dp", "ctx"), axis=0, tiled=True),
            lax.all_gather(w_k, ("dp", "ctx"), axis=0, tiled=True),
            lax.all_gather(w_v, ("dp", "ctx"), axis=0, tiled=True),
            lax.all_gather(w_o, ("dp", "ctx"), axis=0, tiled=True),
            lax.all_gather(w_gate, ("dp", "ctx"), axis=0, tiled=True),
            lax.all_gather(w_up, ("dp", "ctx"), axis=0, tiled=True),
            lax.all_gather(w_down, ("dp", "ctx"), axis=0, tiled=True),
        )

    def forward_step(totals, micro_item):
        block_out, kept_state = forward(micro_item[0], micro_item[1], fetch_forward(), gain_set)
        return (totals, block_out.astype(jnp.bfloat16))

    unused, outputs = lax.scan(forward_step, jnp.zeros((), jnp.float32), (tokens, segments))

    def backward_step(totals, micro_item):
        grad_in, operand_set, gain_grad_set = backward(
            micro_item[0], micro_item[1], micro_item[2], fetch_backward(), gain_set
        )
        gain_totals = tuple((left + right for left, right in zip(totals, gain_grad_set)))
        return (gain_totals, (grad_in, operand_set))

    start_gains = tuple((jnp.zeros(gain.shape, jnp.float32) for gain in gain_set))
    gain_totals, (input_grads, operands) = lax.scan(
        backward_step, start_gains, (tokens, segments, cotangent)
    )
    (
        normed_all,
        dq_all,
        dk_all,
        dv_all,
        attended_all,
        dhidden_all,
        normed_two_all,
        dgate_all,
        dup_all,
        act_all,
        gradlow_all,
    ) = operands
    grad_wq = jnp.einsum("mtc,mte->ce", normed_all, dq_all, preferred_element_type=jnp.float32)
    grad_wk = jnp.einsum("mtc,mte->ce", normed_all, dk_all, preferred_element_type=jnp.float32)
    grad_wv = jnp.einsum("mtc,mte->ce", normed_all, dv_all, preferred_element_type=jnp.float32)
    grad_wo = jnp.einsum(
        "mte,mtd->ed", attended_all, dhidden_all, preferred_element_type=jnp.float32
    )
    grad_gate = jnp.einsum(
        "mtd,mtf->df", normed_two_all, dgate_all, preferred_element_type=jnp.float32
    )
    grad_up = jnp.einsum("mtd,mtf->df", normed_two_all, dup_all, preferred_element_type=jnp.float32)
    grad_down = jnp.einsum("mtf,mtd->fd", act_all, gradlow_all, preferred_element_type=jnp.float32)
    weight_set = (grad_wq, grad_wk, grad_wv, grad_wo, grad_gate, grad_up, grad_down)
    split_set = [
        piece.reshape(dp_count, piece.shape[0] // dp_count, piece.shape[1]) for piece in weight_set
    ]
    received = (
        lax.all_to_all(
            split_set[0].astype(jnp.bfloat16), "dp", split_axis=0, concat_axis=0, tiled=True
        ).astype(jnp.float32),
        lax.all_to_all(
            split_set[1].astype(jnp.bfloat16), "dp", split_axis=0, concat_axis=0, tiled=True
        ).astype(jnp.float32),
        lax.all_to_all(
            split_set[2].astype(jnp.bfloat16), "dp", split_axis=0, concat_axis=0, tiled=True
        ).astype(jnp.float32),
        lax.all_to_all(
            split_set[3].astype(jnp.bfloat16), "dp", split_axis=0, concat_axis=0, tiled=True
        ).astype(jnp.float32),
        lax.all_to_all(
            split_set[4].astype(jnp.bfloat16), "dp", split_axis=0, concat_axis=0, tiled=True
        ).astype(jnp.float32),
        lax.all_to_all(
            split_set[5].astype(jnp.bfloat16), "dp", split_axis=0, concat_axis=0, tiled=True
        ).astype(jnp.float32),
        lax.all_to_all(
            split_set[6].astype(jnp.bfloat16), "dp", split_axis=0, concat_axis=0, tiled=True
        ).astype(jnp.float32),
    )
    summed = [jnp.sum(piece, axis=0) for piece in received]
    wq_part, wk_part, wv_part, wo_part, gate_part, up_part, down_part = (
        lax.psum_scatter(
            summed[0].astype(jnp.bfloat16), "ctx", scatter_dimension=0, tiled=True
        ).astype(jnp.float32),
        lax.psum_scatter(
            summed[1].astype(jnp.bfloat16), "ctx", scatter_dimension=0, tiled=True
        ).astype(jnp.float32),
        lax.psum_scatter(
            summed[2].astype(jnp.bfloat16), "ctx", scatter_dimension=0, tiled=True
        ).astype(jnp.float32),
        lax.psum_scatter(
            summed[3].astype(jnp.bfloat16), "ctx", scatter_dimension=0, tiled=True
        ).astype(jnp.float32),
        lax.psum_scatter(
            summed[4].astype(jnp.bfloat16), "ctx", scatter_dimension=0, tiled=True
        ).astype(jnp.float32),
        lax.psum_scatter(
            summed[5].astype(jnp.bfloat16), "ctx", scatter_dimension=0, tiled=True
        ).astype(jnp.float32),
        lax.psum_scatter(
            summed[6].astype(jnp.bfloat16), "ctx", scatter_dimension=0, tiled=True
        ).astype(jnp.float32),
    )
    gattn_sum, gq_sum, gk_sum, gffn_sum = lax.psum(
        (gain_totals[0], gain_totals[1], gain_totals[2], gain_totals[3]), ("dp", "ctx")
    )
    return (
        outputs,
        input_grads,
        wq_part,
        wk_part,
        wv_part,
        wo_part,
        gate_part,
        up_part,
        down_part,
        gattn_sum,
        gq_sum,
        gk_sum,
        gffn_sum,
    )


def solution(mesh):
    in_specs = (
        P("dp", "ctx", None),
        P("dp", None),
        P("dp", "ctx", None),
        P(("dp", "ctx"), None),
        P(("dp", "ctx"), None),
        P(("dp", "ctx"), None),
        P(("dp", "ctx"), None),
        P(("dp", "ctx"), None),
        P(("dp", "ctx"), None),
        P(("dp", "ctx"), None),
        P(),
        P(),
        P(),
        P(),
    )
    out_specs = (
        P("dp", "ctx", None),
        P("dp", "ctx", None),
        P(("dp", "ctx"), None),
        P(("dp", "ctx"), None),
        P(("dp", "ctx"), None),
        P(("dp", "ctx"), None),
        P(("dp", "ctx"), None),
        P(("dp", "ctx"), None),
        P(("dp", "ctx"), None),
        P(),
        P(),
        P(),
        P(),
    )
    return jax.shard_map(
        per_device, mesh=mesh, in_specs=in_specs, out_specs=out_specs, check_vma=False
    )
```

profile of v0, /device:TPU:0, one launch (start us, length us, event | category | flops | bytes accessed | tf_op | source)
XLA Modules:
  0.0 3387.4 jit_solution(7343474171399635428)
XLA Ops:
  14.6 1405.5 %while.58 = (s32[]{:T(128)}, f32[1024]{0:T(1024)}, f32[64]{0:T(128)}, f32[64]{0:T(128)}, f32[1024]{0:T(1024)}, /*index=5*/f32[2,512,1024]{2,1,0:T(8,128)}, bf16[...) while((s32[]{:T(128)}, f32[1024]{0:T(1024)}, ...), condition=%wide.region_30.31_spmd.clone, body=%wide.region_10.30_spmd.clone.sunk | while | flops 37359452160 | bytes 999380736 | solution.py:270
  17.5 58.2 %all-gather.39.cloned.1.call-done = bf16[1024,512]{1,0:T(8,128)(2,1)} async-done(((bf16[32,512]{1,0:T(8,128)(2,1)}), bf16[1024,512]{1,0:T(8,128)(2,1)}) %all-gather.39.cloned.1.call-update) | async-done | bytes 1048592 | tf_op jit(solution)/shard_map/while/body/eval_jaxpr/all_gather | solution.py:249
  80.5 51.2 %all-gather.43.cloned.1.call-done = bf16[1024,512]{1,0:T(8,128)(2,1)} async-done(((bf16[32,512]{1,0:T(8,128)(2,1)}), bf16[1024,512]{1,0:T(8,128)(2,1)}) %all-gather.43.cloned.1.call-update) | async-done | bytes 1048592 | tf_op jit(solution)/shard_map/while/body/eval_jaxpr/all_gather | solution.py:248
  156.5 57.5 %all-gather.47.cloned.1.call-done = bf16[1024,1024]{1,0:T(8,128)(2,1)} async-done(((bf16[32,1024]{1,0:T(8,128)(2,1)}), bf16[1024,1024]{1,0:T(8,128)(2,1)}) %all-gather.47.cloned.1.call-update) | async-done | bytes 2097168 | tf_op jit(solution)/shard_map/while/body/eval_jaxpr/all_gather | solution.py:247
  301.8 78.4 %all-gather.49.cloned.1.call-done = bf16[4608,1024]{1,0:T(8,128)(2,1)} async-done(((bf16[144,1024]{1,0:T(8,128)(2,1)}), bf16[4608,1024]{1,0:T(8,128)(2,1)}) %all-gather.49.cloned.1.call-update) | async-done | bytes 9437200 | tf_op jit(solution)/shard_map/while/body/eval_jaxpr/all_gather | solution.py:253
  391.8 72.5 %all-gather.51.cloned.1.call-done = bf16[1024,4608]{1,0:T(8,128)(2,1)} async-done(((bf16[32,4608]{1,0:T(8,128)(2,1)}), bf16[1024,4608]{1,0:T(8,128)(2,1)}) %all-gather.51.cloned.1.call-update) | async-done | bytes 9437200 | tf_op jit(solution)/shard_map/while/body/eval_jaxpr/all_gather | solution.py:252
  475.2 73.0 %all-gather.53.cloned.1.call-done = bf16[1024,4608]{1,0:T(8,128)(2,1)} async-done(((bf16[32,4608]{1,0:T(8,128)(2,1)}), bf16[1024,4608]{1,0:T(8,128)(2,1)}) %all-gather.53.cloned.1.call-update) | async-done | bytes 9437200 | tf_op jit(solution)/shard_map/while/body/eval_jaxpr/all_gather | solution.py:251
  719.0 55.3 %all-gather.39.cloned.1.call-done = bf16[1024,512]{1,0:T(8,128)(2,1)} async-done(((bf16[32,512]{1,0:T(8,128)(2,1)}), bf16[1024,512]{1,0:T(8,128)(2,1)}) %all-gather.39.cloned.1.call-update) | async-done | bytes 1048592 | tf_op jit(solution)/shard_map/while/body/eval_jaxpr/all_gather | solution.py:249
  779.1 51.2 %all-gather.43.cloned.1.call-done = bf16[1024,512]{1,0:T(8,128)(2,1)} async-done(((bf16[32,512]{1,0:T(8,128)(2,1)}), bf16[1024,512]{1,0:T(8,128)(2,1)}) %all-gather.43.cloned.1.call-update) | async-done | bytes 1048592 | tf_op jit(solution)/shard_map/while/body/eval_jaxpr/all_gather | solution.py:248
  854.9 57.5 %all-gather.47.cloned.1.call-done = bf16[1024,1024]{1,0:T(8,128)(2,1)} async-done(((bf16[32,1024]{1,0:T(8,128)(2,1)}), bf16[1024,1024]{1,0:T(8,128)(2,1)}) %all-gather.47.cloned.1.call-update) | async-done | bytes 2097168 | tf_op jit(solution)/shard_map/while/body/eval_jaxpr/all_gather | solution.py:247
  1000.3 78.2 %all-gather.49.cloned.1.call-done = bf16[4608,1024]{1,0:T(8,128)(2,1)} async-done(((bf16[144,1024]{1,0:T(8,128)(2,1)}), bf16[4608,1024]{1,0:T(8,128)(2,1)}) %all-gather.49.cloned.1.call-update) | async-done | bytes 9437200 | tf_op jit(solution)/shard_map/while/body/eval_jaxpr/all_gather | solution.py:253
  1090.1 72.5 %all-gather.51.cloned.1.call-done = bf16[1024,4608]{1,0:T(8,128)(2,1)} async-done(((bf16[32,4608]{1,0:T(8,128)(2,1)}), bf16[1024,4608]{1,0:T(8,128)(2,1)}) %all-gather.51.cloned.1.call-update) | async-done | bytes 9437200 | tf_op jit(solution)/shard_map/while/body/eval_jaxpr/all_gather | solution.py:252
  1173.6 72.9 %all-gather.53.cloned.1.call-done = bf16[1024,4608]{1,0:T(8,128)(2,1)} async-done(((bf16[32,4608]{1,0:T(8,128)(2,1)}), bf16[1024,4608]{1,0:T(8,128)(2,1)}) %all-gather.53.cloned.1.call-update) | async-done | bytes 9437200 | tf_op jit(solution)/shard_map/while/body/eval_jaxpr/all_gather | solution.py:251
  1611.2 152.6 %all-to-all-done.5 = bf16[16,64,4608]{2,1,0:T(8,128)(2,1)} async-done(((bf16[16,64,4608]{2,1,0:T(8,128)(2,1)}), bf16[16,64,4608]{2,1,0:T(8,128)(2,1)}, u32[]{:S(2)}, u32[]{:S(2)}) %all-to-all-start.5) | async-done | bytes 9437216 | tf_op jit(solution)/shard_map/all_to_all | solution.py:317
  1763.8 41.1 %all-to-all-start.4 = ((bf16[16,64,4608]{2,1,0:T(8,128)(2,1)}), bf16[16,64,4608]{2,1,0:T(8,128)(2,1)}, u32[]{:S(2)}, u32[]{:S(2)}) async-start(bf16[16,64,4608]{2,1,0:T(8,128)(2,1)} %bitcast.567), calls=%async_computation.10 | async-start | bytes 18874368 | tf_op jit(solution)/shard_map/all_to_all | solution.py:314
  1821.5 152.3 %all-to-all-done.4 = bf16[16,64,4608]{2,1,0:T(8,128)(2,1)} async-done(((bf16[16,64,4608]{2,1,0:T(8,128)(2,1)}), bf16[16,64,4608]{2,1,0:T(8,128)(2,1)}, u32[]{:S(2)}, u32[]{:S(2)}) %all-to-all-start.4) | async-done | bytes 9437216 | tf_op jit(solution)/shard_map/all_to_all | solution.py:314
  1973.8 40.7 %all-to-all-start.6 = ((bf16[16,288,1024]{2,1,0:T(8,128)(2,1)}), bf16[16,288,1024]{2,1,0:T(8,128)(2,1)}, u32[]{:S(2)}, u32[]{:S(2)}) async-start(bf16[16,288,1024]{2,1,0:T(8,128)(2,1)} %bitcast.566), calls=%async_computation.14 | async-start | bytes 18874368 | tf_op jit(solution)/shard_map/all_to_all | solution.py:320
  2037.0 146.5 %all-to-all-done.6 = bf16[16,288,1024]{2,1,0:T(8,128)(2,1)} async-done(((bf16[16,288,1024]{2,1,0:T(8,128)(2,1)}), bf16[16,288,1024]{2,1,0:T(8,128)(2,1)}, u32[]{:S(2)}, u32[]{:S(2)}) %all-to-all-start.6) | async-done | bytes 9437216 | tf_op jit(solution)/shard_map/all_to_all | solution.py:320
  2190.5 76.0 %all-reduce = (f32[1024]{0:T(1024)}, f32[64]{0:T(128)}, f32[64]{0:T(128)}, f32[1024]{0:T(1024)}) all-reduce(f32[1024]{0:T(1024)S(1)} %copy-done.56, f32[64]{0:T(128)S(1)} %copy-done.62, f32[64]{0:T(128)S(1)} %copy-done.65, f32[1024]{0:T(1024)S(1)} %copy-done.59), channel_id=1, replica_groups=mesh['dp'=16,'ctx'=2] {'dp','ctx'}, use_global_device_ids=true, to_apply=%region_45.46 | all-reduce | flops 2176 | bytes 17408 | tf_op jit(solution)/shard_map/psum | solution.py:348
  2279.4 1100.3 %while.57 = (s32[]{:T(128)}, bf16[2,512,1024]{2,1,0:T(8,128)(2,1)}, bf16[2,512,1024]{2,1,0:T(8,128)(2,1)S(1)}, f32[1024]{0:T(1024)S(1)}, bf16[32,512]{1,0:T(8,12...) while((s32[]{:T(128)}, bf16[2,512,1024]{2,1,0:T(8,128)(2,1)}, ...), condition=%wide.region_9.10_spmd, body=%wide.region_0.9_spmd.sunk | while | flops 19996454912 | bytes 331045184 | solution.py:260
  2281.3 56.4 %all-gather.19.cloned.1.call-done = bf16[1024,512]{1,0:T(8,128)(2,1)} async-done(((bf16[32,512]{1,0:T(8,128)(2,1)}), bf16[1024,512]{1,0:T(8,128)(2,1)}) %all-gather.19.cloned.1.call-update) | async-done | bytes 1048592 | tf_op jit(solution)/shard_map/while/body/eval_jaxpr/all_gather | solution.py:238
  2342.4 51.1 %all-gather.23.cloned.1.call-done = bf16[1024,512]{1,0:T(8,128)(2,1)} async-done(((bf16[32,512]{1,0:T(8,128)(2,1)}), bf16[1024,512]{1,0:T(8,128)(2,1)}) %all-gather.23.cloned.1.call-update) | async-done | bytes 1048592 | tf_op jit(solution)/shard_map/while/body/eval_jaxpr/all_gather | solution.py:237
  2417.7 57.5 %all-gather.27.cloned.1.call-done = bf16[1024,1024]{1,0:T(8,128)(2,1)} async-done(((bf16[32,1024]{1,0:T(8,128)(2,1)}), bf16[1024,1024]{1,0:T(8,128)(2,1)}) %all-gather.27.cloned.1.call-update) | async-done | bytes 2097168 | tf_op jit(solution)/shard_map/while/body/eval_jaxpr/all_gather | solution.py:236
  2561.3 79.8 %all-gather.33.cloned.1.call-done = bf16[1024,4608]{1,0:T(8,128)(2,1)} async-done(((bf16[32,4608]{1,0:T(8,128)(2,1)}), bf16[1024,4608]{1,0:T(8,128)(2,1)}) %all-gather.33.cloned.1.call-update) | async-done | bytes 9437200 | tf_op jit(solution)/shard_map/while/body/eval_jaxpr/all_gather | solution.py:240
  2652.7 72.2 %all-gather.31.cloned.1.call-done = bf16[4608,1024]{1,0:T(8,128)(2,1)} async-done(((bf16[144,1024]{1,0:T(8,128)(2,1)}), bf16[4608,1024]{1,0:T(8,128)(2,1)}) %all-gather.31.cloned.1.call-update) | async-done | bytes 9437200 | tf_op jit(solution)/shard_map/while/body/eval_jaxpr/all_gather | solution.py:242
  2724.9 84.0 %all-gather.35.cloned.1.call-done = bf16[1024,4608]{1,0:T(8,128)(2,1)} async-done(((bf16[32,4608]{1,0:T(8,128)(2,1)}), bf16[1024,4608]{1,0:T(8,128)(2,1)}) %all-gather.35.cloned.1.call-update) | async-done | bytes 9437200 | tf_op jit(solution)/shard_map/while/body/eval_jaxpr/all_gather | solution.py:241
  2832.1 54.8 %all-gather.19.cloned.1.call-done = bf16[1024,512]{1,0:T(8,128)(2,1)} async-done(((bf16[32,512]{1,0:T(8,128)(2,1)}), bf16[1024,512]{1,0:T(8,128)(2,1)}) %all-gather.19.cloned.1.call-update) | async-done | bytes 1048592 | tf_op jit(solution)/shard_map/while/body/eval_jaxpr/all_gather | solution.py:238
  2891.9 50.9 %all-gather.23.cloned.1.call-done = bf16[1024,512]{1,0:T(8,128)(2,1)} async-done(((bf16[32,512]{1,0:T(8,128)(2,1)}), bf16[1024,512]{1,0:T(8,128)(2,1)}) %all-gather.23.cloned.1.call-update) | async-done | bytes 1048592 | tf_op jit(solution)/shard_map/while/body/eval_jaxpr/all_gather | solution.py:237
  2967.0 57.7 %all-gather.27.cloned.1.call-done = bf16[1024,1024]{1,0:T(8,128)(2,1)} async-done(((bf16[32,1024]{1,0:T(8,128)(2,1)}), bf16[1024,1024]{1,0:T(8,128)(2,1)}) %all-gather.27.cloned.1.call-update) | async-done | bytes 2097168 | tf_op jit(solution)/shard_map/while/body/eval_jaxpr/all_gather | solution.py:236
  3110.6 79.8 %all-gather.33.cloned.1.call-done = bf16[1024,4608]{1,0:T(8,128)(2,1)} async-done(((bf16[32,4608]{1,0:T(8,128)(2,1)}), bf16[1024,4608]{1,0:T(8,128)(2,1)}) %all-gather.33.cloned.1.call-update) | async-done | bytes 9437200 | tf_op jit(solution)/shard_map/while/body/eval_jaxpr/all_gather | solution.py:240
  3202.0 72.2 %all-gather.31.cloned.1.call-done = bf16[4608,1024]{1,0:T(8,128)(2,1)} async-done(((bf16[144,1024]{1,0:T(8,128)(2,1)}), bf16[4608,1024]{1,0:T(8,128)(2,1)}) %all-gather.31.cloned.1.call-update) | async-done | bytes 9437200 | tf_op jit(solution)/shard_map/while/body/eval_jaxpr/all_gather | solution.py:242
  3274.2 84.0 %all-gather.35.cloned.1.call-done = bf16[1024,4608]{1,0:T(8,128)(2,1)} async-done(((bf16[32,4608]{1,0:T(8,128)(2,1)}), bf16[1024,4608]{1,0:T(8,128)(2,1)}) %all-gather.35.cloned.1.call-update) | async-done | bytes 9437200 | tf_op jit(solution)/shard_map/while/body/eval_jaxpr/all_gather | solution.py:241
  (670 shorter events, 1174.0 us)
Async XLA Ops:
  79.0 157.2 %all-gather.45.cloned.1.call-start = ((), (), s32[]{:S(2)}) async-start(), calls=%async_computation.36 | async-start | bytes 1572864 | tf_op jit(solution)/shard_map/while/body/eval_jaxpr/all_gather | solution.py:79
  138.5 157.5 %all-gather.37.cloned.1.call-start = ((), (), s32[]{:S(2)}) async-start(), calls=%async_computation.32 | async-start | bytes 2162688 | tf_op jit(solution)/shard_map/while/body/eval_jaxpr/all_gather | solution.py:250
  139.1 241.2 %all-gather.49.cloned.1.call-start = ((), (), s32[]{:S(2)}) async-start(), calls=%async_computation.38 | async-start | bytes 9732096 | tf_op jit(solution)/shard_map/while/body/eval_jaxpr/all_gather | solution.py:253
  139.8 324.4 %all-gather.51.cloned.1.call-start = ((), (), s32[]{:S(2)}) async-start(), calls=%async_computation.39 | async-start | bytes 9732096 | tf_op jit(solution)/shard_map/while/body/eval_jaxpr/all_gather | solution.py:252
  140.6 407.7 %all-gather.53.cloned.1.call-start = ((), (), s32[]{:S(2)}) async-start(), calls=%async_computation.40 | async-start | bytes 9732096 | tf_op jit(solution)/shard_map/while/body/eval_jaxpr/all_gather | solution.py:251
  141.3 554.9 %reduce-scatter.26.cloned.1.call-start = ((), (), s32[]{:S(2)}) async-start(), calls=%async_computation.42 | async-start | bytes 1572864 | tf_op jit(solution)/shard_map/while/body/eval_jaxpr/reduce_scatter | solution.py:180
  777.7 157.0 %all-gather.45.cloned.1.call-start = ((), (), s32[]{:S(2)}) async-start(), calls=%async_computation.36 | async-start | bytes 1572864 | tf_op jit(solution)/shard_map/while/body/eval_jaxpr/all_gather | solution.py:79
  837.1 157.4 %all-gather.37.cloned.1.call-start = ((), (), s32[]{:S(2)}) async-start(), calls=%async_computation.32 | async-start | bytes 2162688 | tf_op jit(solution)/shard_map/while/body/eval_jaxpr/all_gather | solution.py:250
  837.7 240.9 %all-gather.49.cloned.1.call-start = ((), (), s32[]{:S(2)}) async-start(), calls=%async_computation.38 | async-start | bytes 9732096 | tf_op jit(solution)/shard_map/while/body/eval_jaxpr/all_gather | solution.py:253
  838.3 324.3 %all-gather.51.cloned.1.call-start = ((), (), s32[]{:S(2)}) async-start(), calls=%async_computation.39 | async-start | bytes 9732096 | tf_op jit(solution)/shard_map/while/body/eval_jaxpr/all_gather | solution.py:252
  839.0 407.4 %all-gather.53.cloned.1.call-start = ((), (), s32[]{:S(2)}) async-start(), calls=%async_computation.40 | async-start | bytes 9732096 | tf_op jit(solution)/shard_map/while/body/eval_jaxpr/all_gather | solution.py:251
  839.6 554.3 %reduce-scatter.26.cloned.1.call-start = ((), (), s32[]{:S(2)}) async-start(), calls=%async_computation.42 | async-start | bytes 1572864 | tf_op jit(solution)/shard_map/while/body/eval_jaxpr/reduce_scatter | solution.py:180
  1583.5 180.2 %all-to-all-start.5 = ((bf16[16,64,4608]{2,1,0:T(8,128)(2,1)}), bf16[16,64,4608]{2,1,0:T(8,128)(2,1)}, u32[]{:S(2)}, u32[]{:S(2)}) async-start(bf16[16,64,4608]{2,1,0:T(8,128)(2,1)} %bitcast.568), calls=%async_computation.12 | async-start | bytes 18874368 | tf_op jit(solution)/shard_map/all_to_all | solution.py:317
  1763.8 210.0 %all-to-all-start.4 = ((bf16[16,64,4608]{2,1,0:T(8,128)(2,1)}), bf16[16,64,4608]{2,1,0:T(8,128)(2,1)}, u32[]{:S(2)}, u32[]{:S(2)}) async-start(bf16[16,64,4608]{2,1,0:T(8,128)(2,1)} %bitcast.567), calls=%async_computation.10 | async-start | bytes 18874368 | tf_op jit(solution)/shard_map/all_to_all | solution.py:314
  1973.8 209.7 %all-to-all-start.6 = ((bf16[16,288,1024]{2,1,0:T(8,128)(2,1)}), bf16[16,288,1024]{2,1,0:T(8,128)(2,1)}, u32[]{:S(2)}, u32[]{:S(2)}) async-start(bf16[16,288,1024]{2,1,0:T(8,128)(2,1)} %bitcast.566), calls=%async_computation.14 | async-start | bytes 18874368 | tf_op jit(solution)/shard_map/all_to_all | solution.py:320
  2014.5 252.0 %reduce-scatter.14.cloned.1.call-start = ((), (), s32[]{:S(2)}) async-start(), calls=%async_computation.18 | async-start | bytes 98304 | tf_op jit(solution)/shard_map/reduce_scatter | solution.py:332
  2016.6 251.3 %reduce-scatter.12.cloned.1.call-start = ((), (), s32[]{:S(2)}) async-start(), calls=%async_computation.17 | async-start | bytes 98304 | tf_op jit(solution)/shard_map/reduce_scatter | solution.py:329
  2018.7 250.6 %reduce-scatter.10.cloned.1.call-start = ((), (), s32[]{:S(2)}) async-start(), calls=%async_computation.16 | async-start | bytes 196608 | tf_op jit(solution)/shard_map/reduce_scatter | solution.py:326
  2021.5 249.4 %reduce-scatter.16.cloned.1.call-start = ((), (), s32[]{:S(2)}) async-start(), calls=%async_computation.19 | async-start | bytes 196608 | tf_op jit(solution)/shard_map/reduce_scatter | solution.py:335
  2024.2 248.1 %reduce-scatter.20.cloned.1.call-start = ((), (), s32[]{:S(2)}) async-start(), calls=%async_computation.21 | async-start | bytes 884736 | tf_op jit(solution)/shard_map/reduce_scatter | solution.py:341
  2030.3 243.9 %reduce-scatter.18.cloned.1.call-start = ((), (), s32[]{:S(2)}) async-start(), calls=%async_computation.20 | async-start | bytes 884736 | tf_op jit(solution)/shard_map/reduce_scatter | solution.py:338
  2036.4 239.6 %reduce-scatter.22.cloned.1.call-start = ((), (), s32[]{:S(2)}) async-start(), calls=%async_computation.22 | async-start | bytes 884736 | tf_op jit(solution)/shard_map/reduce_scatter | solution.py:344
  2341.0 155.8 %all-gather.25.cloned.1.call-start = ((), (), s32[]{:S(2)}) async-start(), calls=%async_computation.26 | async-start | bytes 1572864 | tf_op jit(solution)/shard_map/while/body/eval_jaxpr/all_gather | solution.py:79
  2399.5 157.4 %all-gather.29.cloned.1.call-start = ((), (), s32[]{:S(2)}) async-start(), calls=%async_computation.28 | async-start | bytes 2162688 | tf_op jit(solution)/shard_map/while/body/eval_jaxpr/all_gather | solution.py:239
  2400.2 240.9 %all-gather.33.cloned.1.call-start = ((), (), s32[]{:S(2)}) async-start(), calls=%async_computation.30 | async-start | bytes 9732096 | tf_op jit(solution)/shard_map/while/body/eval_jaxpr/all_gather | solution.py:240
  2400.9 324.0 %all-gather.31.cloned.1.call-start = ((), (), s32[]{:S(2)}) async-start(), calls=%async_computation.29 | async-start | bytes 9732096 | tf_op jit(solution)/shard_map/while/body/eval_jaxpr/all_gather | solution.py:242
  2401.5 407.4 %all-gather.35.cloned.1.call-start = ((), (), s32[]{:S(2)}) async-start(), calls=%async_computation.31 | async-start | bytes 9732096 | tf_op jit(solution)/shard_map/while/body/eval_jaxpr/all_gather | solution.py:241
  2890.5 155.8 %all-gather.25.cloned.1.call-start = ((), (), s32[]{:S(2)}) async-start(), calls=%async_computation.26 | async-start | bytes 1572864 | tf_op jit(solution)/shard_map/while/body/eval_jaxpr/all_gather | solution.py:79
  2948.7 157.4 %all-gather.29.cloned.1.call-start = ((), (), s32[]{:S(2)}) async-start(), calls=%async_computation.28 | async-start | bytes 2162688 | tf_op jit(solution)/shard_map/while/body/eval_jaxpr/all_gather | solution.py:239
  2949.3 241.0 %all-gather.33.cloned.1.call-start = ((), (), s32[]{:S(2)}) async-start(), calls=%async_computation.30 | async-start | bytes 9732096 | tf_op jit(solution)/shard_map/while/body/eval_jaxpr/all_gather | solution.py:240
  2950.1 324.1 %all-gather.31.cloned.1.call-start = ((), (), s32[]{:S(2)}) async-start(), calls=%async_computation.29 | async-start | bytes 9732096 | tf_op jit(solution)/shard_map/while/body/eval_jaxpr/all_gather | solution.py:242
  2950.7 407.6 %all-gather.35.cloned.1.call-start = ((), (), s32[]{:S(2)}) async-start(), calls=%async_computation.31 | async-start | bytes 9732096 | tf_op jit(solution)/shard_map/while/body/eval_jaxpr/all_gather | solution.py:241
  (162 other events, 4804.4 us)
Sparse Core Ops, SparseCore 0:
  19.2 56.4 all-gather.38
  78.9 52.6 all-gather.42
  133.9 20.2 all-gather.40
  157.4 56.4 all-gather.46
  239.5 56.4 all-gather.36
  299.3 80.8 all-gather.48
  383.6 80.6 all-gather.50
  467.6 80.6 all-gather.52
  720.5 53.6 all-gather.38
  777.6 52.6 all-gather.42
  832.3 20.2 all-gather.40
  855.9 56.4 all-gather.46
  937.9 56.4 all-gather.36
  997.7 80.8 all-gather.48
  1081.9 80.6 all-gather.50
  1165.8 80.6 all-gather.52
  2283.7 53.8 all-gather.18
  2340.8 52.6 all-gather.22
  2395.1 20.2 all-gather.20
  2418.7 56.4 all-gather.26
  2500.3 56.4 all-gather.28
  2560.2 80.8 all-gather.32
  2644.3 80.6 all-gather.30
  2728.3 80.6 all-gather.34
  2834.6 52.2 all-gather.18
  2890.1 52.6 all-gather.22
  2944.4 20.2 all-gather.20
  2968.1 56.4 all-gather.26
  3049.6 56.4 all-gather.28
  3109.4 80.8 all-gather.32
  3193.6 80.6 all-gather.30
  3277.6 80.6 all-gather.34
  (8 shorter events, 156.1 us)
Sparse Core Ops, SparseCore 1:
  2017.8 10.2 reduce-scatter.13
  2030.6 9.9 reduce-scatter.11
  2043.2 10.2 reduce-scatter.9
  2056.2 10.1 reduce-scatter.15
  2069.3 15.2 reduce-scatter.19
  2087.5 15.2 reduce-scatter.17
  2190.6 50.7 reduce-scatter.21
where the time goes:
time: 3390 us
  waiting for transfers between devices  2310 us (68%)
  matrix products  566 us (17%)
  other arithmetic  210 us (6%)
  starting transfers between devices  128 us (4%)
  blocking collectives  76 us (2%)
  local copies, waits for them, and re-layouts  75.2 us (2%)
    all_gather x2, waiting for transfers between devices, fetch_forward(): lax.all_gather(w_up, ('dp', 'ctx'), axis=0, tiled=True)  168 us
    all_gather x2, waiting for transfers between devices, fetch_forward(): lax.all_gather(w_gate, ('dp', 'ctx'), axis=0, tiled=True)  160 us
    all_gather x2, waiting for transfers between devices, fetch_backward(): lax.all_gather(w_down, ('dp', 'ctx'), axis=0, tiled=True)  157 us
    all_to_all x1, waiting for transfers between devices, per_device(): lax.all_to_all(split_set[5].astype(jnp.bfloat16), 'dp', split_axis=0, con...  153 us
    all_to_all x1, waiting for transfers between devices, per_device(): lax.all_to_all(split_set[4].astype(jnp.bfloat16), 'dp', split_axis=0, con...  152 us
    all_to_all x1, waiting for transfers between devices, per_device(): lax.all_to_all(split_set[6].astype(jnp.bfloat16), 'dp', split_axis=0, con...  146 us
    all_gather x2, waiting for transfers between devices, fetch_backward(): lax.all_gather(w_gate, ('dp', 'ctx'), axis=0, tiled=True)  146 us
    all_gather x2, waiting for transfers between devices, fetch_backward(): lax.all_gather(w_up, ('dp', 'ctx'), axis=0, tiled=True)  145 us
  transfers between devices with their start and end apart: 54, of which 45 were waited for; matrix products, arithmetic and copies ran while one was open for 16% of the time, Pallas kernels for 0%

commit v1 on v0

v1 whole, which is shorter than its diff:
```python
import functools

import jax
import jax.numpy as jnp
from jax import lax
from jax.experimental import pallas as pl
from jax.experimental.pallas import tpu as pltpu
from jax.sharding import PartitionSpec as P

epsilon = 1e-05
rope_base = 1000000.0
AXES = ("dp", "ctx")
BF = jnp.bfloat16
F32 = jnp.float32
LANES = 128
VMEM_LIMIT = 56 * 2**20
NN = (((1,), (0,)), ((), ()))
NT = (((1,), (1,)), ((), ()))
TN = (((0,), (0,)), ((), ()))


def mm(a, b, dims=NN):
    return lax.dot_general(a, b, dims, preferred_element_type=F32)


def params(semantics=None):
    return pltpu.CompilerParams(
        vmem_limit_bytes=VMEM_LIMIT,
        dimension_semantics=semantics,
    )


def resident(shape):
    zeros = (0,) * len(shape)
    return pl.BlockSpec(shape, lambda *_: zeros, pipeline_mode=pl.Buffered(1))


def largest_block(size, most):
    return max(b for b in range(1, min(size, most) + 1) if size % b == 0)


def head_sum(field, ones):
    wide = ones.shape[0]
    high = field.astype(BF)
    low = (field - high.astype(F32)).astype(BF)
    parts = [
        mm(high[:, c : c + wide], ones) + mm(low[:, c : c + wide], ones)
        for c in range(0, field.shape[1], wide)
    ]
    return jnp.concatenate(parts, axis=1)


def swap_halves(field, head):
    half = head // 2
    width = field.shape[1]
    lane = lax.broadcasted_iota(jnp.int32, field.shape, 1)
    return jnp.where(
        lane % head < half,
        pltpu.roll(field, width - half, 1),
        pltpu.roll(field, half, 1),
    )


def spread(table, width):
    return jnp.concatenate([table] * (width // table.shape[1]), axis=1)


def qkv_kernel(
    q_width, kv_width, head, scale,
    x_ref, w_ref, g_ref, gqk_ref, cos_ref, sin_ref, ones_ref,
    normed_ref, q_ref, kv_ref, raw_ref,
):
    x = x_ref[...].astype(F32)
    inverse = lax.rsqrt(jnp.mean(x * x, axis=-1, keepdims=True) + epsilon)
    normed = (x * inverse * g_ref[...]).astype(BF)
    normed_ref[...] = normed
    qk = q_width + kv_width
    ones = ones_ref[...]
    wide = ones.shape[0]
    cos = spread(cos_ref[...], wide)
    sin = spread(sin_ref[...], wide)
    for c in range(0, qk, wide):
        raw = mm(normed, w_ref[:, c : c + wide])
        raw_ref[:, c : c + wide] = raw
        inv = lax.rsqrt(head_sum(raw * raw, ones) * (1.0 / head) + epsilon)
        field = raw * inv * gqk_ref[:, c : c + wide]
        turned = (field * cos + swap_halves(field, head) * sin).astype(BF)
        if c < q_width:
            q_ref[:, c : c + wide] = turned * jnp.asarray(scale, BF)
        else:
            kv_ref[:, c - q_width : c - q_width + wide] = turned
    kv_ref[:, kv_width:] = mm(normed, w_ref[:, qk:]).astype(BF)


def qkv_call(x, w, g, gqk, cos, sin, ones, q_width, kv_width, head):
    total, width = x.shape
    block = largest_block(total, 256)
    qk = q_width + kv_width

    def rows(n):
        return pl.BlockSpec((block, n), lambda i: (i, 0))

    return pl.pallas_call(
        functools.partial(qkv_kernel, q_width, kv_width, head, head ** (-0.5)),
        grid=(total // block,),
        in_specs=[
            rows(width), resident(w.shape), resident(g.shape), resident(gqk.shape),
            rows(LANES), rows(LANES), resident(ones.shape),
        ],
        out_specs=[rows(width), rows(q_width), rows(2 * kv_width), rows(qk)],
        out_shape=[
            jax.ShapeDtypeStruct((total, width), BF),
            jax.ShapeDtypeStruct((total, q_width), BF),
            jax.ShapeDtypeStruct((total, 2 * kv_width), BF),
            jax.ShapeDtypeStruct((total, qk), F32),
        ],
        compiler_params=params(),
        name="qkv_rope",
    )(x, w, g, gqk, cos, sin, ones)


def pad_head(pair, odd, fill):
    lane = lax.broadcasted_iota(jnp.int32, pair.shape, 1)
    if odd:
        pair = pltpu.roll(pair, LANES // 2, 1)
    return jnp.where(lane < LANES // 2, pair, jnp.asarray(fill, pair.dtype))


def attend_kernel(
    block_q, block_k, heads,
    low_ref, start_ref, q_ref, k_ref, v_ref, first_ref,
    out_ref, total_ref, k_scr, v_scr,
):
    s = pl.program_id(0)
    rows = q_ref.shape[1]
    length = k_ref.shape[1]
    start = start_ref[0]
    half = LANES // 2
    for h in range(heads):
        c = h // 2 * LANES
        k_scr[h] = pad_head(k_ref[0, :, c : c + LANES].astype(F32), h % 2, 0).astype(BF)
        v_scr[h] = pad_head(v_ref[0, :, c : c + LANES].astype(F32), h % 2, 1).astype(BF)
    lane = lax.broadcasted_iota(jnp.int32, (block_q, LANES), 1)
    key_lane = lax.broadcasted_iota(jnp.int32, (2 * block_q, block_k), 1)
    row = lax.broadcasted_iota(jnp.int32, (2 * block_q, 1), 0) % block_q

    def q_step(i, carry):
        at = pl.multiple_of(i * block_q, block_q)
        first = first_ref[0, pl.ds(at, block_q), :]
        first = jnp.concatenate([first, first], axis=0)
        last = row + (start + at)
        queries = []
        for h in range(heads):
            pair = q_ref[0, pl.ds(at, block_q), h * LANES : (h + 1) * LANES].astype(F32)
            queries.append(
                jnp.concatenate([pad_head(pair, 0, 0), pad_head(pair, 1, 0)], axis=0).astype(BF)
            )

        def k_step(j, sums):
            key_at = pl.multiple_of(j * block_k, block_k)
            key = key_lane + key_at
            live = (key >= first) & (key <= last)
            new = []
            for h in range(heads):
                scores = mm(queries[h], k_scr[h, pl.ds(key_at, block_k), :], NT)
                expo = jnp.where(live, jnp.exp(scores), 0.0).astype(BF)
                new.append(sums[h] + mm(expo, v_scr[h, pl.ds(key_at, block_k), :]))
            return tuple(new)

        end = (start + at + block_q - 1) // block_k + 1
        sums = lax.fori_loop(
            low_ref[s, i], end, k_step,
            tuple(jnp.zeros((2 * block_q, LANES), F32) for _ in range(heads)),
        )
        for h in range(heads):
            even, odd = sums[h][:block_q], sums[h][block_q:]
            both = jnp.where(lane < half, even, pltpu.roll(odd, half, 1))
            tot = jnp.where(lane < half, pltpu.roll(even, half, 1), odd)
            cols = slice(h * LANES, (h + 1) * LANES)
            out_ref[0, pl.ds(at, block_q), cols] = both / tot
            total_ref[0, pl.ds(at, block_q), cols] = tot
        return carry

    lax.fori_loop(0, rows // block_q, q_step, 0)


def attend_call(q, kv, first, low, start, block_q, block_k):
    seqs, rows, q_width = q.shape
    length = kv.shape[1]
    kv_width = kv.shape[2] // 2
    kv_heads = q_width // LANES
    heads = largest_block(kv_heads, 4)
    steps = kv_heads // heads
    half = LANES // 2
    spec_q = pl.BlockSpec((1, rows, heads * LANES), lambda s, p, *_: (s, 0, p))
    return pl.pallas_call(
        functools.partial(attend_kernel, block_q, block_k, heads),
        grid_spec=pltpu.PrefetchScalarGridSpec(
            num_scalar_prefetch=2,
            grid=(seqs, steps),
            in_specs=[
                spec_q,
                pl.BlockSpec((1, length, heads * half), lambda s, p, *_: (s, 0, p)),
                pl.BlockSpec((1, length, heads * half), lambda s, p, *_: (s, 0, p + steps)),
                pl.BlockSpec((1, rows, 1), lambda s, p, *_: (s, 0, 0)),
            ],
            out_specs=[spec_q, spec_q],
            scratch_shapes=[
                pltpu.VMEM((heads, length, LANES), BF),
                pltpu.VMEM((heads, length, LANES), BF),
            ],
        ),
        out_shape=[jax.ShapeDtypeStruct(q.shape, F32)] * 2,
        compiler_params=params(),
        name="attend",
    )(low, start, q, kv, kv, first)


def attend_back_kernel(
    block_q, block_k, heads,
    low_ref, start_ref, q_ref, do_ref, de_ref, k_ref, v_ref, first_ref,
    dq_ref, dk_ref, dv_ref, k_scr, v_scr, dk_scr, dv_scr,
):
    s = pl.program_id(0)
    rows = q_ref.shape[1]
    length = k_ref.shape[1]
    start = start_ref[0]
    half = LANES // 2
    for h in range(heads):
        c = h // 2 * LANES
        k_scr[h] = pad_head(k_ref[0, :, c : c + LANES].astype(F32), h % 2, 0).astype(BF)
        v_scr[h] = pad_head(v_ref[0, :, c : c + LANES].astype(F32), h % 2, 1).astype(BF)
    dk_scr[...] = jnp.zeros_like(dk_scr)
    dv_scr[...] = jnp.zeros_like(dv_scr)
    lane = lax.broadcasted_iota(jnp.int32, (block_q, LANES), 1)
    key_row = lax.broadcasted_iota(jnp.int32, (block_k, 2 * block_q), 0)
    column = lax.broadcasted_iota(jnp.int32, (1, 2 * block_q), 1) % block_q

    def tail(pair, odd, delta):
        if odd:
            pair = pltpu.roll(pair, half, 1)
        else:
            delta = pltpu.roll(delta, half, 1)
        part0 = delta.astype(BF).astype(F32)
        part1 = (delta - part0).astype(BF).astype(F32)
        part2 = delta - part0 - part1
        rest = jnp.where(
            lane == half, part0, jnp.where(lane == half + 1, part1, jnp.where(lane == half + 2, part2, 0.0))
        )
        return jnp.where(lane < half, pair, -rest)

    def q_step(i, carry):
        at = pl.multiple_of(i * block_q, block_q)
        first = first_ref[0, :, pl.ds(at, block_q)]
        first = jnp.concatenate([first, first], axis=1)
        last = column + (start + at)
        queries, grads = [], []
        for h in range(heads):
            cols = slice(h * LANES, (h + 1) * LANES)
            pair = q_ref[0, pl.ds(at, block_q), cols].astype(F32)
            queries.append(
                jnp.concatenate([pad_head(pair, 0, 0), pad_head(pair, 1, 0)], axis=0).astype(BF)
            )
            pair = do_ref[0, pl.ds(at, block_q), cols].astype(F32)
            delta = de_ref[0, pl.ds(at, block_q), cols]
            grads.append(
                jnp.concatenate([tail(pair, 0, delta), tail(pair, 1, delta)], axis=0).astype(BF)
            )

        def k_step(j, sums):
            key_at = pl.multiple_of(j * block_k, block_k)
            key = key_row + key_at
            live = (key >= first) & (key <= last)
            new = []
            for h in range(heads):
                k = k_scr[h, pl.ds(key_at, block_k), :]
                v = v_scr[h, pl.ds(key_at, block_k), :]
                scores = mm(k, queries[h], NT)
                expo = jnp.where(live, jnp.exp(scores), 0.0)
                change = mm(v, grads[h], NT)
                d_scores = (expo * change).astype(BF)
                dv_scr[h, pl.ds(key_at, block_k), :] += mm(expo.astype(BF), grads[h])
                dk_scr[h, pl.ds(key_at, block_k), :] += mm(d_scores, queries[h])
                new.append(sums[h] + mm(d_scores, k, TN))
            return tuple(new)

        end = (start + at + block_q - 1) // block_k + 1
        sums = lax.fori_loop(
            low_ref[s, i], end, k_step,
            tuple(jnp.zeros((2 * block_q, LANES), F32) for _ in range(heads)),
        )
        for h in range(heads):
            even, odd = sums[h][:block_q], sums[h][block_q:]
            cols = slice(h * LANES, (h + 1) * LANES)
            dq_ref[0, pl.ds(at, block_q), cols] = jnp.where(
                lane < half, even, pltpu.roll(odd, half, 1)
            )
        return carry

    lax.fori_loop(0, rows // block_q, q_step, 0)
    wide = lax.broadcasted_iota(jnp.int32, (length, LANES), 1)
    for h in range(0, heads, 2):
        cols = slice(h // 2 * LANES, (h // 2 + 1) * LANES)
        for grad, scr in ((dk_ref, dk_scr), (dv_ref, dv_scr)):
            grad[0, :, cols] = jnp.where(
                wide < half, scr[h], pltpu.roll(scr[h + 1], half, 1)
            ).astype(BF)


def attend_back_call(q, d_out, delta, kv, first, low, start, block_q, block_k):
    seqs, rows, q_width = q.shape
    length = kv.shape[1]
    kv_width = kv.shape[2] // 2
    kv_heads = q_width // LANES
    heads = largest_block(kv_heads, 4)
    steps = kv_heads // heads
    half = LANES // 2
    spec_q = pl.BlockSpec((1, rows, heads * LANES), lambda s, p, *_: (s, 0, p))
    spec_kv = pl.BlockSpec((1, length, heads * half), lambda s, p, *_: (s, 0, p))
    return pl.pallas_call(
        functools.partial(attend_back_kernel, block_q, block_k, heads),
        grid_spec=pltpu.PrefetchScalarGridSpec(
            num_scalar_prefetch=2,
            grid=(seqs, steps),
            in_specs=[
                spec_q, spec_q, spec_q, spec_kv,
                pl.BlockSpec((1, length, heads * half), lambda s, p, *_: (s, 0, p + steps)),
                pl.BlockSpec((1, 1, rows), lambda s, p, *_: (s, 0, 0)),
            ],
            out_specs=[spec_q, spec_kv, spec_kv],
            scratch_shapes=[
                pltpu.VMEM((heads, length, LANES), BF),
                pltpu.VMEM((heads, length, LANES), BF),
                pltpu.VMEM((heads, length, LANES), F32),
                pltpu.VMEM((heads, length, LANES), F32),
            ],
        ),
        out_shape=[
            jax.ShapeDtypeStruct(q.shape, F32),
            jax.ShapeDtypeStruct((seqs, length, kv_width), BF),
            jax.ShapeDtypeStruct((seqs, length, kv_width), BF),
        ],
        compiler_params=params(),
        name="attend_back",
    )(low, start, q, d_out, delta, kv, kv, first)


def hidden_kernel(a_ref, w_ref, x_ref, g_ref, att_ref, hidden_ref, normed_ref):
    attended = a_ref[...].astype(BF)
    att_ref[...] = attended
    hidden = x_ref[...].astype(F32) + mm(attended, w_ref[...])
    hidden_ref[...] = hidden
    inverse = lax.rsqrt(jnp.mean(hidden * hidden, axis=-1, keepdims=True) + epsilon)
    normed_ref[...] = (hidden * inverse * g_ref[...]).astype(BF)


def hidden_call(mixed, w_o, x, g):
    total, width = x.shape
    q_width = mixed.shape[1]
    block = largest_block(total, 256)

    def rows(n):
        return pl.BlockSpec((block, n), lambda i: (i, 0))

    return pl.pallas_call(
        hidden_kernel,
        grid=(total // block,),
        in_specs=[rows(q_width), resident(w_o.shape), rows(width), resident(g.shape)],
        out_specs=[rows(q_width), rows(width), rows(width)],
        out_shape=[
            jax.ShapeDtypeStruct((total, q_width), BF),
            jax.ShapeDtypeStruct((total, width), F32),
            jax.ShapeDtypeStruct((total, width), BF),
        ],
        compiler_params=params(),
        name="hidden",
    )(mixed, w_o, x, g)


def ffn_kernel(
    block_t,
    n_ref, c_ref, wg_ref, wu_ref, wd_ref,
    out_ref, dn_ref, gg_ref, gu_ref, gd_ref,
    n_scr, c_scr, act_scr, dg_scr, du_scr,
):
    total, width = n_ref.shape
    chunk = wg_ref.shape[1]

    @pl.when(pl.program_id(0) == 0)
    def _():
        c_scr[...] = c_ref[...].astype(BF)
        n_scr[...] = n_ref[...].T
        out_ref[...] = jnp.zeros_like(out_ref)
        dn_ref[...] = jnp.zeros_like(dn_ref)

    def t_step(i, carry):
        at = pl.ds(pl.multiple_of(i * block_t, block_t), block_t)
        normed = n_ref[at, :]
        gate = mm(normed, wg_ref[...])
        up = mm(normed, wu_ref[...])
        d_act = mm(c_scr[at, :], wd_ref[...], NT)
        sig = 1.0 / (1.0 + jnp.exp(-gate))
        silu = gate * sig
        act = (silu * up).astype(BF)
        d_gate = (d_act * up * (sig * (1.0 + gate - silu))).astype(BF)
        d_up = (d_act * silu).astype(BF)
        act_scr[at, :] = act
        dg_scr[at, :] = d_gate
        du_scr[at, :] = d_up
        out_ref[at, :] += mm(act, wd_ref[...])
        dn_ref[at, :] += mm(d_gate, wg_ref[...], NT) + mm(d_up, wu_ref[...], NT)
        return carry

    lax.fori_loop(0, total // block_t, t_step, 0)

    def d_step(i, carry):
        at = pl.ds(pl.multiple_of(i * 256, 256), 256)
        normed = n_scr[at, :]
        gg_ref[at, :] = mm(normed, dg_scr[...]).astype(BF)
        gu_ref[at, :] = mm(normed, du_scr[...]).astype(BF)
        return carry

    lax.fori_loop(0, width // 256, d_step, 0)
    for c in range(0, chunk, 256):
        gd_ref[c : c + 256, :] = mm(act_scr[:, c : c + 256], c_scr[...], TN).astype(BF)


def ffn_call(normed, cotangent, w_gate, w_up, w_down):
    total, width = normed.shape
    hidden = w_gate.shape[1]
    chunk = largest_block(hidden, 512)
    block_t = largest_block(total, 256)
    cols = pl.BlockSpec((width, chunk), lambda i: (0, i))
    rows = pl.BlockSpec((chunk, width), lambda i: (i, 0))
    return pl.pallas_call(
        functools.partial(ffn_kernel, block_t),
        grid=(hidden // chunk,),
        in_specs=[resident(normed.shape), resident(normed.shape), cols, cols, rows],
        out_specs=[resident(normed.shape), resident(normed.shape), cols, cols, rows],
        out_shape=[
            jax.ShapeDtypeStruct((total, width), F32),
            jax.ShapeDtypeStruct((total, width), F32),
            jax.ShapeDtypeStruct(w_gate.shape, BF),
            jax.ShapeDtypeStruct(w_gate.shape, BF),
            jax.ShapeDtypeStruct(w_down.shape, BF),
        ],
        scratch_shapes=[
            pltpu.VMEM((width, total), BF),
            pltpu.VMEM((total, width), BF),
            pltpu.VMEM((total, chunk), BF),
            pltpu.VMEM((total, chunk), BF),
            pltpu.VMEM((total, chunk), BF),
        ],
        compiler_params=params(),
        cost_estimate=pl.CostEstimate(
            flops=18 * total * width * hidden, bytes_accessed=12 * width * hidden, transcendentals=0
        ),
        name="ffn",
    )(normed, cotangent, w_gate, w_up, w_down)


def middle_kernel(
    head,
    f_ref, dn_ref, h_ref, c_ref, g_ref, w_ref, o_ref, l_ref, ones_ref,
    out_ref, dh_ref, low_ref, do_ref, de_ref, gain_ref,
):
    @pl.when(pl.program_id(0) == 0)
    def _():
        gain_ref[...] = jnp.zeros_like(gain_ref)

    hidden = h_ref[...]
    out_ref[...] = (hidden + f_ref[...]).astype(BF)
    inverse = lax.rsqrt(jnp.mean(hidden * hidden, axis=-1, keepdims=True) + epsilon)
    incoming = dn_ref[...]
    unit = hidden * inverse
    gain_ref[...] += jnp.sum(unit * incoming, axis=0, keepdims=True)
    scaled = incoming * g_ref[...]
    shared = jnp.mean(unit * scaled, axis=-1, keepdims=True)
    d_hidden = c_ref[...] + inverse * (scaled - unit * shared)
    dh_ref[...] = d_hidden
    low = d_hidden.astype(BF)
    low_ref[...] = low
    ones = ones_ref[...]
    wide = ones.shape[0]
    for c in range(0, o_ref.shape[1], wide):
        cols = slice(c, c + wide)
        d_att = mm(low, w_ref[cols, :], NT)
        ratio = 1.0 / l_ref[:, cols]
        do_ref[:, cols] = (d_att * ratio).astype(BF)
        de_ref[:, cols] = head_sum(d_att * o_ref[:, cols], ones) * ratio


def middle_call(ffn, d_normed, hidden, cotangent, g, w_o, mixed, totals, ones, head):
    total, width = hidden.shape
    q_width = mixed.shape[1]
    block = largest_block(total, 256)

    def rows(n):
        return pl.BlockSpec((block, n), lambda i: (i, 0))

    return pl.pallas_call(
        functools.partial(middle_kernel, head),
        grid=(total // block,),
        in_specs=[
            rows(width), rows(width), rows(width), rows(width), resident(g.shape),
            resident(w_o.shape), rows(q_width), rows(q_width), resident(ones.shape),
        ],
        out_specs=[
            rows(width), rows(width), rows(width), rows(q_width), rows(q_width), resident((1, width)),
        ],
        out_shape=[
            jax.ShapeDtypeStruct((total, width), BF),
            jax.ShapeDtypeStruct((total, width), F32),
            jax.ShapeDtypeStruct((total, width), BF),
            jax.ShapeDtypeStruct((total, q_width), BF),
            jax.ShapeDtypeStruct((total, q_width), F32),
            jax.ShapeDtypeStruct((1, width), F32),
        ],
        compiler_params=params(),
        name="middle",
    )(ffn, d_normed, hidden, cotangent, g, w_o, mixed, totals, ones)


def last_kernel(
    q_width, kv_width, head, scale,
    dq_ref, dk_ref, dv_ref, raw_ref, gqk_ref, cos_ref, sin_ref, ones_ref, w_ref, x_ref, g_ref, dh_ref,
    d_ref, in_ref, gain_ref, gq_ref, gk_ref,
):
    @pl.when(pl.program_id(0) == 0)
    def _():
        gain_ref[...] = jnp.zeros_like(gain_ref)
        gq_ref[...] = jnp.zeros_like(gq_ref)
        gk_ref[...] = jnp.zeros_like(gk_ref)

    ones = ones_ref[...]
    wide = ones.shape[0]
    cos = spread(cos_ref[...], wide)
    sin = spread(sin_ref[...], wide)
    qk = q_width + kv_width
    for c in range(0, qk, wide):
        cols = slice(c, c + wide)
        if c < q_width:
            grad, total = dq_ref[:, cols] * scale, gq_ref
        else:
            grad, total = dk_ref[:, c - q_width : c - q_width + wide].astype(F32), gk_ref
        grad = grad * cos + swap_halves(grad * sin, head)
        raw = raw_ref[:, cols]
        inv = lax.rsqrt(head_sum(raw * raw, ones) * (1.0 / head) + epsilon)
        unit = raw * inv
        gained = jnp.sum(unit * grad, axis=0, keepdims=True)
        total[...] += sum(gained[:, i : i + LANES] for i in range(0, wide, LANES))
        scaled = grad * gqk_ref[:, cols]
        shared = head_sum(unit * scaled, ones) * (1.0 / head)
        d_ref[:, cols] = (inv * (scaled - unit * shared)).astype(BF)
    d_ref[:, qk:] = dv_ref[...].astype(BF)
    d_normed = mm(d_ref[...], w_ref[...], NT)
    x = x_ref[...].astype(F32)
    inverse = lax.rsqrt(jnp.mean(x * x, axis=-1, keepdims=True) + epsilon)
    unit = x * inverse
    gain_ref[...] += jnp.sum(unit * d_normed, axis=0, keepdims=True)
    scaled = d_normed * g_ref[...]
    shared = jnp.mean(unit * scaled, axis=-1, keepdims=True)
    in_ref[...] = dh_ref[...] + inverse * (scaled - unit * shared)


def last_call(dq, dk, dv, raw, gqk, cos, sin, ones, w, x, g, d_hidden, head):
    total, width = x.shape
    q_width, kv_width = dq.shape[1], dk.shape[1]
    block = largest_block(total, 256)

    def rows(n):
        return pl.BlockSpec((block, n), lambda i: (i, 0))

    return pl.pallas_call(
        functools.partial(last_kernel, q_width, kv_width, head, head ** (-0.5)),
        grid=(total // block,),
        in_specs=[
            rows(q_width), rows(kv_width), rows(kv_width), rows(q_width + kv_width),
            resident(gqk.shape), rows(LANES), rows(LANES), resident(ones.shape),
            resident(w.shape), rows(width), resident(g.shape), rows(width),
        ],
        out_specs=[
            rows(w.shape[1]), rows(width),
            resident((1, width)), resident((1, LANES)), resident((1, LANES)),
        ],
        out_shape=[
            jax.ShapeDtypeStruct((total, w.shape[1]), BF),
            jax.ShapeDtypeStruct((total, width), F32),
            jax.ShapeDtypeStruct((1, width), F32),
            jax.ShapeDtypeStruct((1, LANES), F32),
            jax.ShapeDtypeStruct((1, LANES), F32),
        ],
        compiler_params=params(),
        name="last",
    )(dq, dk, dv, raw, gqk, cos, sin, ones, w, x, g, d_hidden)


def per_device(
    tokens, segments, cotangent, w_q, w_k, w_v, w_o, w_gate, w_up, w_down, g_attn, g_q, g_k, g_ffn
):
    seqs, rows, width = tokens.shape
    length = segments.shape[1]
    head = g_q.shape[0]
    q_width, kv_width = w_q.shape[1], w_k.shape[1]
    kv_heads = kv_width // head
    q_heads = q_width // head
    total = seqs * rows
    row_start = lax.axis_index("ctx") * rows

    def fetch(weight):
        return lax.all_gather(weight, AXES, axis=0, tiled=True)

    w_qkv = fetch(jnp.concatenate([w_q, w_k, w_v], axis=1))
    w_o = fetch(w_o)
    w_gate = fetch(w_gate)
    w_up = fetch(w_up)
    w_down = fetch(w_down)

    seg_rows = lax.dynamic_slice_in_dim(segments, row_start, rows, 1)
    first = jnp.sum((segments[:, None, :] < seg_rows[:, :, None]).astype(jnp.int32), axis=-1)
    query_pos = row_start + jnp.arange(rows, dtype=jnp.int32)
    positions = (query_pos[None, :] - first).reshape(total)
    frequency = rope_base ** (-jnp.arange(0, head, 2, dtype=F32) / head)
    angles = positions.astype(F32)[:, None] * frequency[None, :]
    cos, sin = jnp.cos(angles), jnp.sin(angles)
    cos = jnp.concatenate([cos] * (2 * LANES // head), axis=1)
    sin = jnp.concatenate([-sin, sin] * (LANES // head), axis=1)
    wide = 2 * LANES
    member = jnp.arange(wide) // head
    ones = (member[:, None] == member[None, :]).astype(BF)
    gqk = jnp.concatenate([g_q] * q_heads + [g_k] * kv_heads)[None, :]
    block_q, block_k = min(128, rows), 128
    low = first[:, ::block_q] // block_k
    start = jnp.full((1,), row_start, jnp.int32)

    x = tokens.reshape(total, width)
    normed, q, kv, raw = qkv_call(
        x, w_qkv, g_attn[None, :], gqk, cos, sin, ones, q_width, kv_width, head
    )
    kv = lax.all_gather(kv.reshape(seqs, rows, 2 * kv_width), "ctx", axis=1, tiled=True)
    q = q.reshape(seqs, rows, q_width)
    mixed, totals = attend_call(q, kv, first[:, :, None], low, start, block_q, block_k)
    mixed, totals = mixed.reshape(total, q_width), totals.reshape(total, q_width)
    attended, hidden, normed_two = hidden_call(mixed, w_o, x, g_ffn[None, :])

    def send(grad):
        return lax.psum_scatter(
            grad.astype(BF), AXES, scatter_dimension=0, tiled=True
        ).astype(F32)

    cotangent = cotangent.reshape(total, width)
    ffn, d_normed_two, grad_gate, grad_up, grad_down = ffn_call(
        normed_two, cotangent, w_gate, w_up, w_down
    )
    out_gate, out_up, out_down = send(grad_gate), send(grad_up), send(grad_down)
    outputs, d_hidden, d_low, d_out, delta, grad_gffn = middle_call(
        ffn, d_normed_two, hidden, cotangent, g_ffn[None, :], w_o, mixed, totals, ones, head
    )
    out_o = send(mm(attended, d_low, TN))
    dq, dk, dv = attend_back_call(
        q, d_out.reshape(q.shape), delta.reshape(q.shape), kv, first[:, None, :], low, start,
        block_q, block_k,
    )
    dkv = lax.psum_scatter(
        jnp.concatenate([dk, dv], axis=2), "ctx", scatter_dimension=1, tiled=True
    ).reshape(total, 2 * kv_width)
    d_qkv, input_grad, grad_gattn, grad_gq, grad_gk = last_call(
        dq.reshape(total, q_width), dkv[:, :kv_width], dkv[:, kv_width:], raw, gqk, cos, sin, ones,
        w_qkv, x, g_attn[None, :], d_hidden, head,
    )
    out_qkv = send(mm(normed, d_qkv, TN))

    def fold(grad):
        return jnp.sum(grad.reshape(LANES // head, head), axis=0)

    gains = lax.psum(
        (grad_gattn[0], fold(grad_gq), fold(grad_gk), grad_gffn[0]), AXES
    )
    return (
        outputs.reshape(tokens.shape),
        input_grad.reshape(tokens.shape),
        out_qkv[:, :q_width],
        out_qkv[:, q_width : q_width + kv_width],
        out_qkv[:, q_width + kv_width :],
        out_o,
        out_gate,
        out_up,
        out_down,
        *gains,
    )


def solution(mesh):
    split = P("dp", "ctx", None)
    shard = P(("dp", "ctx"), None)
    in_specs = (split, P("dp", None), split) + (shard,) * 7 + (P(),) * 4
    out_specs = (split, split) + (shard,) * 7 + (P(),) * 4
    return jax.shard_map(
        per_device, mesh=mesh, in_specs=in_specs, out_specs=out_specs, check_vma=False
    )
```

time: 3390 us -> 1440 us (0.42)
  waiting for transfers between devices: 2310 us -> 1080 us
  matrix products: 566 us -> 13.6 us
  Pallas kernels: 0 us -> 260 us
  other arithmetic: 210 us -> 21 us
  starting transfers between devices: 128 us -> 0.87 us
  local copies, waits for them, and re-layouts: 75.2 us -> 12.3 us
  blocking collectives: 76 us -> 37.1 us
    all_gather x36 -> x6, waiting for transfers between devices: 1730 us -> 380 us  [the longest x5 329 us: fetch(): return lax.all_gather(weight, AXES, axis=0, tiled=True)]
    reduce_scatter x11 -> x6, waiting for transfers between devices: 11 us -> 695 us  [the longest x5 627 us: send(): lax.psum_scatter(grad.astype(BF), AXES, scatter_dimension=0, tiled=True)]
    dot_general x61 -> x2, matrix products: 566 us -> 13.6 us  [mm(): return lax.dot_general(a, b, dims, preferred_element_type=F32)]
    all_to_all x7 -> x0, waiting for transfers between devices: 547 us -> none  [the longest x1 153 us: per_device(): lax.all_to_all(split_set[5].astype(jnp.bfloat16), 'dp', split_axis=0, con...]
    pallas_call x0 -> x7, Pallas kernels: none -> 260 us  [the longest x1 113 us: ffn_call(): pl.pallas_call(functools.partial(ffn_kernel, block_t), grid=(hidden // ch...]
    all_to_all x7 -> x0, starting transfers between devices: 124 us -> none  [the longest x1 41.1 us: per_device(): lax.all_to_all(split_set[4].astype(jnp.bfloat16), 'dp', split_axis=0, con...]
    reduce_sum x19 -> x3, other arithmetic: 95.3 us -> 1.29 us  [the longest x1 1.25 us: per_device(): jnp.sum((segments[:, None, :] < seg_rows[:, :, None]).astype(jnp.int32),...]
    convert_element_type x25 -> x5, other arithmetic: 87.1 us -> 7.72 us  [the longest x4 6.96 us: send(): return lax.psum_scatter(grad.astype(BF), AXES, scatter_dimension=0, tiled...]
  transfers between devices with their start and end apart: 54 -> 12, of which waited for: 45 -> 12; matrix products, arithmetic and copies ran while one was open for 16% -> 3% of each run, Pallas kernels for 0% -> 4%
where the time goes in v1:
time: 1440 us
  waiting for transfers between devices  1080 us (75%)
  Pallas kernels  260 us (18%)
  blocking collectives  37.1 us (3%)
  other arithmetic  21 us (1%)
    reduce_scatter x5, waiting for transfers between devices, send(): lax.psum_scatter(grad.astype(BF), AXES, scatter_dimension=0, tiled=True)  627 us
    all_gather x5, waiting for transfers between devices, fetch(): return lax.all_gather(weight, AXES, axis=0, tiled=True)  329 us
    pallas_call x1, Pallas kernels, ffn_call(): pl.pallas_call(functools.partial(ffn_kernel, block_t), grid=(hidden // ch...  113 us
    reduce_scatter x1, waiting for transfers between devices, per_device(): lax.psum_scatter(jnp.concatenate([dk, dv], axis=2), 'ctx', scatter_dimens...  68.3 us
    pallas_call x1, Pallas kernels, attend_back_call(): pl.pallas_call(functools.partial(attend_back_kernel, block_q, block_k, he...  54.8 us
    all_gather x1, waiting for transfers between devices, per_device(): lax.all_gather(kv.reshape(seqs, rows, 2 * kv_width), 'ctx', axis=1, tiled...  50.5 us
    psum x1, blocking collectives, per_device(): lax.psum((grad_gattn[0], fold(grad_gq), fold(grad_gk), grad_gffn[0]), AXES)  37.1 us
    pallas_call x1, Pallas kernels, attend_call(): pl.pallas_call(functools.partial(attend_kernel, block_q, block_k, heads),...  31.8 us
  transfers between devices with their start and end apart: 12, of which 12 were waited for; matrix products, arithmetic and copies ran while one was open for 3% of the time, Pallas kernels for 4%

profile of v1, /device:TPU:0, one launch (start us, length us, event | category | flops | bytes accessed | tf_op | source)
XLA Modules:
  0.0 1438.4 jit_solution(2128211266824010673)
XLA Ops:
  7.2 1.5 pad_maximum_fusion.3
  12.8 1.9 fusion
  14.7 1.8 pad_maximum_fusion.1
  17.3 59.1 %all-gather.7.cloned.1.call-done.w_ref = bf16[1024,2048]{1,0:T(8,128)(2,1)} async-done(((bf16[32,2048]{1,0:T(8,128)(2,1)}), bf16[1024,2048]{1,0:T(8,128)(2,1)}) %all-gather.7.cloned.1.call-update) | async-done | bytes 4194320 | tf_op jit(solution)/shard_map/all_gather | solution.py:611
  76.4 17.2 %qkv_rope.1 = (bf16[1024,1024]{1,0:T(8,128)(2,1)}, bf16[1024,1024]{1,0:T(8,128)(2,1)}, bf16[1024,1024]{1,0:T(8,128)(2,1)}, f32[1024,1536]{1,0:T(8,128)}) custom-call(bf16[1024,1024]{1,0:T(8,128)(2,1)} %bitcast.25, bf16[1024,2048]{1,0:T(8,128)(2,1)} %all-gather.7.cloned.1.call-done.w_ref, f32[1,1024]{1,0:T(1,128)} %bitcast.41, ...), custom_call_target="tpu_custom_call" | custom-call | tf_op jit(solution)/shard_map/qkv_rope/pallas_call | solution.py:103
  98.6 50.5 %all-gather.9.cloned.1.call-done.k_ref.v_ref = bf16[2,1024,1024]{2,1,0:T(8,128)(2,1)} async-done(((bf16[2,512,1024]{2,1,0:T(8,128)(2,1)}), bf16[2,1024,1024]{2,1,0:T(8,128)(2,1)}) %all-gather.9.cloned.1.call-update) | async-done | bytes 4194320 | tf_op jit(solution)/shard_map/all_gather | solution.py:640
  149.0 31.8 %attend.1 = (f32[2,512,1024]{2,1,0:T(8,128)}, f32[2,512,1024]{2,1,0:T(8,128)}) custom-call(s32[2,4]{1,0:T(2,128)} %and_select_fusion.1.low_ref, s32[1]{0:T(128)} %bitcast.start_ref, bf16[2,512,1024]{2,1,0:T(8,128)(2,1)} %bitcast.30, bf16[2,1024,1024]{2,1,0:T(8,128)(2,1)} %all-gather.9.cloned.1.call-done.k_ref.v_ref, ...), custom_call_target="tpu_custom_call" | custom-call | tf_op jit(solution)/shard_map/attend/pallas_call | solution.py:196
  180.8 27.9 %all-gather.11.cloned.1.call-done.w_ref = bf16[1024,1024]{1,0:T(8,128)(2,1)} async-done(((bf16[32,1024]{1,0:T(8,128)(2,1)}), bf16[1024,1024]{1,0:T(8,128)(2,1)}) %all-gather.11.cloned.1.call-update) | async-done | bytes 2097168 | tf_op jit(solution)/shard_map/all_gather | solution.py:611
  208.7 8.2 hidden.1
  217.0 75.5 %all-gather.13.cloned.1.call-done.wg_ref = bf16[1024,4608]{1,0:T(8,128)(2,1)} async-done(((bf16[32,4608]{1,0:T(8,128)(2,1)}), bf16[1024,4608]{1,0:T(8,128)(2,1)}) %all-gather.13.cloned.1.call-update) | async-done | bytes 9437200 | tf_op jit(solution)/shard_map/all_gather | solution.py:611
  292.4 83.4 %all-gather.15.cloned.1.call-done.wu_ref = bf16[1024,4608]{1,0:T(8,128)(2,1)} async-done(((bf16[32,4608]{1,0:T(8,128)(2,1)}), bf16[1024,4608]{1,0:T(8,128)(2,1)}) %all-gather.15.cloned.1.call-update) | async-done | bytes 9437200 | tf_op jit(solution)/shard_map/all_gather | solution.py:611
  375.8 83.4 %all-gather.17.cloned.1.call-done.wd_ref = bf16[4608,1024]{1,0:T(8,128)(2,1)} async-done(((bf16[144,1024]{1,0:T(8,128)(2,1)}), bf16[4608,1024]{1,0:T(8,128)(2,1)}) %all-gather.17.cloned.1.call-update) | async-done | bytes 9437200 | tf_op jit(solution)/shard_map/all_gather | solution.py:611
  459.3 113.2 %ffn.1 = (f32[1024,1024]{1,0:T(8,128)}, f32[1024,1024]{1,0:T(8,128)}, bf16[1024,4608]{1,0:T(8,128)(2,1)}, bf16[1024,4608]{1,0:T(8,128)(2,1)}, bf16[4608,1024]{1,0:T(8,128)(2,1)}) custom-call(bf16[1024,1024]{1,0:T(8,128)(2,1)} %get-tuple-element.44.n_ref, f32[1024,1024]{1,0:T(8,128)} %bitcast.32, bf16[1024,4608]{1,0:T(8,128)(2,1)} %all-gather.13.cloned.1.call-done.wg_ref, ...), custom_call_target="tpu_custom_call" | custom-call | flops 86973087744 | bytes 56623104 | tf_op jit(solution)/shard_map/ffn/pallas_call | solution.py:435
  572.5 17.0 %middle.1 = (bf16[1024,1024]{1,0:T(8,128)(2,1)}, f32[1024,1024]{1,0:T(8,128)}, bf16[1024,1024]{1,0:T(8,128)(2,1)}, bf16[1024,1024]{1,0:T(8,128)(2,1)}, f32[1024,1024]{1,0:T(8,128)}, /*index=5*/f32[1,1024]{1,0:T(1,128)}) custom-call(f32[1024,1024]{1,0:T(8,128)} %get-tuple-element.45.f_ref, f32[1024,1024]{1,0:T(8,128)} %get-tuple-element.46.dn_ref, ...), custom_call_target="tpu_custom_call" | custom-call | tf_op jit(solution)/shard_map/middle/pallas_call | solution.py:501
  589.5 54.8 %attend_back.1 = (f32[2,512,1024]{2,1,0:T(8,128)}, bf16[2,1024,512]{2,1,0:T(8,128)(2,1)}, bf16[2,1024,512]{2,1,0:T(8,128)(2,1)}) custom-call(s32[2,4]{1,0:T(2,128)} %and_select_fusion.1.low_ref, s32[1]{0:T(128)} %bitcast.start_ref, bf16[2,512,1024]{2,1,0:T(8,128)(2,1)} %bitcast.31, bf16[2,512,1024]{2,1,0:T(8,128)(2,1)} %bitcast.39, ...), custom_call_target="tpu_custom_call" | custom-call | tf_op jit(solution)/shard_map/attend_back/pallas_call | solution.py:320
  644.4 4.8 pad_maximum_fusion
  650.8 5.3 convolution_convert_fusion.1
  658.2 68.3 %reduce-scatter.7.cloned.1.call-done = bf16[2,512,1024]{2,1,0:T(8,128)(2,1)} async-done(((bf16[2,1024,1024]{2,1,0:T(8,128)(2,1)}), bf16[2,512,1024]{2,1,0:T(8,128)(2,1)}) %reduce-scatter.7.cloned.1.call-update) | async-done | bytes 2097168 | tf_op jit(solution)/shard_map/reduce_scatter | solution.py:664
  726.5 3.0 fusion.1
  729.5 17.9 %last.1 = (bf16[1024,2048]{1,0:T(8,128)(2,1)}, f32[1024,1024]{1,0:T(8,128)}, f32[1,1024]{1,0:T(1,128)}, f32[1,128]{1,0:T(1,128)}, f32[1,128]{1,0:T(1,128)}) custom-call(f32[1024,1024]{1,0:T(8,128)} %bitcast.34, bf16[1024,512]{1,0:T(8,128)(2,1)} %get-tuple-element.74.dk_ref, bf16[1024,512]{1,0:T(8,128)(2,1)} %get-tuple-element.73.dv_ref, ...), custom_call_target="tpu_custom_call" | custom-call | tf_op jit(solution)/shard_map/last/pallas_call | solution.py:574
  747.4 8.3 convolution_convert_fusion
  755.7 110.7 %reduce-scatter.11.cloned.1.call-done = bf16[32,1024]{1,0:T(8,128)(2,1)} async-done(((bf16[1024,1024]{1,0:T(8,128)(2,1)}), bf16[32,1024]{1,0:T(8,128)(2,1)}) %reduce-scatter.11.cloned.1.call-update) | async-done | bytes 65552 | tf_op jit(solution)/shard_map/reduce_scatter | solution.py:647
  866.4 1.5 convert_element_type.48
  870.0 37.1 %all-reduce = (f32[1024]{0:T(1024)}, f32[64]{0:T(128)}, f32[64]{0:T(128)}, f32[1024]{0:T(1024)}) all-reduce(f32[1024]{0:T(1024)S(1)} %bitcast.47, f32[64]{0:T(128)S(1)} %reduce_sum.28, f32[64]{0:T(128)S(1)} %reduce_sum.29, f32[1024]{0:T(1024)S(1)} %bitcast.46), channel_id=1, replica_groups=mesh['dp'=16,'ctx'=2] {'dp','ctx'}, use_global_device_ids=true, to_apply=%region_7.8 | all-reduce | flops 2176 | bytes 17408 | tf_op jit(solution)/shard_map/psum | solution.py:676
  907.1 96.7 %reduce-scatter.13.cloned.1.call-done = bf16[32,4608]{1,0:T(8,128)(2,1)} async-done(((bf16[1024,4608]{1,0:T(8,128)(2,1)}), bf16[32,4608]{1,0:T(8,128)(2,1)}) %reduce-scatter.13.cloned.1.call-update) | async-done | bytes 294928 | tf_op jit(solution)/shard_map/reduce_scatter | solution.py:647
  1003.8 1.8 convert_element_type.49
  1005.6 139.6 %reduce-scatter.15.cloned.1.call-done = bf16[32,4608]{1,0:T(8,128)(2,1)} async-done(((bf16[1024,4608]{1,0:T(8,128)(2,1)}), bf16[32,4608]{1,0:T(8,128)(2,1)}) %reduce-scatter.15.cloned.1.call-update) | async-done | bytes 294928 | tf_op jit(solution)/shard_map/reduce_scatter | solution.py:647
  1145.2 1.8 convert_element_type.50
  1147.0 138.7 %reduce-scatter.17.cloned.1.call-done = bf16[144,1024]{1,0:T(8,128)(2,1)} async-done(((bf16[4608,1024]{1,0:T(8,128)(2,1)}), bf16[144,1024]{1,0:T(8,128)(2,1)}) %reduce-scatter.17.cloned.1.call-update) | async-done | bytes 294928 | tf_op jit(solution)/shard_map/reduce_scatter | solution.py:647
  1285.7 1.8 convert_element_type.51
  1287.5 141.1 %reduce-scatter.9.cloned.1.call-done = bf16[32,2048]{1,0:T(8,128)(2,1)} async-done(((bf16[1024,2048]{1,0:T(8,128)(2,1)}), bf16[32,2048]{1,0:T(8,128)(2,1)}) %reduce-scatter.9.cloned.1.call-update) | async-done | bytes 131088 | tf_op jit(solution)/shard_map/reduce_scatter | solution.py:647
  1430.1 1.5 slice.26
  (58 shorter events, 16.8 us)
Async XLA Ops:
  7.2 69.2 %all-gather.7.cloned.1.call-start = ((), (), s32[]{:S(2)}) async-start(), calls=%async_computation.6 | async-start | bytes 4325376 | tf_op jit(solution)/shard_map/all_gather | solution.py:611
  8.8 140.3 %all-gather.9.cloned.1.call-start = ((), (), s32[]{:S(2)}) async-start(), calls=%async_computation.7 | async-start | bytes 6291456 | tf_op jit(solution)/shard_map/all_gather | solution.py:640
  93.6 115.1 %all-gather.11.cloned.1.call-start = ((), (), s32[]{:S(2)}) async-start(), calls=%async_computation.8 | async-start | bytes 2162688 | tf_op jit(solution)/shard_map/all_gather | solution.py:611
  94.3 198.1 %all-gather.13.cloned.1.call-start = ((), (), s32[]{:S(2)}) async-start(), calls=%async_computation.9 | async-start | bytes 9732096 | tf_op jit(solution)/shard_map/all_gather | solution.py:611
  94.9 280.9 %all-gather.15.cloned.1.call-start = ((), (), s32[]{:S(2)}) async-start(), calls=%async_computation.10 | async-start | bytes 9732096 | tf_op jit(solution)/shard_map/all_gather | solution.py:611
  95.5 363.8 %all-gather.17.cloned.1.call-start = ((), (), s32[]{:S(2)}) async-start(), calls=%async_computation.11 | async-start | bytes 9732096 | tf_op jit(solution)/shard_map/all_gather | solution.py:611
  96.1 630.4 %reduce-scatter.7.cloned.1.call-start = ((), (), s32[]{:S(2)}) async-start(), calls=%async_computation.12 | async-start | bytes 6291456 | tf_op jit(solution)/shard_map/reduce_scatter | solution.py:664
  649.2 1.6 copy-start.3
  649.2 217.2 %reduce-scatter.11.cloned.1.call-start = ((), (), s32[]{:S(2)}) async-start(), calls=%async_computation.14 | async-start | bytes 2162688 | tf_op jit(solution)/shard_map/reduce_scatter | solution.py:647
  656.1 347.7 %reduce-scatter.13.cloned.1.call-start = ((), (), s32[]{:S(2)}) async-start(), calls=%async_computation.15 | async-start | bytes 9732096 | tf_op jit(solution)/shard_map/reduce_scatter | solution.py:647
  656.9 488.3 %reduce-scatter.15.cloned.1.call-start = ((), (), s32[]{:S(2)}) async-start(), calls=%async_computation.16 | async-start | bytes 9732096 | tf_op jit(solution)/shard_map/reduce_scatter | solution.py:647
  657.4 628.2 %reduce-scatter.17.cloned.1.call-start = ((), (), s32[]{:S(2)}) async-start(), calls=%async_computation.17 | async-start | bytes 9732096 | tf_op jit(solution)/shard_map/reduce_scatter | solution.py:647
  658.2 770.5 %reduce-scatter.9.cloned.1.call-start = ((), (), s32[]{:S(2)}) async-start(), calls=%async_computation.13 | async-start | bytes 4325376 | tf_op jit(solution)/shard_map/reduce_scatter | solution.py:647
  729.5 17.9 %copy-start.2 = (bf16[1024,1024]{1,0:T(8,128)(2,1)S(1)}, bf16[1024,1024]{1,0:T(8,128)(2,1)}, u32[]{:S(2)}) copy-start(bf16[1024,1024]{1,0:T(8,128)(2,1)} %get-tuple-element.58) | copy-start | bytes 6291460
  755.7 112.7 %copy-start.5 = (f32[1,128]{1,0:T(1,128)S(1)}, f32[1,128]{1,0:T(1,128)}, u32[]{:S(2)}) copy-start(f32[1,128]{1,0:T(1,128)} %get-tuple-element.66) | copy-start | bytes 1540
  755.7 113.5 %copy-start.4 = (f32[1,128]{1,0:T(1,128)S(1)}, f32[1,128]{1,0:T(1,128)}, u32[]{:S(2)}) copy-start(f32[1,128]{1,0:T(1,128)} %get-tuple-element.67) | copy-start | bytes 1540
  755.7 114.2 %copy-start = (f32[1,1024]{1,0:T(1,128)S(1)}, f32[1,1024]{1,0:T(1,128)}, u32[]{:S(2)}) copy-start(f32[1,1024]{1,0:T(1,128)} %get-tuple-element.68) | copy-start | bytes 12292
  755.7 114.2 %copy-start.1 = (f32[1,1024]{1,0:T(1,128)S(1)}, f32[1,1024]{1,0:T(1,128)}, u32[]{:S(2)}) copy-start(f32[1,1024]{1,0:T(1,128)} %get-tuple-element.65) | copy-start | bytes 12292
Sparse Core Ops, SparseCore 0:
  11.6 64.7 all-gather.6
  93.7 55.2 all-gather.8
  152.0 56.6 all-gather.10
  211.5 80.8 all-gather.12
  295.2 80.6 all-gather.14
  378.6 80.6 all-gather.16
  649.3 77.1 reduce-scatter.6
  728.8 137.4 reduce-scatter.10
  872.3 131.4 reduce-scatter.12
  1010.5 134.5 reduce-scatter.14
  1151.1 134.5 reduce-scatter.16
  1287.9 140.6 reduce-scatter.8

commit v2 on v1

--- a/solution.py
+++ b/solution.py
@@ -14,6 +14,8 @@
 F32 = jnp.float32
 LANES = 128
 VMEM_LIMIT = 56 * 2**20
+AHEAD = 4
+OWN = 6
 NN = (((1,), (0,)), ((), ()))
 NT = (((1,), (1,)), ((), ()))
 TN = (((0,), (0,)), ((), ()))
@@ -595,6 +597,294 @@
     )(dq, dk, dv, raw, gqk, cos, sin, ones, w, x, g, d_hidden)
 
 
+class Place:
+    def __init__(self):
+        dp = lax.axis_index("dp")
+        self.x = lax.axis_index("ctx")
+        self.c = lax.rem(dp, 2)
+        self.y = lax.rem(dp // 2, 2)
+        self.z = dp // 4
+
+    def peer(self, z=None, y=None, c=None, x=None):
+        z = self.z if z is None else z
+        y = self.y if y is None else y
+        c = self.c if c is None else c
+        x = self.x if x is None else x
+        return {"dp": (z * 2 + y) * 2 + c, "ctx": x}
+
+    def up(self, d):
+        return lax.rem(self.z + d, 4)
+
+    def peers(self):
+        return [self.peer(z=self.up(d)) for d in (1, 2, 3)] + [
+            self.peer(x=1 - self.x), self.peer(y=1 - self.y), self.peer(c=1 - self.c)
+        ]
+
+
+def greet(place):
+    barrier = pltpu.get_barrier_semaphore()
+    peers = place.peers()
+    for peer in peers:
+        pl.semaphore_signal(barrier, inc=1, device_id=peer, device_id_type=pl.DeviceIdType.MESH)
+    pl.semaphore_wait(barrier, len(peers))
+
+
+def remote(src, dst, sems, at, peer):
+    send, recv = sems
+    return pltpu.make_async_remote_copy(
+        src_ref=src, dst_ref=dst, send_sem=send.at[at], recv_sem=recv.at[at],
+        device_id=peer, device_id_type=pl.DeviceIdType.MESH,
+    )
+
+
+def gather_kernel(pieces, count, *refs):
+    ins, outs = refs[:count], refs[count : 2 * count]
+    sems, local = refs[2 * count : 2 * count + 2], refs[2 * count + 2]
+    me = Place()
+    greet(me)
+
+    def block(p, z, y, c, x):
+        array, rows, cols, _ = pieces[p]
+        return outs[array].at[z, y, c, x, rows, cols]
+
+    def own(p):
+        array, rows, cols, _ = pieces[p]
+        return ins[array].at[rows, cols]
+
+    every = slice(None)
+
+    def to_z(p):
+        return [
+            remote(own(p), block(p, me.z, me.y, me.c, me.x), sems, (p, d - 1), me.peer(z=me.up(d)))
+            for d in (1, 2, 3)
+        ]
+
+    def keep(p):
+        return pltpu.make_async_copy(own(p), block(p, me.z, me.y, me.c, me.x), local.at[p])
+
+    def first(p):
+        mine = block(p, every, me.y, me.c, me.x)
+        peer = me.peer(x=1 - me.x) if pieces[p][3] else me.peer(y=1 - me.y)
+        return [remote(mine, mine, sems, (p, 3), peer)]
+
+    def second(p):
+        if pieces[p][3]:
+            mine, peer = block(p, every, me.y, me.c, every), me.peer(y=1 - me.y)
+        else:
+            mine, peer = block(p, every, every, me.c, me.x), me.peer(x=1 - me.x)
+        return [remote(mine, mine, sems, (p, 4), peer)]
+
+    def third(p):
+        mine = block(p, every, every, me.c, every)
+        return [remote(mine, mine, sems, (p, 5), me.peer(c=1 - me.c))]
+
+    n = len(pieces)
+    stages = [to_z, first, second, third]
+    pair = 2
+
+    def begin(p):
+        keep(p).start()
+        for copy in to_z(p):
+            copy.start()
+
+    for p in range(min(n, AHEAD)):
+        begin(p)
+    for t in range(0, n + 3 * pair, pair):
+        for p in range(t + AHEAD, min(n, t + AHEAD + pair)):
+            begin(p)
+        for s in (1, 2, 3):
+            for p in range(t - (s - 1) * pair, t - (s - 1) * pair + pair):
+                if 0 <= p < n:
+                    if s == 1:
+                        keep(p).wait()
+                    for copy in stages[s - 1](p):
+                        copy.wait_recv()
+                    for copy in stages[s](p):
+                        copy.start()
+    for p in range(n):
+        third(p)[0].wait_recv()
+    for p in range(n):
+        for stage in stages:
+            for copy in stage(p):
+                copy.wait_send()
+
+
+def gather_call(shards, pieces, collective):
+    count = len(shards)
+    outs = pl.pallas_call(
+        functools.partial(gather_kernel, pieces, count),
+        in_specs=[pl.BlockSpec(memory_space=pl.ANY)] * count,
+        out_specs=[pl.BlockSpec(memory_space=pl.ANY)] * count,
+        out_shape=[jax.ShapeDtypeStruct((4, 2, 2, 2) + s.shape, s.dtype) for s in shards],
+        scratch_shapes=[
+            pltpu.SemaphoreType.DMA((len(pieces), 6)),
+            pltpu.SemaphoreType.DMA((len(pieces), 6)),
+            pltpu.SemaphoreType.DMA((len(pieces),)),
+        ],
+        compiler_params=pltpu.CompilerParams(
+            collective_id=collective, has_side_effects=True, vmem_limit_bytes=VMEM_LIMIT
+        ),
+        name="gather",
+    )(*shards)
+    return [o.reshape(32 * s.shape[0], s.shape[1]) for o, s in zip(outs, shards)]
+
+
+def add_into(total, more):
+    def step(i, carry):
+        total[i] = (total[i].astype(F32) + more[i].astype(F32)).astype(total.dtype)
+        return carry
+
+    lax.fori_loop(0, total.shape[0], step, 0)
+
+
+def scatter_kernel(pieces, count, *refs):
+    ins, outs = refs[:count], refs[count : 2 * count]
+    n = len(pieces)
+    shapes, homes = piece_homes(pieces)
+    scratch = refs[2 * count : 2 * count + 5 * len(shapes)]
+    homes = [
+        (scratch[5 * k : 5 * k + 4], i, scratch[5 * k + 4].at[i % OWN], (k, i % OWN)) for k, i in homes
+    ]
+    sems, local = refs[-3:-1], refs[-1]
+    me = Place()
+    greet(me)
+    every = slice(None)
+
+    def at(p, s):
+        return homes[p][0][s].at[homes[p][1]]
+
+    def part(p, c):
+        array, rows, cols, _ = pieces[p]
+        return ins[array].at[every, every, c, every, rows, cols]
+
+    def load(p):
+        return pltpu.make_async_copy(part(p, me.c), homes[p][2], local.at[homes[p][3]])
+
+    def pairs(p):
+        return [remote(part(p, 1 - me.c), at(p, 0), sems, (p, 0), me.peer(c=1 - me.c))]
+
+    def first(p):
+        if pieces[p][3]:
+            give, peer = at(p, 0).at[every, every, 1 - me.x], me.peer(x=1 - me.x)
+        else:
+            give, peer = at(p, 0).at[every, 1 - me.y], me.peer(y=1 - me.y)
+        return [remote(give, at(p, 1), sems, (p, 1), peer)]
+
+    def second(p):
+        if pieces[p][3]:
+            peer, other = me.peer(y=1 - me.y), 1 - me.y
+        else:
+            peer, other = me.peer(x=1 - me.x), 1 - me.x
+        return [remote(at(p, 1).at[every, other], at(p, 2), sems, (p, 2), peer)]
+
+    def third(p):
+        return [
+            remote(at(p, 2).at[me.up(d)], at(p, 3).at[d - 1], sems, (p, 2 + d), me.peer(z=me.up(d)))
+            for d in (1, 2, 3)
+        ]
+
+    stages = [pairs, first, second, third]
+
+    def settle(p, s):
+        if s == 0:
+            load(p).wait()
+            add_into(at(p, 0), homes[p][2])
+        elif s == 1:
+            kept = at(p, 0).at[every, every, me.x] if pieces[p][3] else at(p, 0).at[every, me.y]
+            add_into(at(p, 1), kept)
+        elif s == 2:
+            add_into(at(p, 2), at(p, 1).at[every, me.y if pieces[p][3] else me.x])
+        else:
+            array, rows, cols, _ = pieces[p]
+            more = at(p, 3)
+            outs[array][rows, cols] = (
+                at(p, 2)[me.z].astype(F32) + more[0].astype(F32) + more[1].astype(F32) + more[2].astype(F32)
+            )
+
+    pair = 2
+
+    def begin(p):
+        load(p).start()
+        for copy in pairs(p):
+            copy.start()
+
+    for p in range(min(n, AHEAD)):
+        begin(p)
+    for t in range(0, n + 3 * pair, pair):
+        for s in range(4):
+            for p in range(t - s * pair, t - s * pair + pair):
+                if 0 <= p < n:
+                    for copy in stages[s](p):
+                        copy.wait_recv()
+                    settle(p, s)
+                    if s < 3:
+                        for copy in stages[s + 1](p):
+                            copy.start()
+            if s == 0:
+                for p in range(t + AHEAD, min(n, t + AHEAD + pair)):
+                    begin(p)
+    for p in range(n):
+        for stage in stages:
+            for copy in stage(p):
+                copy.wait_send()
+
+
+def piece_homes(pieces):
+    shapes, homes = [], []
+    for _, rows, cols, _ in pieces:
+        shape = (rows.stop - rows.start, cols.stop - cols.start)
+        if shape not in shapes:
+            shapes.append(shape)
+        kind = shapes.index(shape)
+        homes.append((kind, sum(k == kind for k, _ in homes)))
+    return shapes, homes
+
+
+def scatter_call(grads, pieces, collective):
+    count = len(grads)
+    shards = [(g.shape[0] // 32, g.shape[1]) for g in grads]
+    grads = [g.reshape((4, 2, 2, 2) + s) for g, s in zip(grads, shards)]
+    shapes, homes = piece_homes(pieces)
+    scratch = []
+    for kind, shape in enumerate(shapes):
+        n = sum(k == kind for k, _ in homes)
+        scratch += [
+            pltpu.VMEM((n, 4, 2, 2) + shape, BF),
+            pltpu.VMEM((n, 4, 2) + shape, BF),
+            pltpu.VMEM((n, 4) + shape, BF),
+            pltpu.VMEM((n, 3) + shape, BF),
+            pltpu.VMEM((OWN, 4, 2, 2) + shape, BF),
+        ]
+    return pl.pallas_call(
+        functools.partial(scatter_kernel, pieces, count),
+        in_specs=[pl.BlockSpec(memory_space=pl.ANY)] * count,
+        out_specs=[pl.BlockSpec(memory_space=pltpu.VMEM)] * count,
+        out_shape=[jax.ShapeDtypeStruct(s, F32) for s in shards],
+        scratch_shapes=scratch + [
+            pltpu.SemaphoreType.DMA((len(pieces), 6)),
+            pltpu.SemaphoreType.DMA((len(pieces), 6)),
+            pltpu.SemaphoreType.DMA((len(shapes), OWN)),
+        ],
+        compiler_params=pltpu.CompilerParams(
+            collective_id=collective, has_side_effects=True, vmem_limit_bytes=VMEM_LIMIT
+        ),
+        name="scatter",
+    )(*grads)
+
+
+def col_pieces(array, rows, cols, width=512, high=None):
+    high = high or rows
+    return [
+        (array, slice(r, r + high), slice(c, c + width), (c // width) % 2 == 0)
+        for r in range(0, rows, high)
+        for c in range(0, cols, width)
+    ]
+
+
+def interleave(one, two):
+    return [p for pair in zip(one, two) for p in pair]
+
+
 def per_device(
     tokens, segments, cotangent, w_q, w_k, w_v, w_o, w_gate, w_up, w_down, g_attn, g_q, g_k, g_ffn
 ):
@@ -610,11 +900,20 @@
     def fetch(weight):
         return lax.all_gather(weight, AXES, axis=0, tiled=True)
 
-    w_qkv = fetch(jnp.concatenate([w_q, w_k, w_v], axis=1))
-    w_o = fetch(w_o)
-    w_gate = fetch(w_gate)
-    w_up = fetch(w_up)
+    w_qkv = jnp.concatenate([w_q, w_k, w_v], axis=1)
+    own_kernels = (lax.axis_size("dp"), lax.axis_size("ctx")) == (16, 2)
+    share = w_q.shape[0]
+    gate_pieces = interleave(
+        [(0,) + p[1:3] + (True,) for p in col_pieces(0, share, w_gate.shape[1])],
+        [(1,) + p[1:3] + (False,) for p in col_pieces(1, share, w_up.shape[1])],
+    )
+    qkv_pieces = col_pieces(0, share, w_qkv.shape[1])
+    o_pieces = col_pieces(1, share, w_o.shape[1])
     w_down = fetch(w_down)
+    if own_kernels:
+        w_qkv, w_o = gather_call([w_qkv, w_o], qkv_pieces + o_pieces, 0)
+    else:
+        w_qkv, w_o, w_gate, w_up = fetch(w_qkv), fetch(w_o), fetch(w_gate), fetch(w_up)
 
     seg_rows = lax.dynamic_slice_in_dim(segments, row_start, rows, 1)
     first = jnp.sum((segments[:, None, :] < seg_rows[:, :, None]).astype(jnp.int32), axis=-1)
@@ -649,14 +948,20 @@
         ).astype(F32)
 
     cotangent = cotangent.reshape(total, width)
+    if own_kernels:
+        normed_two, w_gate, w_up = lax.optimization_barrier((normed_two, w_gate, w_up))
+        w_gate, w_up = gather_call([w_gate, w_up], gate_pieces, 1)
     ffn, d_normed_two, grad_gate, grad_up, grad_down = ffn_call(
         normed_two, cotangent, w_gate, w_up, w_down
     )
-    out_gate, out_up, out_down = send(grad_gate), send(grad_up), send(grad_down)
+    if own_kernels:
+        out_gate, out_up = scatter_call([grad_gate, grad_up], gate_pieces, 2)
+    else:
+        out_gate, out_up, out_down = send(grad_gate), send(grad_up), send(grad_down)
     outputs, d_hidden, d_low, d_out, delta, grad_gffn = middle_call(
         ffn, d_normed_two, hidden, cotangent, g_ffn[None, :], w_o, mixed, totals, ones, head
     )
-    out_o = send(mm(attended, d_low, TN))
+    grad_o = mm(attended, d_low, TN).astype(BF)
     dq, dk, dv = attend_back_call(
         q, d_out.reshape(q.shape), delta.reshape(q.shape), kv, first[:, None, :], low, start,
         block_q, block_k,
@@ -668,7 +973,14 @@
         dq.reshape(total, q_width), dkv[:, :kv_width], dkv[:, kv_width:], raw, gqk, cos, sin, ones,
         w_qkv, x, g_attn[None, :], d_hidden, head,
     )
-    out_qkv = send(mm(normed, d_qkv, TN))
+    grad_qkv = mm(normed, d_qkv, TN).astype(BF)
+    if own_kernels:
+        down_pieces = [(2,) + p[1:] for p in col_pieces(2, w_down.shape[0] // 32, width, 256, 48)]
+        out_qkv, out_o, out_down = scatter_call(
+            [grad_qkv, grad_o, grad_down], down_pieces + o_pieces + qkv_pieces, 3
+        )
+    else:
+        out_qkv, out_o = send(grad_qkv), send(grad_o)
 
     def fold(grad):
         return jnp.sum(grad.reshape(LANES // head, head), axis=0)

time: 1440 us -> 830 us (0.58)
  waiting for transfers between devices: 1080 us -> 54.6 us
  Pallas kernels: 260 us -> 681 us
    reduce_scatter x5 -> x0, waiting for transfers between devices: 627 us -> none  [send(): lax.psum_scatter(grad.astype(BF), AXES, scatter_dimension=0, tiled=True)]
    pallas_call x0 -> x4, Pallas kernels: none -> 427 us  [the longest x2 253 us: scatter_call(): pl.pallas_call(functools.partial(scatter_kernel, pieces, count), in_specs...]
    all_gather x5 -> x1, waiting for transfers between devices: 329 us -> 0.02 us  [fetch(): return lax.all_gather(weight, AXES, axis=0, tiled=True)]
    reduce_scatter x1, waiting for transfers between devices: 68.3 us -> 0.01 us  [per_device(): lax.psum_scatter(jnp.concatenate([dk, dv], axis=2), 'ctx', scatter_dimens...]
  transfers between devices with their start and end apart: 12 -> 3, of which waited for: 12 -> 1; matrix products, arithmetic and copies ran while one was open for 3% -> 1% of each run, Pallas kernels for 4% -> 40%
where the time goes in v2:
time: 830 us; the launch traced here: 831 us
  Pallas kernels  681 us (82%)
  waiting for transfers between devices  54.6 us (7%)
  blocking collectives  39.4 us (5%)
  local copies, waits for them, and re-layouts  16.2 us (2%)
  other arithmetic  14.1 us (2%)
  between operations  13.9 us (2%)
  matrix products  12.3 us (1%)
    pallas_call x2, Pallas kernels, scatter_call(): pl.pallas_call(functools.partial(scatter_kernel, pieces, count), in_specs...  253 us
    pallas_call x2, Pallas kernels, gather_call(): pl.pallas_call(functools.partial(gather_kernel, pieces, count), in_specs=...  174 us
    pallas_call x1, Pallas kernels, ffn_call(): pl.pallas_call(functools.partial(ffn_kernel, block_t), grid=(hidden // ch...  113 us
    all_gather x1, waiting for transfers between devices, per_device(): lax.all_gather(kv.reshape(seqs, rows, 2 * kv_width), 'ctx', axis=1, tiled...  53.8 us
    pallas_call x1, Pallas kernels, attend_back_call(): pl.pallas_call(functools.partial(attend_back_kernel, block_q, block_k, he...  50.5 us
    psum x1, blocking collectives, per_device(): lax.psum((grad_gattn[0], fold(grad_gq), fold(grad_gk), grad_gffn[0]), AXES)  39.4 us
    pallas_call x1, Pallas kernels, attend_call(): pl.pallas_call(functools.partial(attend_kernel, block_q, block_k, heads),...  29.5 us
    pallas_call x1, Pallas kernels, last_call(): pl.pallas_call(functools.partial(last_kernel, q_width, kv_width, head, he...  17.9 us
  transfers between devices with their start and end apart: 3, of which 1 were waited for; matrix products, arithmetic and copies ran while one was open for 1% of the time, Pallas kernels for 40%

profile of v2, /device:TPU:0, one launch (start us, length us, event | category | flops | bytes accessed | tf_op | source)
XLA Modules:
  0.0 831.3 jit_solution(12070307857350738465)
XLA Ops:
  7.3 0.7 constant_dynamic-slice_fusion
  8.0 1.3 convert_reduce_fusion
  9.2 0.8 compare_convert_fusion.ones_ref
  10.0 1.3 concatenate.16
  11.9 1.9 fusion
  13.8 1.5 pad_maximum_fusion.3.refs_0_
  15.4 45.7 %gather.2 = (bf16[4,2,2,2,32,2048]{5,4,3,2,1,0:T(8,128)(2,1)}, bf16[4,2,2,2,32,1024]{5,4,3,2,1,0:T(8,128)(2,1)}) custom-call(bf16[32,2048]{1,0:T(8,128)(2,1)} %pad_maximum_fusion.3.refs_0_, bf16[32,1024]{1,0:T(8,128)(2,1)} %refs_1_.1), custom_call_target="tpu_custom_call" | custom-call | tf_op jit(solution)/shard_map/gather/pallas_call | solution.py:714
  61.0 1.8 pad_maximum_fusion.1
  62.9 17.2 %qkv_rope.1 = (bf16[1024,1024]{1,0:T(8,128)(2,1)}, bf16[1024,1024]{1,0:T(8,128)(2,1)}, bf16[1024,1024]{1,0:T(8,128)(2,1)}, f32[1024,1536]{1,0:T(8,128)}) custom-call(bf16[1024,1024]{1,0:T(8,128)(2,1)} %bitcast.34, bf16[1024,2048]{1,0:T(8,128)(2,1)} %bitcast.37, f32[1,1024]{1,0:T(1,128)} %bitcast.59, f32[1,1536]{1,0:T(1,128)} %broadcast_in_dim.14.gqk_ref, ...), custom_call_target="tpu_custom_call" | custom-call | tf_op jit(solution)/shard_map/qkv_rope/pallas_call | solution.py:105
  80.1 0.7 all-gather.5.cloned.1.call-update
  81.8 1.0 copy.30.first_ref
  83.4 53.8 %all-gather.3.cloned.1.call-done.k_ref.v_ref = bf16[2,1024,1024]{2,1,0:T(8,128)(2,1)} async-done(((bf16[2,512,1024]{2,1,0:T(8,128)(2,1)}), bf16[2,1024,1024]{2,1,0:T(8,128)(2,1)}) %all-gather.3.cloned.1.call-update) | async-done | bytes 4194320 | tf_op jit(solution)/shard_map/all_gather | solution.py:939
  137.2 29.5 %attend.1 = (f32[2,512,1024]{2,1,0:T(8,128)}, f32[2,512,1024]{2,1,0:T(8,128)}) custom-call(s32[2,4]{1,0:T(2,128)} %and_select_fusion.1.low_ref, s32[1]{0:T(128)} %bitcast.start_ref, bf16[2,512,1024]{2,1,0:T(8,128)(2,1)} %bitcast.46, bf16[2,1024,1024]{2,1,0:T(8,128)(2,1)} %all-gather.3.cloned.1.call-done.k_ref.v_ref, ...), custom_call_target="tpu_custom_call" | custom-call | tf_op jit(solution)/shard_map/attend/pallas_call | solution.py:198
  166.7 8.3 hidden.1
  175.0 128.3 %gather.3 = (bf16[4,2,2,2,32,4608]{5,4,3,2,1,0:T(8,128)(2,1)}, bf16[4,2,2,2,32,4608]{5,4,3,2,1,0:T(8,128)(2,1)}) custom-call(bf16[32,4608]{1,0:T(8,128)(2,1)} %refs_0_, bf16[32,4608]{1,0:T(8,128)(2,1)} %refs_1_.2), custom_call_target="tpu_custom_call" | custom-call | tf_op jit(solution)/shard_map/gather/pallas_call | solution.py:714
  303.3 113.2 %ffn.1 = (f32[1024,1024]{1,0:T(8,128)}, f32[1024,1024]{1,0:T(8,128)}, bf16[1024,4608]{1,0:T(8,128)(2,1)}, bf16[1024,4608]{1,0:T(8,128)(2,1)}, bf16[4608,1024]{1,0:T(8,128)(2,1)}) custom-call(bf16[1024,1024]{1,0:T(8,128)(2,1)} %get-tuple-element.59.n_ref, f32[1024,1024]{1,0:T(8,128)} %bitcast.48, bf16[1024,4608]{1,0:T(8,128)(2,1)} %bitcast.66, ...), custom_call_target="tpu_custom_call" | custom-call | flops 86973087744 | bytes 56623104 | tf_op jit(solution)/shard_map/ffn/pallas_call | solution.py:437
  416.5 17.1 %middle.1 = (bf16[1024,1024]{1,0:T(8,128)(2,1)}, f32[1024,1024]{1,0:T(8,128)}, bf16[1024,1024]{1,0:T(8,128)(2,1)}, bf16[1024,1024]{1,0:T(8,128)(2,1)}, f32[1024,1024]{1,0:T(8,128)}, /*index=5*/f32[1,1024]{1,0:T(1,128)}) custom-call(f32[1024,1024]{1,0:T(8,128)} %get-tuple-element.64.f_ref, f32[1024,1024]{1,0:T(8,128)} %get-tuple-element.65.dn_ref, ...), custom_call_target="tpu_custom_call" | custom-call | tf_op jit(solution)/shard_map/middle/pallas_call | solution.py:503
  433.5 50.5 %attend_back.1 = (f32[2,512,1024]{2,1,0:T(8,128)}, bf16[2,1024,512]{2,1,0:T(8,128)(2,1)}, bf16[2,1024,512]{2,1,0:T(8,128)(2,1)}) custom-call(s32[2,4]{1,0:T(2,128)} %and_select_fusion.1.low_ref, s32[1]{0:T(128)} %bitcast.start_ref, bf16[2,512,1024]{2,1,0:T(8,128)(2,1)} %bitcast.47, bf16[2,512,1024]{2,1,0:T(8,128)(2,1)} %bitcast.57, ...), custom_call_target="tpu_custom_call" | custom-call | tf_op jit(solution)/shard_map/attend_back/pallas_call | solution.py:322
  484.1 4.8 pad_maximum_fusion
  488.9 169.5 %scatter.3 = (f32[32,4608]{1,0:T(8,128)}, f32[32,4608]{1,0:T(8,128)}) custom-call(bf16[4,2,2,2,32,4608]{5,4,3,2,1,0:T(8,128)(2,1)} %bitcast.41, bf16[4,2,2,2,32,4608]{5,4,3,2,1,0:T(8,128)(2,1)} %bitcast.42), custom_call_target="tpu_custom_call" | custom-call | tf_op jit(solution)/shard_map/scatter/pallas_call | solution.py:858
  658.4 3.7 convolution_convert_fusion.1
  662.1 3.0 fusion.1
  665.1 17.9 %last.1 = (bf16[1024,2048]{1,0:T(8,128)(2,1)}, f32[1024,1024]{1,0:T(8,128)}, f32[1,1024]{1,0:T(1,128)}, f32[1,128]{1,0:T(1,128)}, f32[1,128]{1,0:T(1,128)}) custom-call(f32[1024,1024]{1,0:T(8,128)} %bitcast.50, bf16[1024,512]{1,0:T(8,128)(2,1)} %get-tuple-element.98.dk_ref, bf16[1024,512]{1,0:T(8,128)(2,1)} %get-tuple-element.97.dv_ref, ...), custom_call_target="tpu_custom_call" | custom-call | tf_op jit(solution)/shard_map/last/pallas_call | solution.py:576
  683.0 8.6 %convolution_convert_fusion = bf16[1024,2048]{1,0:T(8,128)(2,1)} fusion(bf16[1024,1024]{1,0:T(8,128)(2,1)S(1)} %copy-done.4, bf16[1024,2048]{1,0:T(8,128)(2,1)} %get-tuple-element.78), kind=kOutput, calls=%fused_computation.2 | convolution fusion | flops 4297064448 | bytes 10485760 | tf_op jit(solution)/shard_map/dot_general | solution.py:25
  691.5 83.5 %scatter.2 = (f32[32,2048]{1,0:T(8,128)}, f32[32,1024]{1,0:T(8,128)}, f32[144,1024]{1,0:T(8,128)}) custom-call(bf16[4,2,2,2,32,2048]{5,4,3,2,1,0:T(8,128)(2,1)} %bitcast.53, bf16[4,2,2,2,32,1024]{5,4,3,2,1,0:T(8,128)(2,1)} %bitcast.54, bf16[4,2,2,2,144,1024]{5,4,3,2,1,0:T(8,128)(2,1)} %bitcast.43), custom_call_target="tpu_custom_call" | custom-call | tf_op jit(solution)/shard_map/scatter/pallas_call | solution.py:858
  775.1 1.5 fusion.2
  776.6 1.6 slice.21
  780.3 39.4 %all-reduce = (f32[1024]{0:T(1024)}, f32[64]{0:T(128)}, f32[64]{0:T(128)}, f32[1024]{0:T(1024)}) all-reduce(f32[1024]{0:T(1024)S(1)} %bitcast.65, f32[64]{0:T(128)S(1)} %reduce_sum.28, f32[64]{0:T(128)S(1)} %reduce_sum.29, f32[1024]{0:T(1024)S(1)} %bitcast.64), channel_id=1, replica_groups=mesh['dp'=16,'ctx'=2] {'dp','ctx'}, use_global_device_ids=true, to_apply=%region_2.3 | all-reduce | flops 2176 | bytes 17408 | tf_op jit(solution)/shard_map/psum | solution.py:988
  819.7 1.6 copy.36
  821.2 0.8 copy.37
  822.1 0.8 copy.38
  822.9 1.9 copy.39
  (41 shorter events, 4.3 us)
Async XLA Ops:
  7.2 130.0 %all-gather.3.cloned.1.call-start = ((), (), s32[]{:S(2)}) async-start(), calls=%async_computation.1 | async-start | bytes 6291456 | tf_op jit(solution)/shard_map/all_gather | solution.py:939
  80.1 223.2 %all-gather.5.cloned.1.call-start = ((), (), s32[]{:S(2)}) async-start(), calls=%async_computation.2 | async-start | bytes 9732096 | tf_op jit(solution)/shard_map/all_gather | solution.py:901
  80.9 581.2 %reduce-scatter.2.cloned.1.call-start = ((), (), s32[]{:S(2)}) async-start(), calls=%async_computation.3 | async-start | bytes 6291456 | tf_op jit(solution)/shard_map/reduce_scatter | solution.py:969
  488.9 169.5 %copy-start.5 = (bf16[1024,1024]{1,0:T(8,128)(2,1)S(1)}, bf16[1024,1024]{1,0:T(8,128)(2,1)}, u32[]{:S(2)}) copy-start(bf16[1024,1024]{1,0:T(8,128)(2,1)} %get-tuple-element.79) | copy-start | bytes 6291460
  488.9 169.5 %copy-start.6 = (bf16[1024,1024]{1,0:T(8,128)(2,1)S(1)}, bf16[1024,1024]{1,0:T(8,128)(2,1)}, u32[]{:S(2)}) copy-start(bf16[1024,1024]{1,0:T(8,128)(2,1)} %get-tuple-element.80) | copy-start | bytes 6291460
  665.1 17.9 %copy-start.4 = (bf16[1024,1024]{1,0:T(8,128)(2,1)S(1)}, bf16[1024,1024]{1,0:T(8,128)(2,1)}, u32[]{:S(2)}) copy-start(bf16[1024,1024]{1,0:T(8,128)(2,1)} %get-tuple-element.77) | copy-start | bytes 6291460
  691.5 87.2 %copy-start.8 = (f32[1,128]{1,0:T(1,128)S(1)}, f32[1,128]{1,0:T(1,128)}, u32[]{:S(2)}) copy-start(f32[1,128]{1,0:T(1,128)} %get-tuple-element.90) | copy-start | bytes 1540
  691.5 88.0 %copy-start.7 = (f32[1,128]{1,0:T(1,128)S(1)}, f32[1,128]{1,0:T(1,128)}, u32[]{:S(2)}) copy-start(f32[1,128]{1,0:T(1,128)} %get-tuple-element.91) | copy-start | bytes 1540
  691.5 88.7 %copy-start.2 = (f32[1,1024]{1,0:T(1,128)S(1)}, f32[1,1024]{1,0:T(1,128)}, u32[]{:S(2)}) copy-start(f32[1,1024]{1,0:T(1,128)} %get-tuple-element.92) | copy-start | bytes 12292
  691.5 88.7 %copy-start.3 = (f32[1,1024]{1,0:T(1,128)S(1)}, f32[1,1024]{1,0:T(1,128)}, u32[]{:S(2)}) copy-start(f32[1,1024]{1,0:T(1,128)} %get-tuple-element.89) | copy-start | bytes 12292
  691.5 129.7 %copy-start.1 = (f32[32,4608]{1,0:T(8,128)S(1)}, f32[32,4608]{1,0:T(8,128)}, u32[]{:S(2)}) copy-start(f32[32,4608]{1,0:T(8,128)} %get-tuple-element.125) | copy-start | bytes 1769476
  691.5 130.5 %copy-start = (f32[32,4608]{1,0:T(8,128)S(1)}, f32[32,4608]{1,0:T(8,128)}, u32[]{:S(2)}) copy-start(f32[32,4608]{1,0:T(8,128)} %get-tuple-element.126) | copy-start | bytes 1769476
Sparse Core Ops, SparseCore 0:
  80.2 56.9 all-gather.2
  140.1 104.9 all-gather.4
  489.0 131.3 reduce-scatter.1

commit v3 on v2

--- a/solution.py
+++ b/solution.py
@@ -67,58 +67,60 @@
     return jnp.concatenate([table] * (width // table.shape[1]), axis=1)
 
 
-def qkv_kernel(
-    q_width, kv_width, head, scale,
-    x_ref, w_ref, g_ref, gqk_ref, cos_ref, sin_ref, ones_ref,
-    normed_ref, q_ref, kv_ref, raw_ref,
+def project_kernel(
+    rope_width, head, scale,
+    x_ref, w_ref, g_ref, gain_ref, cos_ref, sin_ref, ones_ref,
+    normed_ref, out_ref, raw_ref,
 ):
     x = x_ref[...].astype(F32)
     inverse = lax.rsqrt(jnp.mean(x * x, axis=-1, keepdims=True) + epsilon)
     normed = (x * inverse * g_ref[...]).astype(BF)
     normed_ref[...] = normed
-    qk = q_width + kv_width
     ones = ones_ref[...]
     wide = ones.shape[0]
     cos = spread(cos_ref[...], wide)
     sin = spread(sin_ref[...], wide)
-    for c in range(0, qk, wide):
+    for c in range(0, rope_width, wide):
         raw = mm(normed, w_ref[:, c : c + wide])
         raw_ref[:, c : c + wide] = raw
         inv = lax.rsqrt(head_sum(raw * raw, ones) * (1.0 / head) + epsilon)
-        field = raw * inv * gqk_ref[:, c : c + wide]
+        field = raw * inv * gain_ref[:, c : c + wide]
         turned = (field * cos + swap_halves(field, head) * sin).astype(BF)
-        if c < q_width:
-            q_ref[:, c : c + wide] = turned * jnp.asarray(scale, BF)
-        else:
-            kv_ref[:, c - q_width : c - q_width + wide] = turned
-    kv_ref[:, kv_width:] = mm(normed, w_ref[:, qk:]).astype(BF)
-
-
-def qkv_call(x, w, g, gqk, cos, sin, ones, q_width, kv_width, head):
+        out_ref[:, c : c + wide] = turned if scale is None else turned * jnp.asarray(scale, BF)
+    if rope_width < w_ref.shape[1]:
+        out_ref[:, rope_width:] = mm(normed, w_ref[:, rope_width:]).astype(BF)
+
+
+def project_call(x, w, cols, rope_width, g, gains, cos, sin, ones, head, scale, name):
     total, width = x.shape
     block = largest_block(total, 256)
-    qk = q_width + kv_width
+    at, count = cols[0] // cols[1], cols[1]
 
     def rows(n):
         return pl.BlockSpec((block, n), lambda i: (i, 0))
 
     return pl.pallas_call(
-        functools.partial(qkv_kernel, q_width, kv_width, head, head ** (-0.5)),
+        functools.partial(project_kernel, rope_width, head, scale),
         grid=(total // block,),
         in_specs=[
-            rows(width), resident(w.shape), resident(g.shape), resident(gqk.shape),
+            rows(width),
+            pl.BlockSpec((width, count), lambda i: (0, at), pipeline_mode=pl.Buffered(1)),
+            resident(g.shape), resident(gains.shape),
             rows(LANES), rows(LANES), resident(ones.shape),
         ],
-        out_specs=[rows(width), rows(q_width), rows(2 * kv_width), rows(qk)],
+        out_specs=[rows(width), rows(count), rows(rope_width)],
         out_shape=[
             jax.ShapeDtypeStruct((total, width), BF),
-            jax.ShapeDtypeStruct((total, q_width), BF),
-            jax.ShapeDtypeStruct((total, 2 * kv_width), BF),
-            jax.ShapeDtypeStruct((total, qk), F32),
+            jax.ShapeDtypeStruct((total, count), BF),
+            jax.ShapeDtypeStruct((total, rope_width), F32),
         ],
         compiler_params=params(),
-        name="qkv_rope",
-    )(x, w, g, gqk, cos, sin, ones)
+        cost_estimate=pl.CostEstimate(
+            flops=2 * total * width * count, bytes_accessed=2 * width * count + 10 * total * count,
+            transcendentals=0,
+        ),
+        name=name,
+    )(x, w, g, gains, cos, sin, ones)
 
 
 def pad_head(pair, odd, fill):
@@ -129,13 +131,13 @@
 
 
 def attend_kernel(
-    block_q, block_k, heads,
-    low_ref, start_ref, q_ref, k_ref, v_ref, first_ref,
-    out_ref, total_ref, k_scr, v_scr,
+    block_q, block_k, heads, more, last_part,
+    low_ref, high_ref, start_ref, q_ref, k_ref, v_ref, first_ref, *refs,
 ):
+    prior = refs[:2] if more else ()
+    out_ref, total_ref, k_scr, v_scr = refs[len(prior) :]
     s = pl.program_id(0)
     rows = q_ref.shape[1]
-    length = k_ref.shape[1]
     start = start_ref[0]
     half = LANES // 2
     for h in range(heads):
@@ -169,9 +171,8 @@
                 new.append(sums[h] + mm(expo, v_scr[h, pl.ds(key_at, block_k), :]))
             return tuple(new)
 
-        end = (start + at + block_q - 1) // block_k + 1
         sums = lax.fori_loop(
-            low_ref[s, i], end, k_step,
+            low_ref[s, i], high_ref[s, i], k_step,
             tuple(jnp.zeros((2 * block_q, LANES), F32) for _ in range(heads)),
         )
         for h in range(heads):
@@ -179,33 +180,35 @@
             both = jnp.where(lane < half, even, pltpu.roll(odd, half, 1))
             tot = jnp.where(lane < half, pltpu.roll(even, half, 1), odd)
             cols = slice(h * LANES, (h + 1) * LANES)
-            out_ref[0, pl.ds(at, block_q), cols] = both / tot
+            if more:
+                both += prior[0][0, pl.ds(at, block_q), cols]
+                tot += prior[1][0, pl.ds(at, block_q), cols]
+            out_ref[0, pl.ds(at, block_q), cols] = both / tot if last_part else both
             total_ref[0, pl.ds(at, block_q), cols] = tot
         return carry
 
     lax.fori_loop(0, rows // block_q, q_step, 0)
 
 
-def attend_call(q, kv, first, low, start, block_q, block_k):
+def attend_call(q, kv, first, keys, block_q, block_k, prior=(), last_part=True):
     seqs, rows, q_width = q.shape
     length = kv.shape[1]
-    kv_width = kv.shape[2] // 2
     kv_heads = q_width // LANES
     heads = largest_block(kv_heads, 4)
     steps = kv_heads // heads
     half = LANES // 2
     spec_q = pl.BlockSpec((1, rows, heads * LANES), lambda s, p, *_: (s, 0, p))
     return pl.pallas_call(
-        functools.partial(attend_kernel, block_q, block_k, heads),
+        functools.partial(attend_kernel, block_q, block_k, heads, bool(prior), last_part),
         grid_spec=pltpu.PrefetchScalarGridSpec(
-            num_scalar_prefetch=2,
+            num_scalar_prefetch=3,
             grid=(seqs, steps),
             in_specs=[
                 spec_q,
                 pl.BlockSpec((1, length, heads * half), lambda s, p, *_: (s, 0, p)),
                 pl.BlockSpec((1, length, heads * half), lambda s, p, *_: (s, 0, p + steps)),
                 pl.BlockSpec((1, rows, 1), lambda s, p, *_: (s, 0, 0)),
-            ],
+            ] + [spec_q] * len(prior),
             out_specs=[spec_q, spec_q],
             scratch_shapes=[
                 pltpu.VMEM((heads, length, LANES), BF),
@@ -214,15 +217,20 @@
         ),
         out_shape=[jax.ShapeDtypeStruct(q.shape, F32)] * 2,
         compiler_params=params(),
+        cost_estimate=pl.CostEstimate(
+            flops=4 * seqs * rows * length * q_width, bytes_accessed=16 * seqs * rows * q_width,
+            transcendentals=0,
+        ),
         name="attend",
-    )(low, start, q, kv, kv, first)
+    )(*keys, q, kv, kv, first[:, :, None], *prior)
 
 
 def attend_back_kernel(
-    block_q, block_k, heads,
-    low_ref, start_ref, q_ref, do_ref, de_ref, k_ref, v_ref, first_ref,
-    dq_ref, dk_ref, dv_ref, k_scr, v_scr, dk_scr, dv_scr,
+    block_q, block_k, heads, more,
+    low_ref, high_ref, start_ref, q_ref, do_ref, de_ref, k_ref, v_ref, first_ref, *refs,
 ):
+    prior_ref = refs[0] if more else None
+    dq_ref, dk_ref, dv_ref, k_scr, v_scr, dk_scr, dv_scr = refs[int(more) :]
     s = pl.program_id(0)
     rows = q_ref.shape[1]
     length = k_ref.shape[1]
@@ -286,17 +294,17 @@
                 new.append(sums[h] + mm(d_scores, k, TN))
             return tuple(new)
 
-        end = (start + at + block_q - 1) // block_k + 1
         sums = lax.fori_loop(
-            low_ref[s, i], end, k_step,
+            low_ref[s, i], high_ref[s, i], k_step,
             tuple(jnp.zeros((2 * block_q, LANES), F32) for _ in range(heads)),
         )
         for h in range(heads):
             even, odd = sums[h][:block_q], sums[h][block_q:]
             cols = slice(h * LANES, (h + 1) * LANES)
-            dq_ref[0, pl.ds(at, block_q), cols] = jnp.where(
-                lane < half, even, pltpu.roll(odd, half, 1)
-            )
+            grad = jnp.where(lane < half, even, pltpu.roll(odd, half, 1))
+            if more:
+                grad += prior_ref[0, pl.ds(at, block_q), cols]
+            dq_ref[0, pl.ds(at, block_q), cols] = grad
         return carry
 
     lax.fori_loop(0, rows // block_q, q_step, 0)
@@ -309,7 +317,7 @@
             ).astype(BF)
 
 
-def attend_back_call(q, d_out, delta, kv, first, low, start, block_q, block_k):
+def attend_back_call(q, d_out, delta, kv, first, keys, block_q, block_k, prior=()):
     seqs, rows, q_width = q.shape
     length = kv.shape[1]
     kv_width = kv.shape[2] // 2
@@ -320,15 +328,15 @@
     spec_q = pl.BlockSpec((1, rows, heads * LANES), lambda s, p, *_: (s, 0, p))
     spec_kv = pl.BlockSpec((1, length, heads * half), lambda s, p, *_: (s, 0, p))
     return pl.pallas_call(
-        functools.partial(attend_back_kernel, block_q, block_k, heads),
+        functools.partial(attend_back_kernel, block_q, block_k, heads, bool(prior)),
         grid_spec=pltpu.PrefetchScalarGridSpec(
-            num_scalar_prefetch=2,
+            num_scalar_prefetch=3,
             grid=(seqs, steps),
             in_specs=[
                 spec_q, spec_q, spec_q, spec_kv,
                 pl.BlockSpec((1, length, heads * half), lambda s, p, *_: (s, 0, p + steps)),
                 pl.BlockSpec((1, 1, rows), lambda s, p, *_: (s, 0, 0)),
-            ],
+            ] + [spec_q] * len(prior),
             out_specs=[spec_q, spec_kv, spec_kv],
             scratch_shapes=[
                 pltpu.VMEM((heads, length, LANES), BF),
@@ -343,8 +351,12 @@
             jax.ShapeDtypeStruct((seqs, length, kv_width), BF),
         ],
         compiler_params=params(),
+        cost_estimate=pl.CostEstimate(
+            flops=10 * seqs * rows * length * q_width, bytes_accessed=16 * seqs * rows * q_width,
+            transcendentals=0,
+        ),
         name="attend_back",
-    )(low, start, q, d_out, delta, kv, kv, first)
+    )(*keys, q, d_out, delta, kv, kv, first[:, None, :], *prior)
 
 
 def hidden_kernel(a_ref, w_ref, x_ref, g_ref, att_ref, hidden_ref, normed_ref):
@@ -380,17 +392,20 @@
 
 
 def ffn_kernel(
-    block_t,
+    block_t, steps,
     n_ref, c_ref, wg_ref, wu_ref, wd_ref,
-    out_ref, dn_ref, gg_ref, gu_ref, gd_ref,
-    n_scr, c_scr, act_scr, dg_scr, du_scr,
+    out_ref, dn_ref, gd_ref, gg_ref, gu_ref,
+    n_scr, act_scr, dg_scr, du_scr, *refs,
 ):
     total, width = n_ref.shape
     chunk = wg_ref.shape[1]
-
-    @pl.when(pl.program_id(0) == 0)
+    step = pl.program_id(0)
+    sums = GradSums(gg_ref, gu_ref, refs) if refs else None
+
+    @pl.when(step == 0)
     def _():
-        c_scr[...] = c_ref[...].astype(BF)
+        if sums:
+            sums.hello()
         n_scr[...] = n_ref[...].T
         out_ref[...] = jnp.zeros_like(out_ref)
         dn_ref[...] = jnp.zeros_like(dn_ref)
@@ -400,7 +415,7 @@
         normed = n_ref[at, :]
         gate = mm(normed, wg_ref[...])
         up = mm(normed, wu_ref[...])
-        d_act = mm(c_scr[at, :], wd_ref[...], NT)
+        d_act = mm(c_ref[at, :], wd_ref[...], NT)
         sig = 1.0 / (1.0 + jnp.exp(-gate))
         silu = gate * sig
         act = (silu * up).astype(BF)
@@ -413,52 +428,158 @@
         dn_ref[at, :] += mm(d_gate, wg_ref[...], NT) + mm(d_up, wu_ref[...], NT)
         return carry
 
-    lax.fori_loop(0, total // block_t, t_step, 0)
-
     def d_step(i, carry):
         at = pl.ds(pl.multiple_of(i * 256, 256), 256)
         normed = n_scr[at, :]
-        gg_ref[at, :] = mm(normed, dg_scr[...]).astype(BF)
-        gu_ref[at, :] = mm(normed, du_scr[...]).astype(BF)
+        gate = mm(normed, dg_scr[...]).astype(BF)
+        up = mm(normed, du_scr[...]).astype(BF)
+        if sums:
+            sums.keep(step, i, gate, up)
+        else:
+            gg_ref[at, :] = gate
+            gu_ref[at, :] = up
         return carry
 
-    lax.fori_loop(0, width // 256, d_step, 0)
-    for c in range(0, chunk, 256):
-        gd_ref[c : c + 256, :] = mm(act_scr[:, c : c + 256], c_scr[...], TN).astype(BF)
-
-
-def ffn_call(normed, cotangent, w_gate, w_up, w_down):
+    @pl.when(step < steps)
+    def _():
+        lax.fori_loop(0, total // block_t, t_step, 0)
+        lax.fori_loop(0, width // 256, d_step, 0)
+        for c in range(0, chunk, 256):
+            gd_ref[c : c + 256, :] = mm(act_scr[:, c : c + 256], c_ref[...], TN).astype(BF)
+
+    if sums:
+        sums.advance(step, steps)
+
+
+class GradSums:
+    def __init__(self, gg_ref, gu_ref, refs):
+        self.outs = (gg_ref, gu_ref)
+        self.made, self.r0, self.r1, self.r2, self.r3, self.send, self.recv = refs
+        self.me = Place()
+
+    def hello(self):
+        barrier = pltpu.get_barrier_semaphore()
+        for peer in self.me.peers():
+            pl.semaphore_signal(
+                barrier, inc=1, device_id=peer, device_id_type=pl.DeviceIdType.MESH
+            )
+
+    def keep(self, step, i, gate, up):
+        shape = self.made.shape[3:]
+        self.made[lax.rem(step, 2), 0, i] = gate.reshape(shape)
+        self.made[lax.rem(step, 2), 1, i] = up.reshape(shape)
+
+    def hop(self, k, j, s):
+        me, every = self.me, slice(None)
+        sems = (self.send, self.recv)
+        r0, r1, r2, r3 = (r.at[k, j] for r in (self.r0, self.r1, self.r2, self.r3))
+        to_x, to_y = me.peer(x=1 - me.x), me.peer(y=1 - me.y)
+        if s == 0:
+            give = self.made.at[lax.rem(k, 2), j, every, every, 1 - me.c]
+            return [remote(give, r0, sems, (k, j, 0), me.peer(c=1 - me.c))]
+        if s == 1:
+            if j == 0:
+                return [remote(r0.at[every, every, 1 - me.x], r1, sems, (k, j, 1), to_x)]
+            return [remote(r0.at[every, 1 - me.y], r1, sems, (k, j, 1), to_y)]
+        if s == 2:
+            other, peer = (1 - me.y, to_y) if j == 0 else (1 - me.x, to_x)
+            return [remote(r1.at[every, other], r2, sems, (k, j, 2), peer)]
+        return [
+            remote(r2.at[me.up(d)], r3.at[d - 1], sems, (k, j, 2 + d), me.peer(z=me.up(d)))
+            for d in (1, 2, 3)
+        ]
+
+    def settle(self, k, j, s):
+        me, every = self.me, slice(None)
+        r0, r1, r2, r3 = (r.at[k, j] for r in (self.r0, self.r1, self.r2, self.r3))
+        for copy in self.hop(k, j, s):
+            copy.wait()
+        if s == 0:
+            add_into(r0, self.made.at[lax.rem(k, 2), j, every, every, me.c])
+        elif s == 1:
+            add_into(r1, r0.at[every, every, me.x] if j == 0 else r0.at[every, me.y])
+        elif s == 2:
+            add_into(r2, r1.at[every, me.y if j == 0 else me.x])
+        else:
+            width = r2.shape[-1]
+            cols = pl.ds(pl.multiple_of(k * width, width), width)
+            self.outs[j][:, cols] = (
+                r2[me.z].astype(F32) + r3[0].astype(F32) + r3[1].astype(F32) + r3[2].astype(F32)
+            )
+
+    def advance(self, step, steps):
+        @pl.when(step == 0)
+        def _():
+            pl.semaphore_wait(pltpu.get_barrier_semaphore(), len(self.me.peers()))
+
+        for s in (3, 2, 1, 0):
+            k = step - 1 - s
+
+            @pl.when((k >= 0) & (k < steps))
+            def _(s=s, k=k):
+                for j in (0, 1):
+                    self.settle(k, j, s)
+                    if s < 3:
+                        for copy in self.hop(k, j, s + 1):
+                            copy.start()
+
+        @pl.when(step < steps)
+        def _():
+            for j in (0, 1):
+                for copy in self.hop(step, j, 0):
+                    copy.start()
+
+
+def ffn_call(normed, grad_low, w_gate, w_up, w_down, collective=None):
     total, width = normed.shape
     hidden = w_gate.shape[1]
     chunk = largest_block(hidden, 512)
+    steps = hidden // chunk
     block_t = largest_block(total, 256)
-    cols = pl.BlockSpec((width, chunk), lambda i: (0, i))
-    rows = pl.BlockSpec((chunk, width), lambda i: (i, 0))
+    fused = collective is not None
+    last = steps - 1
+    cols = pl.BlockSpec((width, chunk), lambda i: (0, jnp.minimum(i, last)))
+    rows = pl.BlockSpec((chunk, width), lambda i: (jnp.minimum(i, last), 0))
+    grads = [jax.ShapeDtypeStruct(w_gate.shape, BF)] * 2
+    scratch = []
+    if fused:
+        share = width // 32
+        grads = [jax.ShapeDtypeStruct((share, hidden), F32)] * 2
+        piece = (share, chunk)
+        scratch = [
+            pltpu.VMEM((2, 2, 4, 2, 2, 2) + piece, BF),
+            pltpu.VMEM((steps, 2, 4, 2, 2) + piece, BF),
+            pltpu.VMEM((steps, 2, 4, 2) + piece, BF),
+            pltpu.VMEM((steps, 2, 4) + piece, BF),
+            pltpu.VMEM((steps, 2, 3) + piece, BF),
+            pltpu.SemaphoreType.DMA((steps, 2, 6)),
+            pltpu.SemaphoreType.DMA((steps, 2, 6)),
+        ]
+    grad_spec = resident(grads[0].shape) if fused else cols
     return pl.pallas_call(
-        functools.partial(ffn_kernel, block_t),
-        grid=(hidden // chunk,),
+        functools.partial(ffn_kernel, block_t, steps),
+        grid=(steps + 4 * fused,),
         in_specs=[resident(normed.shape), resident(normed.shape), cols, cols, rows],
-        out_specs=[resident(normed.shape), resident(normed.shape), cols, cols, rows],
+        out_specs=[resident(normed.shape), resident(normed.shape), rows, grad_spec, grad_spec],
         out_shape=[
             jax.ShapeDtypeStruct((total, width), F32),
             jax.ShapeDtypeStruct((total, width), F32),
-            jax.ShapeDtypeStruct(w_gate.shape, BF),
-            jax.ShapeDtypeStruct(w_gate.shape, BF),
             jax.ShapeDtypeStruct(w_down.shape, BF),
-        ],
+        ] + grads,
         scratch_shapes=[
             pltpu.VMEM((width, total), BF),
-            pltpu.VMEM((total, width), BF),
             pltpu.VMEM((total, chunk), BF),
             pltpu.VMEM((total, chunk), BF),
             pltpu.VMEM((total, chunk), BF),
-        ],
-        compiler_params=params(),
+        ] + scratch,
+        compiler_params=pltpu.CompilerParams(
+            vmem_limit_bytes=60 * 2**20, collective_id=collective, has_side_effects=fused
+        ),
         cost_estimate=pl.CostEstimate(
             flops=18 * total * width * hidden, bytes_accessed=12 * width * hidden, transcendentals=0
         ),
         name="ffn",
-    )(normed, cotangent, w_gate, w_up, w_down)
+    )(normed, grad_low, w_gate, w_up, w_down)
 
 
 def middle_kernel(
@@ -525,9 +646,12 @@
 
 def last_kernel(
     q_width, kv_width, head, scale,
-    dq_ref, dk_ref, dv_ref, raw_ref, gqk_ref, cos_ref, sin_ref, ones_ref, w_ref, x_ref, g_ref, dh_ref,
-    d_ref, in_ref, gain_ref, gq_ref, gk_ref,
+    dq_ref, dk_ref, dv_ref, rawq_ref, rawk_ref, gqk_ref, cos_ref, sin_ref, ones_ref, w_ref, x_ref, g_ref,
+    dh_ref, *refs,
 ):
+    got_ref = refs[0] if len(refs) == 6 else None
+    d_ref, in_ref, gain_ref, gq_ref, gk_ref = refs[-5:]
+
     @pl.when(pl.program_id(0) == 0)
     def _():
         gain_ref[...] = jnp.zeros_like(gain_ref)
@@ -542,11 +666,13 @@
     for c in range(0, qk, wide):
         cols = slice(c, c + wide)
         if c < q_width:
-            grad, total = dq_ref[:, cols] * scale, gq_ref
+            grad, total, raw = dq_ref[:, cols] * scale, gq_ref, rawq_ref[:, cols]
         else:
-            grad, total = dk_ref[:, c - q_width : c - q_width + wide].astype(F32), gk_ref
+            at = slice(c - q_width, c - q_width + wide)
+            grad, total, raw = dk_ref[:, at].astype(F32), gk_ref, rawk_ref[:, at]
+            if got_ref is not None:
+                grad += got_ref[:, at].astype(F32)
         grad = grad * cos + swap_halves(grad * sin, head)
-        raw = raw_ref[:, cols]
         inv = lax.rsqrt(head_sum(raw * raw, ones) * (1.0 / head) + epsilon)
         unit = raw * inv
         gained = jnp.sum(unit * grad, axis=0, keepdims=True)
@@ -554,7 +680,10 @@
         scaled = grad * gqk_ref[:, cols]
         shared = head_sum(unit * scaled, ones) * (1.0 / head)
         d_ref[:, cols] = (inv * (scaled - unit * shared)).astype(BF)
-    d_ref[:, qk:] = dv_ref[...].astype(BF)
+    d_values = dv_ref[...].astype(F32)
+    if got_ref is not None:
+        d_values += got_ref[:, kv_width:].astype(F32)
+    d_ref[:, qk:] = d_values.astype(BF)
     d_normed = mm(d_ref[...], w_ref[...], NT)
     x = x_ref[...].astype(F32)
     inverse = lax.rsqrt(jnp.mean(x * x, axis=-1, keepdims=True) + epsilon)
@@ -565,7 +694,7 @@
     in_ref[...] = dh_ref[...] + inverse * (scaled - unit * shared)
 
 
-def last_call(dq, dk, dv, raw, gqk, cos, sin, ones, w, x, g, d_hidden, head):
+def last_call(dq, dk, dv, raw_q, raw_k, gqk, cos, sin, ones, w, x, g, d_hidden, head, got=()):
     total, width = x.shape
     q_width, kv_width = dq.shape[1], dk.shape[1]
     block = largest_block(total, 256)
@@ -577,10 +706,10 @@
         functools.partial(last_kernel, q_width, kv_width, head, head ** (-0.5)),
         grid=(total // block,),
         in_specs=[
-            rows(q_width), rows(kv_width), rows(kv_width), rows(q_width + kv_width),
+            rows(q_width), rows(kv_width), rows(kv_width), rows(q_width), rows(kv_width),
             resident(gqk.shape), rows(LANES), rows(LANES), resident(ones.shape),
             resident(w.shape), rows(width), resident(g.shape), rows(width),
-        ],
+        ] + [rows(2 * kv_width)] * len(got),
         out_specs=[
             rows(w.shape[1]), rows(width),
             resident((1, width)), resident((1, LANES)), resident((1, LANES)),
@@ -594,7 +723,7 @@
         ],
         compiler_params=params(),
         name="last",
-    )(dq, dk, dv, raw, gqk, cos, sin, ones, w, x, g, d_hidden)
+    )(dq, dk, dv, raw_q, raw_k, gqk, cos, sin, ones, w, x, g, d_hidden, *got)
 
 
 class Place:
@@ -737,7 +866,11 @@
     lax.fori_loop(0, total.shape[0], step, 0)
 
 
-def scatter_kernel(pieces, count, *refs):
+def scatter_kernel(pieces, count, gains, *refs):
+    if gains:
+        gain_ref, gain_out = refs[count], refs[2 * count + 1]
+        sum_scr, got_scr, z_scr, gain_send, gain_recv = refs[-5:]
+        refs = refs[:count] + refs[count + 1 : 2 * count + 1] + refs[2 * count + 2 : -5]
     ins, outs = refs[:count], refs[count : 2 * count]
     n = len(pieces)
     shapes, homes = piece_homes(pieces)
@@ -808,9 +941,44 @@
         for copy in pairs(p):
             copy.start()
 
+    hops = []
+    if gains:
+        near = [me.peer(c=1 - me.c), me.peer(x=1 - me.x), me.peer(y=1 - me.y)]
+        hops = [
+            [remote(sum_scr.at[i], got_scr.at[i], (gain_send, gain_recv), i, peer)]
+            for i, peer in enumerate(near)
+        ] + [[
+            remote(sum_scr.at[3], z_scr.at[me.z], (gain_send, gain_recv), 2 + d, me.peer(z=me.up(d)))
+            for d in (1, 2, 3)
+        ]]
+
+    def gain_step(i):
+        if i == 0:
+            sum_scr[0] = gain_ref[...]
+        else:
+            for copy in hops[i - 1]:
+                copy.wait_recv()
+            if i < 4:
+                sum_scr[i] = sum_scr[i - 1] + got_scr[i - 1]
+        if i == 3:
+            z_scr[me.z] = sum_scr[3]
+        if i < 4:
+            for copy in hops[i]:
+                copy.start()
+        else:
+            gain_out[...] = (z_scr[0] + z_scr[1]) + (z_scr[2] + z_scr[3])
+            for hop in hops:
+                for copy in hop:
+                    copy.wait_send()
+
     for p in range(min(n, AHEAD)):
         begin(p)
-    for t in range(0, n + 3 * pair, pair):
+    rounds = range(0, n + 3 * pair, pair)
+    for t in rounds:
+        if gains:
+            for i in range(5):
+                if i * (len(rounds) - 1) // 4 == t // pair:
+                    gain_step(i)
         for s in range(4):
             for p in range(t - s * pair, t - s * pair + pair):
                 if 0 <= p < n:
@@ -840,7 +1008,7 @@
     return shapes, homes
 
 
-def scatter_call(grads, pieces, collective):
+def scatter_call(grads, pieces, collective, gains=()):
     count = len(grads)
     shards = [(g.shape[0] // 32, g.shape[1]) for g in grads]
     grads = [g.reshape((4, 2, 2, 2) + s) for g, s in zip(grads, shards)]
@@ -856,20 +1024,32 @@
             pltpu.VMEM((OWN, 4, 2, 2) + shape, BF),
         ]
     return pl.pallas_call(
-        functools.partial(scatter_kernel, pieces, count),
-        in_specs=[pl.BlockSpec(memory_space=pl.ANY)] * count,
-        out_specs=[pl.BlockSpec(memory_space=pltpu.VMEM)] * count,
-        out_shape=[jax.ShapeDtypeStruct(s, F32) for s in shards],
+        functools.partial(scatter_kernel, pieces, count, len(gains)),
+        in_specs=[pl.BlockSpec(memory_space=pl.ANY)] * count
+        + [pl.BlockSpec(memory_space=pltpu.VMEM)] * len(gains),
+        out_specs=[pl.BlockSpec(memory_space=pltpu.VMEM)] * (count + len(gains)),
+        out_shape=[jax.ShapeDtypeStruct(s, F32) for s in shards]
+        + [jax.ShapeDtypeStruct(g.shape, F32) for g in gains],
         scratch_shapes=scratch + [
             pltpu.SemaphoreType.DMA((len(pieces), 6)),
             pltpu.SemaphoreType.DMA((len(pieces), 6)),
             pltpu.SemaphoreType.DMA((len(shapes), OWN)),
+        ] + [
+            scratch
+            for g in gains
+            for scratch in (
+                pltpu.VMEM((4,) + g.shape, F32),
+                pltpu.VMEM((3,) + g.shape, F32),
+                pltpu.VMEM((4,) + g.shape, F32),
+                pltpu.SemaphoreType.DMA((6,)),
+                pltpu.SemaphoreType.DMA((6,)),
+            )
         ],
         compiler_params=pltpu.CompilerParams(
             collective_id=collective, has_side_effects=True, vmem_limit_bytes=VMEM_LIMIT
         ),
         name="scatter",
-    )(*grads)
+    )(*grads, *gains)
 
 
 def col_pieces(array, rows, cols, width=512, high=None):
@@ -896,24 +1076,14 @@
     q_heads = q_width // head
     total = seqs * rows
     row_start = lax.axis_index("ctx") * rows
+    own_kernels = (lax.axis_size("dp"), lax.axis_size("ctx")) == (16, 2)
+    share = w_q.shape[0]
 
     def fetch(weight):
         return lax.all_gather(weight, AXES, axis=0, tiled=True)
 
-    w_qkv = jnp.concatenate([w_q, w_k, w_v], axis=1)
-    own_kernels = (lax.axis_size("dp"), lax.axis_size("ctx")) == (16, 2)
-    share = w_q.shape[0]
-    gate_pieces = interleave(
-        [(0,) + p[1:3] + (True,) for p in col_pieces(0, share, w_gate.shape[1])],
-        [(1,) + p[1:3] + (False,) for p in col_pieces(1, share, w_up.shape[1])],
-    )
-    qkv_pieces = col_pieces(0, share, w_qkv.shape[1])
-    o_pieces = col_pieces(1, share, w_o.shape[1])
-    w_down = fetch(w_down)
-    if own_kernels:
-        w_qkv, w_o = gather_call([w_qkv, w_o], qkv_pieces + o_pieces, 0)
-    else:
-        w_qkv, w_o, w_gate, w_up = fetch(w_qkv), fetch(w_o), fetch(w_gate), fetch(w_up)
+    def send(grad):
+        return lax.psum_scatter(grad, AXES, scatter_dimension=0, tiled=True).astype(F32)
 
     seg_rows = lax.dynamic_slice_in_dim(segments, row_start, rows, 1)
     first = jnp.sum((segments[:, None, :] < seg_rows[:, :, None]).astype(jnp.int32), axis=-1)
@@ -927,67 +1097,121 @@
     wide = 2 * LANES
     member = jnp.arange(wide) // head
     ones = (member[:, None] == member[None, :]).astype(BF)
-    gqk = jnp.concatenate([g_q] * q_heads + [g_k] * kv_heads)[None, :]
+    gains_q = jnp.concatenate([g_q] * q_heads)[None, :]
+    gains_k = jnp.concatenate([g_k] * kv_heads)[None, :]
+    x = tokens.reshape(total, width)
+    cotangent = cotangent.reshape(total, width)
+
+    w_qkv = jnp.concatenate([w_q, w_k, w_v], axis=1)
+    w_gate, w_down = fetch(w_gate), fetch(w_down)
+    grad_low = cotangent.astype(BF)
+    if own_kernels:
+        up_pieces = col_pieces(0, share, w_up.shape[1], 256)
+        qkv_pieces = col_pieces(0, share, w_qkv.shape[1])
+        o_pieces = col_pieces(0, share, w_o.shape[1])
+        [w_qkv] = gather_call([w_qkv], qkv_pieces, 0)
+    else:
+        w_qkv, w_o, w_up = fetch(w_qkv), fetch(w_o), fetch(w_up)
+
+    tables = (cos, sin, ones, head)
+    normed, kv, raw_k = project_call(
+        x, w_qkv, (q_width, 2 * kv_width), kv_width, g_attn[None, :], gains_k, *tables, None, "project_kv"
+    )
+    kv = kv.reshape(seqs, rows, 2 * kv_width)
+    if own_kernels:
+        before = lax.ppermute(kv, "ctx", [(0, 1)])
+    _, q, raw_q = project_call(
+        x, w_qkv, (0, q_width), q_width, g_attn[None, :], gains_q, *tables, head ** (-0.5), "project_q"
+    )
+    q = q.reshape(seqs, rows, q_width)
     block_q, block_k = min(128, rows), 128
-    low = first[:, ::block_q] // block_k
-    start = jnp.full((1,), row_start, jnp.int32)
-
-    x = tokens.reshape(total, width)
-    normed, q, kv, raw = qkv_call(
-        x, w_qkv, g_attn[None, :], gqk, cos, sin, ones, q_width, kv_width, head
-    )
-    kv = lax.all_gather(kv.reshape(seqs, rows, 2 * kv_width), "ctx", axis=1, tiled=True)
-    q = q.reshape(seqs, rows, q_width)
-    mixed, totals = attend_call(q, kv, first[:, :, None], low, start, block_q, block_k)
+    at = jnp.arange(0, rows, block_q, dtype=jnp.int32)[None, :]
+    lowest = first[:, ::block_q]
+    zero = jnp.zeros((1,), jnp.int32)
+    if own_kernels:
+        own_first = first - row_start
+        own_keys = (
+            jnp.maximum(lowest - row_start, 0) // block_k,
+            jnp.broadcast_to((at + block_q - 1) // block_k + 1, lowest.shape),
+            zero,
+        )
+        far_first = own_first + rows
+        far_keys = (
+            jnp.clip(lowest - row_start + rows, 0, rows) // block_k,
+            jnp.full(lowest.shape, rows // block_k, jnp.int32),
+            zero + rows,
+        )
+        near = attend_call(q, kv, own_first, own_keys, block_q, block_k, last_part=False)
+        w_o, _ = lax.optimization_barrier((w_o, near))
+        [w_o] = gather_call([w_o], o_pieces, 4)
+        mixed, totals = attend_call(q, before, far_first, far_keys, block_q, block_k, near)
+    else:
+        kv = lax.all_gather(kv, "ctx", axis=1, tiled=True)
+        all_keys = (
+            lowest // block_k,
+            jnp.broadcast_to((row_start + at + block_q - 1) // block_k + 1, lowest.shape),
+            zero + row_start,
+        )
+        mixed, totals = attend_call(q, kv, first, all_keys, block_q, block_k)
     mixed, totals = mixed.reshape(total, q_width), totals.reshape(total, q_width)
     attended, hidden, normed_two = hidden_call(mixed, w_o, x, g_ffn[None, :])
 
-    def send(grad):
-        return lax.psum_scatter(
-            grad.astype(BF), AXES, scatter_dimension=0, tiled=True
-        ).astype(F32)
-
-    cotangent = cotangent.reshape(total, width)
     if own_kernels:
-        normed_two, w_gate, w_up = lax.optimization_barrier((normed_two, w_gate, w_up))
-        w_gate, w_up = gather_call([w_gate, w_up], gate_pieces, 1)
-    ffn, d_normed_two, grad_gate, grad_up, grad_down = ffn_call(
-        normed_two, cotangent, w_gate, w_up, w_down
-    )
-    if own_kernels:
-        out_gate, out_up = scatter_call([grad_gate, grad_up], gate_pieces, 2)
+        normed_two, w_up = lax.optimization_barrier((normed_two, w_up))
+        [w_up] = gather_call([w_up], up_pieces, 1)
+        ffn, d_normed_two, grad_down, out_gate, out_up = ffn_call(
+            normed_two, grad_low, w_gate, w_up, w_down, 2
+        )
     else:
-        out_gate, out_up, out_down = send(grad_gate), send(grad_up), send(grad_down)
+        ffn, d_normed_two, grad_down, out_gate, out_up = ffn_call(
+            normed_two, grad_low, w_gate, w_up, w_down
+        )
+        out_gate, out_up = send(out_gate), send(out_up)
+    out_down = send(grad_down)
     outputs, d_hidden, d_low, d_out, delta, grad_gffn = middle_call(
         ffn, d_normed_two, hidden, cotangent, g_ffn[None, :], w_o, mixed, totals, ones, head
     )
+    d_out, delta = d_out.reshape(q.shape), delta.reshape(q.shape)
+    if own_kernels:
+        far_dq, dk, dv = attend_back_call(
+            q, d_out, delta, before, far_first, far_keys, block_q, block_k
+        )
+        got = lax.ppermute(jnp.concatenate([dk, dv], axis=2), "ctx", [(1, 0)])
+        dq, dk, dv = attend_back_call(
+            q, d_out, delta, kv, own_first, own_keys, block_q, block_k, (far_dq,)
+        )
+        dk, dv, got = dk.reshape(total, kv_width), dv.reshape(total, kv_width), (got.reshape(total, -1),)
+    else:
+        dq, dk, dv = attend_back_call(q, d_out, delta, kv, first, all_keys, block_q, block_k)
+        dkv = lax.psum_scatter(
+            jnp.concatenate([dk, dv], axis=2), "ctx", scatter_dimension=1, tiled=True
+        ).reshape(total, 2 * kv_width)
+        dk, dv, got = dkv[:, :kv_width], dkv[:, kv_width:], ()
     grad_o = mm(attended, d_low, TN).astype(BF)
-    dq, dk, dv = attend_back_call(
-        q, d_out.reshape(q.shape), delta.reshape(q.shape), kv, first[:, None, :], low, start,
-        block_q, block_k,
-    )
-    dkv = lax.psum_scatter(
-        jnp.concatenate([dk, dv], axis=2), "ctx", scatter_dimension=1, tiled=True
-    ).reshape(total, 2 * kv_width)
     d_qkv, input_grad, grad_gattn, grad_gq, grad_gk = last_call(
-        dq.reshape(total, q_width), dkv[:, :kv_width], dkv[:, kv_width:], raw, gqk, cos, sin, ones,
-        w_qkv, x, g_attn[None, :], d_hidden, head,
+        dq.reshape(total, q_width), dk, dv, raw_q, raw_k,
+        jnp.concatenate([gains_q, gains_k], axis=1), cos, sin, ones,
+        w_qkv, x, g_attn[None, :], d_hidden, head, got,
     )
     grad_qkv = mm(normed, d_qkv, TN).astype(BF)
     if own_kernels:
-        down_pieces = [(2,) + p[1:] for p in col_pieces(2, w_down.shape[0] // 32, width, 256, 48)]
-        out_qkv, out_o, out_down = scatter_call(
-            [grad_qkv, grad_o, grad_down], down_pieces + o_pieces + qkv_pieces, 3
-        )
+        flat = jnp.concatenate([grad_gattn, grad_gffn, grad_gq, grad_gk], axis=1).reshape(-1, LANES)
+        flat = jnp.pad(flat, ((0, -flat.shape[0] % 8), (0, 0)))
+        o_pieces = [(1,) + p[1:] for p in o_pieces]
+        out_qkv, out_o, flat = scatter_call([grad_qkv, grad_o], o_pieces + qkv_pieces, 3, (flat,))
+        flat = flat.reshape(1, -1)
+        grad_gattn, grad_gffn = flat[:, :width], flat[:, width : 2 * width]
+        grad_gq = flat[:, 2 * width : 2 * width + LANES]
+        grad_gk = flat[:, 2 * width + LANES : 2 * width + 2 * LANES]
     else:
         out_qkv, out_o = send(grad_qkv), send(grad_o)
+        grad_gattn, grad_gffn, grad_gq, grad_gk = lax.psum(
+            (grad_gattn, grad_gffn, grad_gq, grad_gk), AXES
+        )
 
     def fold(grad):
         return jnp.sum(grad.reshape(LANES // head, head), axis=0)
 
-    gains = lax.psum(
-        (grad_gattn[0], fold(grad_gq), fold(grad_gk), grad_gffn[0]), AXES
-    )
     return (
         outputs.reshape(tokens.shape),
         input_grad.reshape(tokens.shape),
@@ -998,7 +1222,10 @@
         out_gate,
         out_up,
         out_down,
-        *gains,
+        grad_gattn[0],
+        fold(grad_gq),
+        fold(grad_gk),
+        grad_gffn[0],
     )
 
 

time: 830 us -> 611 us (0.74)
  Pallas kernels: 681 us -> 525 us
  waiting for transfers between devices: 54.6 us -> 14.7 us
  blocking collectives: 39.4 us -> 0 us
    pallas_call x5 -> x6, Pallas kernels: 413 us -> 274 us  [the longest x1 153 us: ffn_call(): pl.pallas_call(functools.partial(ffn_kernel, block_t, steps), grid=(steps...]
    all_gather x1 -> x0, waiting for transfers between devices: 53.8 us -> none  [per_device(): lax.all_gather(kv.reshape(seqs, rows, 2 * kv_width), 'ctx', axis=1, tiled...]
    psum x1 -> x0, blocking collectives: 39.4 us -> none  [per_device(): lax.psum((grad_gattn[0], fold(grad_gq), fold(grad_gk), grad_gffn[0]), AXES)]
    pallas_call x2 -> x3, Pallas kernels: 174 us -> 140 us  [gather_call(): pl.pallas_call(functools.partial(gather_kernel, pieces, count), in_specs=...]
    pallas_call x1 -> x2, Pallas kernels: 50.5 us -> 66 us  [attend_back_call(): pl.pallas_call(functools.partial(attend_back_kernel, block_q, block_k, he...]
    ppermute x0 -> x2, waiting for transfers between devices: none -> 13.3 us  [the longest x1 13.3 us: per_device(): got = lax.ppermute(jnp.concatenate([dk, dv], axis=2), 'ctx', [(1, 0)])]
  transfers between devices with their start and end apart: 3 -> 5, of which waited for: 1 -> 1; matrix products, arithmetic and copies ran while one was open for 1% -> 7% of each run, Pallas kernels for 40% -> 61%
where the time goes in v3:
time: 611 us; the launch traced here: 610 us
  Pallas kernels  525 us (86%)
  other arithmetic  18.6 us (3%)
  local copies, waits for them, and re-layouts  17.1 us (3%)
  waiting for transfers between devices  14.7 us (2%)
  matrix products  13.9 us (2%)
  between operations  13.9 us (2%)
  starting transfers between devices  6.63 us (1%)
    pallas_call x1, Pallas kernels, ffn_call(): pl.pallas_call(functools.partial(ffn_kernel, block_t, steps), grid=(steps...  153 us
    pallas_call x3, Pallas kernels, gather_call(): pl.pallas_call(functools.partial(gather_kernel, pieces, count), in_specs=...  140 us
    pallas_call x2, Pallas kernels, attend_back_call(): pl.pallas_call(functools.partial(attend_back_kernel, block_q, block_k, he...  66 us
    pallas_call x1, Pallas kernels, scatter_call(): pl.pallas_call(functools.partial(scatter_kernel, pieces, count, len(gains...  56.8 us
    pallas_call x2, Pallas kernels, attend_call(): pl.pallas_call(functools.partial(attend_kernel, block_q, block_k, heads,...  42.4 us
    pallas_call x2, Pallas kernels, project_call(): pl.pallas_call(functools.partial(project_kernel, rope_width, head, scale)...  21.6 us
    pallas_call x1, Pallas kernels, last_call(): pl.pallas_call(functools.partial(last_kernel, q_width, kv_width, head, he...  18.2 us
    pallas_call x1, Pallas kernels, middle_call(): pl.pallas_call(functools.partial(middle_kernel, head), grid=(total // blo...  17.8 us
  transfers between devices with their start and end apart: 5, of which 1 were waited for; matrix products, arithmetic and copies ran while one was open for 7% of the time, Pallas kernels for 61%

profile of v3, /device:TPU:0, one launch (start us, length us, event | category | flops | bytes accessed | tf_op | source)
XLA Modules:
  0.0 609.8 jit_solution(1549066467152134317)
XLA Ops:
  9.4 1.3 convert_reduce_fusion
  10.7 1.5 pad_maximum_fusion.3.refs_0_
  12.3 42.2 %gather.3 = bf16[4,2,2,2,32,2048]{5,4,3,2,1,0:T(8,128)(2,1)} custom-call(bf16[32,2048]{1,0:T(8,128)(2,1)} %pad_maximum_fusion.3.refs_0_), custom_call_target="tpu_custom_call" | custom-call | tf_op jit(solution)/shard_map/gather/pallas_call | solution.py:843
  55.2 1.9 fusion
  57.1 1.8 pad_maximum_fusion.1
  59.7 9.1 %project_kv.1 = (bf16[1024,1024]{1,0:T(8,128)(2,1)}, bf16[1024,1024]{1,0:T(8,128)(2,1)}, f32[1024,512]{1,0:T(8,128)}) custom-call(bf16[1024,1024]{1,0:T(8,128)(2,1)} %bitcast.46, bf16[1024,2048]{1,0:T(8,128)(2,1)} %bitcast.39, f32[1,1024]{1,0:T(1,128)} %bitcast.72, f32[1,512]{1,0:T(1,128)} %bitcast.68, f32[1024,128]{1,0:T(8,128)} %get-tuple-element.106.cos_ref, ...), custom_call_target="tpu_custom_call" | custom-call | flops 2147483648 | bytes 12582912 | tf_op jit(solution)/shard_map/project_kv/pallas_call | solution.py:102
  68.8 5.2 collective-permute-start
  74.8 1.0 copy.32.first_ref
  75.8 12.5 %project_q.1 = (bf16[1024,1024]{1,0:T(8,128)(2,1)}, bf16[1024,1024]{1,0:T(8,128)(2,1)}, f32[1024,1024]{1,0:T(8,128)}) custom-call(bf16[1024,1024]{1,0:T(8,128)(2,1)} %bitcast.47, bf16[1024,2048]{1,0:T(8,128)(2,1)} %bitcast.40, f32[1,1024]{1,0:T(1,128)} %bitcast.73, f32[1,1024]{1,0:T(1,128)} %bitcast.66, f32[1024,128]{1,0:T(8,128)} %get-tuple-element.106.cos_ref, ...), custom_call_target="tpu_custom_call" | custom-call | flops 2147483648 | bytes 12582912 | tf_op jit(solution)/shard_map/project_q/pallas_call | solution.py:102
  89.5 30.4 %attend.2 = (f32[2,512,1024]{2,1,0:T(8,128)}, f32[2,512,1024]{2,1,0:T(8,128)}) custom-call(s32[2,4]{1,0:T(2,128)} %get-tuple-element.104.low_ref, s32[2,4]{1,0:T(2,128)} %broadcast_in_dim.15.high_ref, s32[1]{0:T(128)} %constant.83.clone.1.start_ref, bf16[2,512,1024]{2,1,0:T(8,128)(2,1)} %bitcast.53, bf16[2,512,1024]{2,1,0:T(8,128)(2,1)} %bitcast.82, ...), custom_call_target="tpu_custom_call" | custom-call | flops 2147483648 | bytes 16777216 | tf_op jit(solution)/shard_map/attend/pallas_call | solution.py:201
  119.9 25.8 %gather.4 = bf16[4,2,2,2,32,1024]{5,4,3,2,1,0:T(8,128)(2,1)} custom-call(bf16[32,1024]{1,0:T(8,128)(2,1)} %refs_0_), custom_call_target="tpu_custom_call" | custom-call | tf_op jit(solution)/shard_map/gather/pallas_call | solution.py:843
  146.7 3.9 bitcast_convert_fusion.c_ref
  151.9 12.0 %attend.3 = (f32[2,512,1024]{2,1,0:T(8,128)}, f32[2,512,1024]{2,1,0:T(8,128)}) custom-call(s32[2,4]{1,0:T(2,128)} %get-tuple-element.105.low_ref, s32[2,4]{1,0:T(2,128)} %broadcast_14_high_ref.2.high_ref, s32[1]{0:T(128)} %constant.76.clone.1.start_ref, bf16[2,512,1024]{2,1,0:T(8,128)(2,1)} %bitcast.54, bf16[2,512,1024]{2,1,0:T(8,128)(2,1)} %copy-done, ...), custom_call_target="tpu_custom_call" | custom-call | flops 2147483648 | bytes 16777216 | tf_op jit(solution)/shard_map/attend/pallas_call | solution.py:201
  164.0 8.4 %hidden.1 = (bf16[1024,1024]{1,0:T(8,128)(2,1)}, f32[1024,1024]{1,0:T(8,128)}, bf16[1024,1024]{1,0:T(8,128)(2,1)}) custom-call(f32[1024,1024]{1,0:T(8,128)} %bitcast.43, bf16[1024,1024]{1,0:T(8,128)(2,1)} %bitcast.37, bf16[1024,1024]{1,0:T(8,128)(2,1)} %bitcast.48, f32[1,1024]{1,0:T(1,128)} %bitcast.63), custom_call_target="tpu_custom_call" | custom-call | tf_op jit(solution)/shard_map/hidden/pallas_call | solution.py:379
  172.4 72.3 %gather.5 = bf16[4,2,2,2,32,4608]{5,4,3,2,1,0:T(8,128)(2,1)} custom-call(bf16[32,4608]{1,0:T(8,128)(2,1)} %refs_0_.1), custom_call_target="tpu_custom_call" | custom-call | tf_op jit(solution)/shard_map/gather/pallas_call | solution.py:843
  244.8 153.4 %ffn.1 = (f32[1024,1024]{1,0:T(8,128)}, f32[1024,1024]{1,0:T(8,128)}, bf16[4608,1024]{1,0:T(8,128)(2,1)}, f32[32,4608]{1,0:T(8,128)}, f32[32,4608]{1,0:T(8,128)}) custom-call(bf16[1024,1024]{1,0:T(8,128)(2,1)} %get-tuple-element.60.n_ref, bf16[1024,1024]{1,0:T(8,128)(2,1)} %bitcast_convert_fusion.c_ref, ...), custom_call_target="tpu_custom_call" | custom-call | flops 86973087744 | bytes 56623104 | tf_op jit(solution)/shard_map/ffn/pallas_call | solution.py:559
  398.8 17.8 %middle.1 = (bf16[1024,1024]{1,0:T(8,128)(2,1)}, f32[1024,1024]{1,0:T(8,128)}, bf16[1024,1024]{1,0:T(8,128)(2,1)}, bf16[1024,1024]{1,0:T(8,128)(2,1)}, f32[1024,1024]{1,0:T(8,128)}, /*index=5*/f32[1,1024]{1,0:T(1,128)}) custom-call(f32[1024,1024]{1,0:T(8,128)} %get-tuple-element.62.f_ref, f32[1024,1024]{1,0:T(8,128)} %get-tuple-element.63.dn_ref, ...), custom_call_target="tpu_custom_call" | custom-call | tf_op jit(solution)/shard_map/middle/pallas_call | solution.py:624
  416.6 13.1 %attend_back.2 = (f32[2,512,1024]{2,1,0:T(8,128)}, bf16[2,512,512]{2,1,0:T(8,128)(2,1)}, bf16[2,512,512]{2,1,0:T(8,128)(2,1)}) custom-call(s32[2,4]{1,0:T(2,128)} %get-tuple-element.105.low_ref, s32[2,4]{1,0:T(2,128)} %broadcast_14_high_ref.2.high_ref, s32[1]{0:T(128)} %constant.76.clone.1.start_ref, bf16[2,512,1024]{2,1,0:T(8,128)(2,1)} %bitcast.55, ...), custom_call_target="tpu_custom_call" | custom-call | flops 5368709120 | bytes 16777216 | tf_op jit(solution)/shard_map/attend_back/pallas_call | solution.py:330
  429.7 1.9 pad_maximum_fusion
  431.7 1.3 collective-permute-start.1
  434.2 52.9 %attend_back.3 = (f32[2,512,1024]{2,1,0:T(8,128)}, bf16[2,512,512]{2,1,0:T(8,128)(2,1)}, bf16[2,512,512]{2,1,0:T(8,128)(2,1)}) custom-call(s32[2,4]{1,0:T(2,128)} %get-tuple-element.104.low_ref, s32[2,4]{1,0:T(2,128)} %broadcast_in_dim.15.high_ref, s32[1]{0:T(128)} %constant.83.clone.1.start_ref, bf16[2,512,1024]{2,1,0:T(8,128)(2,1)} %bitcast.56, ...), custom_call_target="tpu_custom_call" | custom-call | flops 5368709120 | bytes 16777216 | tf_op jit(solution)/shard_map/attend_back/pallas_call | solution.py:330
  487.0 5.4 convolution_convert_fusion.1
  492.4 13.3 %collective-permute-done.1 = bf16[2,512,1024]{2,1,0:T(8,128)(2,1)S(1)} collective-permute-done((bf16[2,512,1024]{2,1,0:T(8,128)(2,1)S(1)}, bf16[2,512,1024]{2,1,0:T(8,128)(2,1)S(1)}, u32[]{:S(2)}, u32[]{:S(2)}) %collective-permute-start.1) | collective-permute-done | bytes 2097184 | tf_op jit(solution)/shard_map/ppermute | solution.py:1179
  505.7 1.3 copy-done.1
  507.0 18.2 %last.1 = (bf16[1024,2048]{1,0:T(8,128)(2,1)}, f32[1024,1024]{1,0:T(8,128)}, f32[1,1024]{1,0:T(1,128)}, f32[1,128]{1,0:T(1,128)}, f32[1,128]{1,0:T(1,128)}) custom-call(f32[1024,1024]{1,0:T(8,128)} %bitcast.50, bf16[1024,512]{1,0:T(8,128)(2,1)} %bitcast.59, bf16[1024,512]{1,0:T(8,128)(2,1)} %bitcast.60, f32[1024,1024]{1,0:T(8,128)} %get-tuple-element.73.rawq_ref, ...), custom_call_target="tpu_custom_call" | custom-call | tf_op jit(solution)/shard_map/last/pallas_call | solution.py:705
  526.6 8.5 %convolution_convert_fusion = bf16[1024,2048]{1,0:T(8,128)(2,1)} fusion(bf16[1024,1024]{1,0:T(8,128)(2,1)S(1)} %copy-done.10, bf16[1024,2048]{1,0:T(8,128)(2,1)} %get-tuple-element.80), kind=kOutput, calls=%fused_computation.1 | convolution fusion | flops 4297064448 | bytes 10485760 | tf_op jit(solution)/shard_map/dot_general | solution.py:25
  535.1 56.8 %scatter.1 = (f32[32,2048]{1,0:T(8,128)}, f32[32,1024]{1,0:T(8,128)}, f32[24,128]{1,0:T(8,128)}) custom-call(bf16[4,2,2,2,32,2048]{5,4,3,2,1,0:T(8,128)(2,1)} %bitcast.51, bf16[4,2,2,2,32,1024]{5,4,3,2,1,0:T(8,128)(2,1)} %bitcast.58, f32[24,128]{1,0:T(8,128)} %pad.4.refs_2_), custom_call_target="tpu_custom_call" | custom-call | tf_op jit(solution)/shard_map/scatter/pallas_call | solution.py:1026
  591.9 1.6 slice.25
  595.4 1.3 fusion.3
  596.7 1.5 fusion.2
  598.2 1.8 convert_element_type.43
  600.0 1.6 copy.38
  (59 shorter events, 14.7 us)
Async XLA Ops:
  7.2 47.3 %copy-start.5 = (f32[64]{0:T(128)S(1)}, f32[64]{0:T(128)}, u32[]{:S(2)}) copy-start(f32[64]{0:T(128)} %param.26) | copy-start | bytes 772
  7.2 237.5 %all-gather.3.cloned.1.call-start = ((), (), s32[]{:S(2)}) async-start(), calls=%async_computation.1 | async-start | bytes 9732096 | tf_op jit(solution)/shard_map/all_gather | solution.py:1083
  7.9 236.8 %all-gather.5.cloned.1.call-start = ((), (), s32[]{:S(2)}) async-start(), calls=%async_computation.2 | async-start | bytes 9732096 | tf_op jit(solution)/shard_map/all_gather | solution.py:1083
  8.7 589.5 %reduce-scatter.2.cloned.1.call-start = ((), (), s32[]{:S(2)}) async-start(), calls=%async_computation.3 | async-start | bytes 9732096 | tf_op jit(solution)/shard_map/reduce_scatter | solution.py:1086
  58.9 15.2 %copy-start.4 = (f32[64]{0:T(128)S(1)}, f32[64]{0:T(128)}, u32[]{:S(2)}) copy-start(f32[64]{0:T(128)} %param.25) | copy-start | bytes 772
  68.8 81.8 %collective-permute-start = (bf16[2,512,1024]{2,1,0:T(8,128)(2,1)}, bf16[2,512,1024]{2,1,0:T(8,128)(2,1)S(1)}, u32[]{:S(2)}, u32[]{:S(2)}) collective-permute-start(bf16[2,512,1024]{2,1,0:T(8,128)(2,1)} %bitcast.81), channel_id=1, source_target_pairs={{0,1},{2,3},{4,5},{6,7},{8,9},{10,11},{12,13},{14,15},{16,17},{18,... | collective-permute-start | bytes 6291464 | tf_op jit(solution)/shard_map/ppermute | solution.py:1122
  150.6 1.3 copy-start
  429.7 3.9 copy-start.6
  429.7 3.9 copy-start.7
  431.7 74.0 %collective-permute-start.1 = (bf16[2,512,1024]{2,1,0:T(8,128)(2,1)S(1)}, bf16[2,512,1024]{2,1,0:T(8,128)(2,1)S(1)}, u32[]{:S(2)}, u32[]{:S(2)}) collective-permute-start(bf16[2,512,1024]{2,1,0:T(8,128)(2,1)S(1)} %pad_maximum_fusion), channel_id=1, source_target_pairs={{1,0},{3,2},{5,4},{7,6},{9,8},{11,10},{13,12},{15,14},{17,16},{19,... | collective-permute-start | bytes 6291464 | tf_op jit(solution)/shard_map/ppermute | solution.py:1179
  434.2 52.9 %copy-start.9 = (bf16[1024,1024]{1,0:T(8,128)(2,1)S(1)}, bf16[1024,1024]{1,0:T(8,128)(2,1)}, u32[]{:S(2)}) copy-start(bf16[1024,1024]{1,0:T(8,128)(2,1)} %get-tuple-element.81) | copy-start | bytes 6291460
  505.7 1.3 copy-start.1
  507.0 18.2 %copy-start.8 = (f32[1,1024]{1,0:T(1,128)S(1)}, f32[1,1024]{1,0:T(1,128)}, u32[]{:S(2)}) copy-start(f32[1,1024]{1,0:T(1,128)} %get-tuple-element.84) | copy-start | bytes 12292
  507.0 19.6 %copy-start.10 = (bf16[1024,1024]{1,0:T(8,128)(2,1)S(1)}, bf16[1024,1024]{1,0:T(8,128)(2,1)}, u32[]{:S(2)}) copy-start(bf16[1024,1024]{1,0:T(8,128)(2,1)} %get-tuple-element.79) | copy-start | bytes 6291460
  535.1 66.5 %copy-start.3 = (f32[32,4608]{1,0:T(8,128)S(1)}, f32[32,4608]{1,0:T(8,128)}, u32[]{:S(2)}) copy-start(f32[32,4608]{1,0:T(8,128)} %get-tuple-element.127) | copy-start | bytes 1769476
  535.1 67.3 %copy-start.2 = (f32[32,4608]{1,0:T(8,128)S(1)}, f32[32,4608]{1,0:T(8,128)}, u32[]{:S(2)}) copy-start(f32[32,4608]{1,0:T(8,128)} %get-tuple-element.128) | copy-start | bytes 1769476
Sparse Core Ops, SparseCore 0:
  10.9 89.3 all-gather.2
  103.3 106.6 all-gather.4
  398.3 142.5 reduce-scatter.1

commit v4 on v3

--- a/solution.py
+++ b/solution.py
@@ -194,7 +194,7 @@
     seqs, rows, q_width = q.shape
     length = kv.shape[1]
     kv_heads = q_width // LANES
-    heads = largest_block(kv_heads, 4)
+    heads = largest_block(kv_heads, 8)
     steps = kv_heads // heads
     half = LANES // 2
     spec_q = pl.BlockSpec((1, rows, heads * LANES), lambda s, p, *_: (s, 0, p))
@@ -322,7 +322,7 @@
     length = kv.shape[1]
     kv_width = kv.shape[2] // 2
     kv_heads = q_width // LANES
-    heads = largest_block(kv_heads, 4)
+    heads = largest_block(kv_heads, 8)
     steps = kv_heads // heads
     half = LANES // 2
     spec_q = pl.BlockSpec((1, rows, heads * LANES), lambda s, p, *_: (s, 0, p))
@@ -391,31 +391,15 @@
     )(mixed, w_o, x, g)
 
 
-def ffn_kernel(
-    block_t, steps,
-    n_ref, c_ref, wg_ref, wu_ref, wd_ref,
-    out_ref, dn_ref, gd_ref, gg_ref, gu_ref,
-    n_scr, act_scr, dg_scr, du_scr, *refs,
-):
-    total, width = n_ref.shape
-    chunk = wg_ref.shape[1]
-    step = pl.program_id(0)
-    sums = GradSums(gg_ref, gu_ref, refs) if refs else None
-
-    @pl.when(step == 0)
-    def _():
-        if sums:
-            sums.hello()
-        n_scr[...] = n_ref[...].T
-        out_ref[...] = jnp.zeros_like(out_ref)
-        dn_ref[...] = jnp.zeros_like(dn_ref)
+def ffn_block(block_t, n_ref, c_ref, wg, wu, wd, out_ref, dn_ref, act_scr, dg_scr, du_scr):
+    total = n_ref.shape[0]
 
     def t_step(i, carry):
         at = pl.ds(pl.multiple_of(i * block_t, block_t), block_t)
         normed = n_ref[at, :]
-        gate = mm(normed, wg_ref[...])
-        up = mm(normed, wu_ref[...])
-        d_act = mm(c_ref[at, :], wd_ref[...], NT)
+        gate = mm(normed, wg())
+        up = mm(normed, wu())
+        d_act = mm(c_ref[at, :], wd(), NT)
         sig = 1.0 / (1.0 + jnp.exp(-gate))
         silu = gate * sig
         act = (silu * up).astype(BF)
@@ -424,50 +408,183 @@
         act_scr[at, :] = act
         dg_scr[at, :] = d_gate
         du_scr[at, :] = d_up
-        out_ref[at, :] += mm(act, wd_ref[...])
-        dn_ref[at, :] += mm(d_gate, wg_ref[...], NT) + mm(d_up, wu_ref[...], NT)
+        out_ref[at, :] += mm(act, wd())
+        dn_ref[at, :] += mm(d_gate, wg(), NT) + mm(d_up, wu(), NT)
         return carry
+
+    lax.fori_loop(0, total // block_t, t_step, 0, unroll=total // block_t)
+
+
+def down_grad(gd_ref, act_scr, c_ref):
+    for c in range(0, act_scr.shape[1], 256):
+        gd_ref[c : c + 256, :] = mm(act_scr[:, c : c + 256], c_ref[...], TN).astype(BF)
+
+
+def ffn_kernel(
+    block_t,
+    n_ref, c_ref, wg_ref, wu_ref, wd_ref,
+    out_ref, dn_ref, gd_ref, gg_ref, gu_ref,
+    n_scr, act_scr, dg_scr, du_scr,
+):
+    @pl.when(pl.program_id(0) == 0)
+    def _():
+        n_scr[...] = n_ref[...].T
+        out_ref[...] = jnp.zeros_like(out_ref)
+        dn_ref[...] = jnp.zeros_like(dn_ref)
+
+    ffn_block(
+        block_t, n_ref, c_ref, lambda: wg_ref[...], lambda: wu_ref[...], lambda: wd_ref[...],
+        out_ref, dn_ref, act_scr, dg_scr, du_scr,
+    )
 
     def d_step(i, carry):
         at = pl.ds(pl.multiple_of(i * 256, 256), 256)
         normed = n_scr[at, :]
-        gate = mm(normed, dg_scr[...]).astype(BF)
-        up = mm(normed, du_scr[...]).astype(BF)
-        if sums:
-            sums.keep(step, i, gate, up)
+        gg_ref[at, :] = mm(normed, dg_scr[...]).astype(BF)
+        gu_ref[at, :] = mm(normed, du_scr[...]).astype(BF)
+        return carry
+
+    width = n_ref.shape[1]
+    lax.fori_loop(0, width // 256, d_step, 0, unroll=width // 256)
+    down_grad(gd_ref, act_scr, c_ref)
+
+
+def ffn_call(normed, grad_low, w_gate, w_up, w_down):
+    total, width = normed.shape
+    hidden = w_gate.shape[1]
+    chunk = largest_block(hidden, 512)
+    block_t = largest_block(total, 256)
+    cols = pl.BlockSpec((width, chunk), lambda i: (0, i))
+    rows = pl.BlockSpec((chunk, width), lambda i: (i, 0))
+    return pl.pallas_call(
+        functools.partial(ffn_kernel, block_t),
+        grid=(hidden // chunk,),
+        in_specs=[resident(normed.shape), resident(normed.shape), cols, cols, rows],
+        out_specs=[resident(normed.shape), resident(normed.shape), rows, cols, cols],
+        out_shape=[
+            jax.ShapeDtypeStruct((total, width), F32),
+            jax.ShapeDtypeStruct((total, width), F32),
+            jax.ShapeDtypeStruct(w_down.shape, BF),
+            jax.ShapeDtypeStruct(w_gate.shape, BF),
+            jax.ShapeDtypeStruct(w_gate.shape, BF),
+        ],
+        scratch_shapes=[
+            pltpu.VMEM((width, total), BF),
+            pltpu.VMEM((total, chunk), BF),
+            pltpu.VMEM((total, chunk), BF),
+            pltpu.VMEM((total, chunk), BF),
+        ],
+        compiler_params=params(),
+        name="ffn",
+    )(normed, grad_low, w_gate, w_up, w_down)
+
+
+class ColumnGather:
+    def __init__(self, me, own, whole, slots, send, recv, keep_sems, load_sems):
+        self.me, self.own, self.whole, self.slots = me, own, whole, slots
+        self.sems, self.keep_sems, self.load_sems = (send, recv), keep_sems, load_sems
+
+    def cols(self, k):
+        width = self.slots.shape[-1]
+        start = k * width
+        return pl.ds(start if isinstance(k, int) else pl.multiple_of(start, width), width)
+
+    def keep(self, j):
+        me = self.me
+        return pltpu.make_async_copy(
+            self.own[j], self.whole[j].at[me.z, me.y, me.c, me.x], self.keep_sems.at[j]
+        )
+
+    def hop(self, k, j, s):
+        me, every = self.me, slice(None)
+        whole = self.whole[j]
+
+        def mine(z, y, c, x):
+            return whole.at[z, y, c, x, every, self.cols(k)]
+
+        if s == 0:
+            give = self.own[j].at[:, self.cols(k)]
+            return [
+                remote(give, mine(me.z, me.y, me.c, me.x), self.sems, (k, j, d - 1), me.peer(z=me.up(d)))
+                for d in (1, 2, 3)
+            ]
+        to_x, to_y = me.peer(x=1 - me.x), me.peer(y=1 - me.y)
+        if s == 1:
+            give, peer = mine(every, me.y, me.c, me.x), (to_x if j == 0 else to_y)
+        elif s == 2 and j == 0:
+            give, peer = mine(every, me.y, me.c, every), to_y
+        elif s == 2:
+            give, peer = mine(every, every, me.c, me.x), to_x
         else:
-            gg_ref[at, :] = gate
-            gu_ref[at, :] = up
-        return carry
-
-    @pl.when(step < steps)
-    def _():
-        lax.fori_loop(0, total // block_t, t_step, 0)
-        lax.fori_loop(0, width // 256, d_step, 0)
-        for c in range(0, chunk, 256):
-            gd_ref[c : c + 256, :] = mm(act_scr[:, c : c + 256], c_ref[...], TN).astype(BF)
-
-    if sums:
-        sums.advance(step, steps)
+            give, peer = mine(every, every, me.c, every), me.peer(c=1 - me.c)
+        return [remote(give, give, self.sems, (k, j, 2 + s), peer)]
+
+    def load(self, k, j):
+        every = slice(None)
+        slot = k % 2 if isinstance(k, int) else lax.rem(k, 2)
+        return pltpu.make_async_copy(
+            self.whole[j].at[every, every, every, every, every, self.cols(k)],
+            self.slots.at[slot, j], self.load_sems.at[slot, j],
+        )
+
+    def start(self, k, s):
+        for j in (0, 1):
+            for copy in self.hop(k, j, s):
+                copy.start()
+
+    def wait(self, k, s):
+        for j in (0, 1):
+            for copy in self.hop(k, j, s):
+                copy.wait()
+
+    def open(self):
+        for j in (0, 1):
+            self.keep(j).start()
+        for k in range(3):
+            self.start(k, 0)
+        for j in (0, 1):
+            self.keep(j).wait()
+        for k, s in ((0, 1), (1, 1), (0, 2), (2, 1), (1, 2), (0, 3), (3, 1), (2, 2), (1, 3), (4, 1), (3, 2), (5, 1)):
+            self.wait(k, s - 1)
+            self.start(k, s)
+            if s == 1:
+                self.start(k + 3, 0)
+        self.fetch(0)
+
+    def fetch(self, k):
+        self.wait(k, 3)
+        for j in (0, 1):
+            self.load(k, j).start()
+
+    def ready(self, k):
+        for j in (0, 1):
+            self.load(k, j).wait()
+
+    def advance(self, step, steps):
+        for s, early in ((1, 6), (2, 4), (3, 2)):
+            k = step + early
+
+            @pl.when(k < steps)
+            def _(k=k, s=s):
+                self.wait(k, s - 1)
+                self.start(k, s)
+
+        @pl.when(step + 9 < steps)
+        def _():
+            self.start(step + 9, 0)
+
+        @pl.when(step + 1 < steps)
+        def _():
+            self.fetch(step + 1)
 
 
 class GradSums:
-    def __init__(self, gg_ref, gu_ref, refs):
-        self.outs = (gg_ref, gu_ref)
-        self.made, self.r0, self.r1, self.r2, self.r3, self.send, self.recv = refs
-        self.me = Place()
-
-    def hello(self):
-        barrier = pltpu.get_barrier_semaphore()
-        for peer in self.me.peers():
-            pl.semaphore_signal(
-                barrier, inc=1, device_id=peer, device_id_type=pl.DeviceIdType.MESH
-            )
-
-    def keep(self, step, i, gate, up):
-        shape = self.made.shape[3:]
-        self.made[lax.rem(step, 2), 0, i] = gate.reshape(shape)
-        self.made[lax.rem(step, 2), 1, i] = up.reshape(shape)
+    def __init__(self, me, outs, made, r0, r1, r2, r3, send, recv):
+        self.me, self.outs, self.made = me, outs, made
+        self.r0, self.r1, self.r2, self.r3, self.send, self.recv = r0, r1, r2, r3, send, recv
+
+    def keep(self, step, i, j, grad):
+        self.made[lax.rem(step, 2), j, i] = grad.astype(BF).reshape(self.made.shape[3:])
 
     def hop(self, k, j, s):
         me, every = self.me, slice(None)
@@ -508,12 +625,8 @@
             )
 
     def advance(self, step, steps):
-        @pl.when(step == 0)
-        def _():
-            pl.semaphore_wait(pltpu.get_barrier_semaphore(), len(self.me.peers()))
-
-        for s in (3, 2, 1, 0):
-            k = step - 1 - s
+        for s, late in ((3, 6), (2, 5), (1, 3), (0, 1)):
+            k = step - late
 
             @pl.when((k >= 0) & (k < steps))
             def _(s=s, k=k):
@@ -523,78 +636,149 @@
                         for copy in self.hop(k, j, s + 1):
                             copy.start()
 
-        @pl.when(step < steps)
-        def _():
-            for j in (0, 1):
-                for copy in self.hop(step, j, 0):
-                    copy.start()
-
-
-def ffn_call(normed, grad_low, w_gate, w_up, w_down, collective=None):
+
+def feed_kernel(
+    block_t, steps, block_m, head,
+    n_ref, c_ref, wd_ref, own_gate, own_up, h_ref, cot_ref, g_ref, w_ref, o_ref, l_ref, ones_ref,
+    gd_ref, gg_ref, gu_ref, all_gate, all_up, out_ref, dh_ref, low_ref, do_ref, de_ref, gain_ref,
+    n_scr, act_scr, dg_scr, du_scr, f_scr, dn_scr, slots, made, r0, r1, r2, r3,
+    g_send, g_recv, s_send, s_recv, keep_sems, load_sems,
+):
+    step = pl.program_id(0)
+    me = Place()
+    gather = ColumnGather(
+        me, (own_gate, own_up), (all_gate, all_up), slots, g_send, g_recv, keep_sems, load_sems
+    )
+    sums = GradSums(me, (gg_ref, gu_ref), made, r0, r1, r2, r3, s_send, s_recv)
+
+    @pl.when(step == 0)
+    def _():
+        greet(me)
+        n_scr[...] = n_ref[...].T
+        f_scr[...] = jnp.zeros_like(f_scr)
+        dn_scr[...] = jnp.zeros_like(dn_scr)
+        gather.open()
+
+    @pl.when(step < steps)
+    def _():
+        gather.ready(step)
+        slot = lax.rem(step, 2)
+        width, chunk = n_ref.shape[1], wd_ref.shape[0]
+        ffn_block(
+            block_t, n_ref, c_ref,
+            lambda: slots[slot, 0].reshape(width, chunk),
+            lambda: slots[slot, 1].reshape(width, chunk),
+            lambda: wd_ref[...],
+            f_scr, dn_scr, act_scr, dg_scr, du_scr,
+        )
+        for i in range(width // 256):
+            normed = n_scr[256 * i : 256 * i + 256, :]
+            sums.keep(step, i, 0, mm(normed, dg_scr[...]))
+            sums.keep(step, i, 1, mm(normed, du_scr[...]))
+        down_grad(gd_ref, act_scr, c_ref)
+
+    gather.advance(step, steps)
+    sums.advance(step, steps)
+
+    @pl.when(step < steps)
+    def _():
+        for j in (0, 1):
+            for copy in sums.hop(step, j, 0):
+                copy.start()
+
+    @pl.when(step == steps)
+    def _():
+        gain_ref[...] = jnp.zeros_like(gain_ref)
+
+    @pl.when(step >= steps)
+    def _():
+        at = pl.ds(pl.multiple_of((step - steps) * block_m, block_m), block_m)
+        middle_block(
+            head, f_scr[at, :], dn_scr[at, :], h_ref, cot_ref, g_ref, w_ref, o_ref, l_ref, ones_ref,
+            out_ref, dh_ref, low_ref, do_ref, de_ref, gain_ref,
+        )
+
+
+def feed_call(
+    normed, grad_low, w_down, own_gate, own_up, hidden, cotangent, g, w_o, mixed, totals, ones, head,
+    collective,
+):
     total, width = normed.shape
-    hidden = w_gate.shape[1]
-    chunk = largest_block(hidden, 512)
-    steps = hidden // chunk
-    block_t = largest_block(total, 256)
-    fused = collective is not None
+    share, units = own_gate.shape
+    q_width = mixed.shape[1]
+    chunk = largest_block(units, 512)
+    steps = units // chunk
+    block_t, block_m = largest_block(total, 256), largest_block(total, 128)
     last = steps - 1
-    cols = pl.BlockSpec((width, chunk), lambda i: (0, jnp.minimum(i, last)))
+    piece = (share, chunk)
+
+    def after(n):
+        return pl.BlockSpec((block_m, n), lambda i: (jnp.maximum(i - steps, 0), 0))
+
+    anywhere = pl.BlockSpec(memory_space=pl.ANY)
     rows = pl.BlockSpec((chunk, width), lambda i: (jnp.minimum(i, last), 0))
-    grads = [jax.ShapeDtypeStruct(w_gate.shape, BF)] * 2
-    scratch = []
-    if fused:
-        share = width // 32
-        grads = [jax.ShapeDtypeStruct((share, hidden), F32)] * 2
-        piece = (share, chunk)
-        scratch = [
+    whole = jax.ShapeDtypeStruct((4, 2, 2, 2, share, units), BF)
+    outs = pl.pallas_call(
+        functools.partial(feed_kernel, block_t, steps, block_m, head),
+        grid=(steps + total // block_m,),
+        in_specs=[
+            resident(normed.shape), resident(normed.shape), rows, anywhere, anywhere,
+            after(width), after(width), resident(g.shape), resident(w_o.shape), after(q_width),
+            after(q_width), resident(ones.shape),
+        ],
+        out_specs=[
+            rows, resident((share, units)), resident((share, units)), anywhere, anywhere,
+            after(width), after(width), after(width), after(q_width), after(q_width),
+            resident((1, width)),
+        ],
+        out_shape=[
+            jax.ShapeDtypeStruct(w_down.shape, BF),
+            jax.ShapeDtypeStruct((share, units), F32),
+            jax.ShapeDtypeStruct((share, units), F32),
+            whole, whole,
+            jax.ShapeDtypeStruct((total, width), BF),
+            jax.ShapeDtypeStruct((total, width), F32),
+            jax.ShapeDtypeStruct((total, width), BF),
+            jax.ShapeDtypeStruct((total, q_width), BF),
+            jax.ShapeDtypeStruct((total, q_width), F32),
+            jax.ShapeDtypeStruct((1, width), F32),
+        ],
+        scratch_shapes=[
+            pltpu.VMEM((width, total), BF),
+            pltpu.VMEM((total, chunk), BF),
+            pltpu.VMEM((total, chunk), BF),
+            pltpu.VMEM((total, chunk), BF),
+            pltpu.VMEM((total, width), F32),
+            pltpu.VMEM((total, width), F32),
+            pltpu.VMEM((2, 2, 4, 2, 2, 2) + piece, BF),
             pltpu.VMEM((2, 2, 4, 2, 2, 2) + piece, BF),
             pltpu.VMEM((steps, 2, 4, 2, 2) + piece, BF),
             pltpu.VMEM((steps, 2, 4, 2) + piece, BF),
             pltpu.VMEM((steps, 2, 4) + piece, BF),
             pltpu.VMEM((steps, 2, 3) + piece, BF),
-            pltpu.SemaphoreType.DMA((steps, 2, 6)),
-            pltpu.SemaphoreType.DMA((steps, 2, 6)),
         ]
-    grad_spec = resident(grads[0].shape) if fused else cols
-    return pl.pallas_call(
-        functools.partial(ffn_kernel, block_t, steps),
-        grid=(steps + 4 * fused,),
-        in_specs=[resident(normed.shape), resident(normed.shape), cols, cols, rows],
-        out_specs=[resident(normed.shape), resident(normed.shape), rows, grad_spec, grad_spec],
-        out_shape=[
-            jax.ShapeDtypeStruct((total, width), F32),
-            jax.ShapeDtypeStruct((total, width), F32),
-            jax.ShapeDtypeStruct(w_down.shape, BF),
-        ] + grads,
-        scratch_shapes=[
-            pltpu.VMEM((width, total), BF),
-            pltpu.VMEM((total, chunk), BF),
-            pltpu.VMEM((total, chunk), BF),
-            pltpu.VMEM((total, chunk), BF),
-        ] + scratch,
+        + [pltpu.SemaphoreType.DMA((steps, 2, 6))] * 4
+        + [pltpu.SemaphoreType.DMA((2,)), pltpu.SemaphoreType.DMA((2, 2))],
         compiler_params=pltpu.CompilerParams(
-            vmem_limit_bytes=60 * 2**20, collective_id=collective, has_side_effects=fused
+            vmem_limit_bytes=62 * 2**20, collective_id=collective, has_side_effects=True
         ),
         cost_estimate=pl.CostEstimate(
-            flops=18 * total * width * hidden, bytes_accessed=12 * width * hidden, transcendentals=0
+            flops=18 * total * width * units, bytes_accessed=12 * width * units, transcendentals=0
         ),
-        name="ffn",
-    )(normed, grad_low, w_gate, w_up, w_down)
-
-
-def middle_kernel(
-    head,
-    f_ref, dn_ref, h_ref, c_ref, g_ref, w_ref, o_ref, l_ref, ones_ref,
+        name="feed",
+    )(
+        normed, grad_low, w_down, own_gate, own_up, hidden, cotangent, g, w_o, mixed, totals, ones
+    )
+    return outs[:3] + outs[5:]
+
+
+def middle_block(
+    head, ffn, incoming, h_ref, c_ref, g_ref, w_ref, o_ref, l_ref, ones_ref,
     out_ref, dh_ref, low_ref, do_ref, de_ref, gain_ref,
 ):
-    @pl.when(pl.program_id(0) == 0)
-    def _():
-        gain_ref[...] = jnp.zeros_like(gain_ref)
-
     hidden = h_ref[...]
-    out_ref[...] = (hidden + f_ref[...]).astype(BF)
+    out_ref[...] = (hidden + ffn).astype(BF)
     inverse = lax.rsqrt(jnp.mean(hidden * hidden, axis=-1, keepdims=True) + epsilon)
-    incoming = dn_ref[...]
     unit = hidden * inverse
     gain_ref[...] += jnp.sum(unit * incoming, axis=0, keepdims=True)
     scaled = incoming * g_ref[...]
@@ -611,6 +795,16 @@
         ratio = 1.0 / l_ref[:, cols]
         do_ref[:, cols] = (d_att * ratio).astype(BF)
         de_ref[:, cols] = head_sum(d_att * o_ref[:, cols], ones) * ratio
+
+
+def middle_kernel(head, f_ref, dn_ref, *refs):
+    gain_ref = refs[-1]
+
+    @pl.when(pl.program_id(0) == 0)
+    def _():
+        gain_ref[...] = jnp.zeros_like(gain_ref)
+
+    middle_block(head, f_ref[...], dn_ref[...], *refs)
 
 
 def middle_call(ffn, d_normed, hidden, cotangent, g, w_o, mixed, totals, ones, head):
@@ -1103,15 +1297,15 @@
     cotangent = cotangent.reshape(total, width)
 
     w_qkv = jnp.concatenate([w_q, w_k, w_v], axis=1)
-    w_gate, w_down = fetch(w_gate), fetch(w_down)
+    w_down = fetch(w_down)
     grad_low = cotangent.astype(BF)
     if own_kernels:
-        up_pieces = col_pieces(0, share, w_up.shape[1], 256)
         qkv_pieces = col_pieces(0, share, w_qkv.shape[1])
         o_pieces = col_pieces(0, share, w_o.shape[1])
         [w_qkv] = gather_call([w_qkv], qkv_pieces, 0)
     else:
-        w_qkv, w_o, w_up = fetch(w_qkv), fetch(w_o), fetch(w_up)
+        w_qkv, w_o = fetch(w_qkv), fetch(w_o)
+        w_gate, w_up = fetch(w_gate), fetch(w_up)
 
     tables = (cos, sin, ones, head)
     normed, kv, raw_k = project_call(
@@ -1124,7 +1318,7 @@
         x, w_qkv, (0, q_width), q_width, g_attn[None, :], gains_q, *tables, head ** (-0.5), "project_q"
     )
     q = q.reshape(seqs, rows, q_width)
-    block_q, block_k = min(128, rows), 128
+    block_q, block_k = min(256, rows), min(256, length)
     at = jnp.arange(0, rows, block_q, dtype=jnp.int32)[None, :]
     lowest = first[:, ::block_q]
     zero = jnp.zeros((1,), jnp.int32)
@@ -1143,7 +1337,7 @@
         )
         near = attend_call(q, kv, own_first, own_keys, block_q, block_k, last_part=False)
         w_o, _ = lax.optimization_barrier((w_o, near))
-        [w_o] = gather_call([w_o], o_pieces, 4)
+        [w_o] = gather_call([w_o], [p[:3] + (True,) for p in o_pieces], 4)
         mixed, totals = attend_call(q, before, far_first, far_keys, block_q, block_k, near)
     else:
         kv = lax.all_gather(kv, "ctx", axis=1, tiled=True)
@@ -1156,21 +1350,20 @@
     mixed, totals = mixed.reshape(total, q_width), totals.reshape(total, q_width)
     attended, hidden, normed_two = hidden_call(mixed, w_o, x, g_ffn[None, :])
 
+    middle_args = (hidden, cotangent, g_ffn[None, :], w_o, mixed, totals, ones, head)
     if own_kernels:
-        normed_two, w_up = lax.optimization_barrier((normed_two, w_up))
-        [w_up] = gather_call([w_up], up_pieces, 1)
-        ffn, d_normed_two, grad_down, out_gate, out_up = ffn_call(
-            normed_two, grad_low, w_gate, w_up, w_down, 2
+        grad_down, out_gate, out_up, outputs, d_hidden, d_low, d_out, delta, grad_gffn = feed_call(
+            normed_two, grad_low, w_down, w_gate, w_up, *middle_args, 2
         )
     else:
         ffn, d_normed_two, grad_down, out_gate, out_up = ffn_call(
             normed_two, grad_low, w_gate, w_up, w_down
         )
         out_gate, out_up = send(out_gate), send(out_up)
+        outputs, d_hidden, d_low, d_out, delta, grad_gffn = middle_call(
+            ffn, d_normed_two, *middle_args
+        )
     out_down = send(grad_down)
-    outputs, d_hidden, d_low, d_out, delta, grad_gffn = middle_call(
-        ffn, d_normed_two, hidden, cotangent, g_ffn[None, :], w_o, mixed, totals, ones, head
-    )
     d_out, delta = d_out.reshape(q.shape), delta.reshape(q.shape)
     if own_kernels:
         far_dq, dk, dv = attend_back_call(

time: 611 us -> 586 us (0.959)
  Pallas kernels: 525 us -> 477 us
  waiting for transfers between devices: 14.7 us -> 26.4 us
    pallas_call x3 -> x2, Pallas kernels: 140 us -> 62.9 us  [gather_call(): pl.pallas_call(functools.partial(gather_kernel, pieces, count), in_specs=...]
    pallas_call x2 -> x1, Pallas kernels: 171 us -> 237 us  [feed_call(): pl.pallas_call(functools.partial(feed_kernel, block_t, steps, block_m, he...]
    pallas_call x2, Pallas kernels: 66 us -> 49.5 us  [attend_back_call(): pl.pallas_call(functools.partial(attend_back_kernel, block_q, block_k, he...]
    ppermute x1, waiting for transfers between devices: 13.3 us -> 25.7 us  [per_device(): got = lax.ppermute(jnp.concatenate([dk, dv], axis=2), 'ctx', [(1, 0)])]
    pallas_call x2, Pallas kernels: 42.4 us -> 31.3 us  [attend_call(): pl.pallas_call(functools.partial(attend_kernel, block_q, block_k, heads,...]
    pallas_call x1, Pallas kernels: 56.8 us -> 48.8 us  [scatter_call(): pl.pallas_call(functools.partial(scatter_kernel, pieces, count, len(gains...]
  transfers between devices with their start and end apart: 5 -> 4, of which waited for: 1 -> 1; matrix products, arithmetic and copies ran while one was open for 7% -> 7% of each run, Pallas kernels for 61% -> 41%
where the time goes in v4:
time: 586 us; the launch traced here: 580 us
  Pallas kernels  477 us (81%)
  waiting for transfers between devices  26.4 us (5%)
  other arithmetic  18.5 us (3%)
  local copies, waits for them, and re-layouts  17.5 us (3%)
  between operations  14.7 us (3%)
  matrix products  14.1 us (2%)
  starting transfers between devices  11.4 us (2%)
    pallas_call x1, Pallas kernels, feed_call(): pl.pallas_call(functools.partial(feed_kernel, block_t, steps, block_m, he...  237 us
    pallas_call x2, Pallas kernels, gather_call(): pl.pallas_call(functools.partial(gather_kernel, pieces, count), in_specs=...  62.9 us
    pallas_call x2, Pallas kernels, attend_back_call(): pl.pallas_call(functools.partial(attend_back_kernel, block_q, block_k, he...  49.5 us
    pallas_call x1, Pallas kernels, scatter_call(): pl.pallas_call(functools.partial(scatter_kernel, pieces, count, len(gains...  48.8 us
    pallas_call x2, Pallas kernels, attend_call(): pl.pallas_call(functools.partial(attend_kernel, block_q, block_k, heads,...  31.3 us
    ppermute x1, waiting for transfers between devices, per_device(): got = lax.ppermute(jnp.concatenate([dk, dv], axis=2), 'ctx', [(1, 0)])  25.7 us
    pallas_call x2, Pallas kernels, project_call(): pl.pallas_call(functools.partial(project_kernel, rope_width, head, scale)...  21.4 us
    pallas_call x1, Pallas kernels, last_call(): pl.pallas_call(functools.partial(last_kernel, q_width, kv_width, head, he...  18.2 us
  transfers between devices with their start and end apart: 4, of which 1 were waited for; matrix products, arithmetic and copies ran while one was open for 7% of the time, Pallas kernels for 41%

profile of v4, /device:TPU:0, one launch (start us, length us, event | category | flops | bytes accessed | tf_op | source)
XLA Modules:
  0.0 579.9 jit_solution(17874829791461904283)
XLA Ops:
  8.7 1.3 convert_reduce_fusion
  10.0 1.5 pad_maximum_fusion.3.refs_0_
  11.5 37.0 %gather.2 = bf16[4,2,2,2,32,2048]{5,4,3,2,1,0:T(8,128)(2,1)} custom-call(bf16[32,2048]{1,0:T(8,128)(2,1)} %pad_maximum_fusion.3.refs_0_), custom_call_target="tpu_custom_call" | custom-call | tf_op jit(solution)/shard_map/gather/pallas_call | solution.py:1037
  49.2 1.9 fusion
  51.1 1.8 pad_maximum_fusion.1
  53.8 9.1 %project_kv.1 = (bf16[1024,1024]{1,0:T(8,128)(2,1)}, bf16[1024,1024]{1,0:T(8,128)(2,1)}, f32[1024,512]{1,0:T(8,128)}) custom-call(bf16[1024,1024]{1,0:T(8,128)(2,1)} %bitcast.39, bf16[1024,2048]{1,0:T(8,128)(2,1)} %bitcast.36, f32[1,1024]{1,0:T(1,128)} %bitcast.70, f32[1,512]{1,0:T(1,128)} %bitcast.64, f32[1024,128]{1,0:T(8,128)} %get-tuple-element.98.cos_ref, ...), custom_call_target="tpu_custom_call" | custom-call | flops 2147483648 | bytes 12582912 | tf_op jit(solution)/shard_map/project_kv/pallas_call | solution.py:102
  62.9 10.0 %collective-permute-start = (bf16[2,512,1024]{2,1,0:T(8,128)(2,1)}, bf16[2,512,1024]{2,1,0:T(8,128)(2,1)S(1)}, u32[]{:S(2)}, u32[]{:S(2)}) collective-permute-start(bf16[2,512,1024]{2,1,0:T(8,128)(2,1)} %bitcast.77), channel_id=1, source_target_pairs={{0,1},{2,3},{4,5},{6,7},{8,9},{10,11},{12,13},{14,15},{16,17},{18,... | collective-permute-start | bytes 6291464 | tf_op jit(solution)/shard_map/ppermute | solution.py:1316
  73.6 1.0 copy.32.first_ref
  74.7 12.3 %project_q.1 = (bf16[1024,1024]{1,0:T(8,128)(2,1)}, bf16[1024,1024]{1,0:T(8,128)(2,1)}, f32[1024,1024]{1,0:T(8,128)}) custom-call(bf16[1024,1024]{1,0:T(8,128)(2,1)} %bitcast.40, bf16[1024,2048]{1,0:T(8,128)(2,1)} %bitcast.37, f32[1,1024]{1,0:T(1,128)} %bitcast.71, f32[1,1024]{1,0:T(1,128)} %bitcast.62, f32[1024,128]{1,0:T(8,128)} %get-tuple-element.98.cos_ref, ...), custom_call_target="tpu_custom_call" | custom-call | flops 2147483648 | bytes 12582912 | tf_op jit(solution)/shard_map/project_q/pallas_call | solution.py:102
  88.2 19.9 %attend.2 = (f32[2,512,1024]{2,1,0:T(8,128)}, f32[2,512,1024]{2,1,0:T(8,128)}) custom-call(s32[2,2]{1,0:T(2,128)} %get-tuple-element.96.low_ref, s32[2,2]{1,0:T(2,128)} %broadcast_in_dim.15.high_ref, s32[1]{0:T(128)} %constant.83.clone.1.start_ref, bf16[2,512,1024]{2,1,0:T(8,128)(2,1)} %bitcast.50, bf16[2,512,1024]{2,1,0:T(8,128)(2,1)} %bitcast.78, ...), custom_call_target="tpu_custom_call" | custom-call | flops 2147483648 | bytes 16777216 | tf_op jit(solution)/shard_map/attend/pallas_call | solution.py:201
  108.1 25.8 %gather.3 = bf16[4,2,2,2,32,1024]{5,4,3,2,1,0:T(8,128)(2,1)} custom-call(bf16[32,1024]{1,0:T(8,128)(2,1)} %refs_0_), custom_call_target="tpu_custom_call" | custom-call | tf_op jit(solution)/shard_map/gather/pallas_call | solution.py:1037
  133.9 1.0 copy.33.first_ref
  134.9 3.8 bitcast_convert_fusion.c_ref
  140.1 11.4 %attend.3 = (f32[2,512,1024]{2,1,0:T(8,128)}, f32[2,512,1024]{2,1,0:T(8,128)}) custom-call(s32[2,2]{1,0:T(2,128)} %get-tuple-element.97.low_ref, s32[2,2]{1,0:T(2,128)} %broadcast_14_high_ref.2.high_ref, s32[1]{0:T(128)} %constant.76.clone.1.start_ref, bf16[2,512,1024]{2,1,0:T(8,128)(2,1)} %bitcast.51, bf16[2,512,1024]{2,1,0:T(8,128)(2,1)} %copy-done, ...), custom_call_target="tpu_custom_call" | custom-call | flops 2147483648 | bytes 16777216 | tf_op jit(solution)/shard_map/attend/pallas_call | solution.py:201
  151.5 8.3 %hidden.1 = (bf16[1024,1024]{1,0:T(8,128)(2,1)}, f32[1024,1024]{1,0:T(8,128)}, bf16[1024,1024]{1,0:T(8,128)(2,1)}) custom-call(f32[1024,1024]{1,0:T(8,128)} %bitcast.48, bf16[1024,1024]{1,0:T(8,128)(2,1)} %bitcast.43, bf16[1024,1024]{1,0:T(8,128)(2,1)} %bitcast.41, f32[1,1024]{1,0:T(1,128)} %bitcast.68), custom_call_target="tpu_custom_call" | custom-call | tf_op jit(solution)/shard_map/hidden/pallas_call | solution.py:379
  159.8 236.8 %feed.1 = (bf16[4608,1024]{1,0:T(8,128)(2,1)}, f32[32,4608]{1,0:T(8,128)}, f32[32,4608]{1,0:T(8,128)}, bf16[4,2,2,2,32,4608]{5,4,3,2,1,0:T(8,128)(2,1)}, bf16[4,...) custom-call(bf16[1024,1024]{1,0:T(8,128)(2,1)} %get-tuple-element.55, ...), custom_call_target="tpu_custom_call" | custom-call | flops 86973087744 | bytes 56623104 | tf_op jit(solution)/shard_map/feed/pallas_call | solution.py:721
  397.2 13.5 %attend_back.2 = (f32[2,512,1024]{2,1,0:T(8,128)}, bf16[2,512,512]{2,1,0:T(8,128)(2,1)}, bf16[2,512,512]{2,1,0:T(8,128)(2,1)}) custom-call(s32[2,2]{1,0:T(2,128)} %get-tuple-element.97.low_ref, s32[2,2]{1,0:T(2,128)} %broadcast_14_high_ref.2.high_ref, s32[1]{0:T(128)} %constant.76.clone.1.start_ref, bf16[2,512,1024]{2,1,0:T(8,128)(2,1)} %bitcast.52, ...), custom_call_target="tpu_custom_call" | custom-call | flops 5368709120 | bytes 16777216 | tf_op jit(solution)/shard_map/attend_back/pallas_call | solution.py:330
  410.7 1.9 pad_maximum_fusion
  412.6 1.3 collective-permute-start.1
  415.1 36.1 %attend_back.3 = (f32[2,512,1024]{2,1,0:T(8,128)}, bf16[2,512,512]{2,1,0:T(8,128)(2,1)}, bf16[2,512,512]{2,1,0:T(8,128)(2,1)}) custom-call(s32[2,2]{1,0:T(2,128)} %get-tuple-element.96.low_ref, s32[2,2]{1,0:T(2,128)} %broadcast_in_dim.15.high_ref, s32[1]{0:T(128)} %constant.83.clone.1.start_ref, bf16[2,512,1024]{2,1,0:T(8,128)(2,1)} %bitcast.53, ...), custom_call_target="tpu_custom_call" | custom-call | flops 5368709120 | bytes 16777216 | tf_op jit(solution)/shard_map/attend_back/pallas_call | solution.py:330
  451.2 5.4 convolution_convert_fusion.1
  456.5 25.7 %collective-permute-done.1 = bf16[2,512,1024]{2,1,0:T(8,128)(2,1)S(1)} collective-permute-done((bf16[2,512,1024]{2,1,0:T(8,128)(2,1)S(1)}, bf16[2,512,1024]{2,1,0:T(8,128)(2,1)S(1)}, u32[]{:S(2)}, u32[]{:S(2)}) %collective-permute-start.1) | collective-permute-done | bytes 2097184 | tf_op jit(solution)/shard_map/ppermute | solution.py:1372
  482.2 1.3 copy-done.1
  483.6 18.2 %last.1 = (bf16[1024,2048]{1,0:T(8,128)(2,1)}, f32[1024,1024]{1,0:T(8,128)}, f32[1,1024]{1,0:T(1,128)}, f32[1,128]{1,0:T(1,128)}, f32[1,128]{1,0:T(1,128)}) custom-call(f32[1024,1024]{1,0:T(8,128)} %bitcast.45, bf16[1024,512]{1,0:T(8,128)(2,1)} %bitcast.57, bf16[1024,512]{1,0:T(8,128)(2,1)} %bitcast.58, f32[1024,1024]{1,0:T(8,128)} %get-tuple-element.65.rawq_ref, ...), custom_call_target="tpu_custom_call" | custom-call | tf_op jit(solution)/shard_map/last/pallas_call | solution.py:899
  503.1 8.8 %convolution_convert_fusion = bf16[1024,2048]{1,0:T(8,128)(2,1)} fusion(bf16[1024,1024]{1,0:T(8,128)(2,1)S(1)} %copy-done.12, bf16[1024,2048]{1,0:T(8,128)(2,1)} %get-tuple-element.72), kind=kOutput, calls=%fused_computation.1 | convolution fusion | flops 4297064448 | bytes 10485760 | tf_op jit(solution)/shard_map/dot_general | solution.py:25
  511.9 48.8 %scatter.1 = (f32[32,2048]{1,0:T(8,128)}, f32[32,1024]{1,0:T(8,128)}, f32[24,128]{1,0:T(8,128)}) custom-call(bf16[4,2,2,2,32,2048]{5,4,3,2,1,0:T(8,128)(2,1)} %bitcast.47, bf16[4,2,2,2,32,1024]{5,4,3,2,1,0:T(8,128)(2,1)} %bitcast.56, f32[24,128]{1,0:T(8,128)} %pad.4.refs_2_), custom_call_target="tpu_custom_call" | custom-call | tf_op jit(solution)/shard_map/scatter/pallas_call | solution.py:1220
  560.8 1.7 slice.25
  564.3 1.3 fusion.3
  565.6 1.5 fusion.2
  567.1 1.8 convert_element_type.43
  568.9 1.3 copy.39
  571.7 0.8 copy.42
  (59 shorter events, 12.7 us)
Async XLA Ops:
  7.2 41.4 %copy-start.7 = (f32[64]{0:T(128)S(1)}, f32[64]{0:T(128)}, u32[]{:S(2)}) copy-start(f32[64]{0:T(128)} %param.26) | copy-start | bytes 772
  7.2 152.6 %all-gather.2.cloned.1.call-start = ((), (), s32[]{:S(2)}) async-start(), calls=%async_computation.1 | async-start | bytes 9732096 | tf_op jit(solution)/shard_map/all_gather | solution.py:1277
  7.9 559.2 %reduce-scatter.2.cloned.1.call-start = ((), (), s32[]{:S(2)}) async-start(), calls=%async_computation.2 | async-start | bytes 9732096 | tf_op jit(solution)/shard_map/reduce_scatter | solution.py:1280
  53.0 20.0 %copy-start.5 = (f32[64]{0:T(128)S(1)}, f32[64]{0:T(128)}, u32[]{:S(2)}) copy-start(f32[64]{0:T(128)} %param.25) | copy-start | bytes 772
  62.9 75.9 %collective-permute-start = (bf16[2,512,1024]{2,1,0:T(8,128)(2,1)}, bf16[2,512,1024]{2,1,0:T(8,128)(2,1)S(1)}, u32[]{:S(2)}, u32[]{:S(2)}) collective-permute-start(bf16[2,512,1024]{2,1,0:T(8,128)(2,1)} %bitcast.77), channel_id=1, source_target_pairs={{0,1},{2,3},{4,5},{6,7},{8,9},{10,11},{12,13},{14,15},{16,17},{18,... | collective-permute-start | bytes 6291464 | tf_op jit(solution)/shard_map/ppermute | solution.py:1316
  138.7 1.3 copy-start
  410.7 3.8 copy-start.8
  410.7 3.8 copy-start.9
  412.6 69.6 %collective-permute-start.1 = (bf16[2,512,1024]{2,1,0:T(8,128)(2,1)S(1)}, bf16[2,512,1024]{2,1,0:T(8,128)(2,1)S(1)}, u32[]{:S(2)}, u32[]{:S(2)}) collective-permute-start(bf16[2,512,1024]{2,1,0:T(8,128)(2,1)S(1)} %pad_maximum_fusion), channel_id=1, source_target_pairs={{1,0},{3,2},{5,4},{7,6},{9,8},{11,10},{13,12},{15,14},{17,16},{19,... | collective-permute-start | bytes 6291464 | tf_op jit(solution)/shard_map/ppermute | solution.py:1372
  415.1 36.1 %copy-start.11 = (bf16[1024,1024]{1,0:T(8,128)(2,1)S(1)}, bf16[1024,1024]{1,0:T(8,128)(2,1)}, u32[]{:S(2)}) copy-start(bf16[1024,1024]{1,0:T(8,128)(2,1)} %get-tuple-element.73) | copy-start | bytes 6291460
  482.2 1.3 copy-start.1
  483.5 18.2 %copy-start.10 = (f32[1,1024]{1,0:T(1,128)S(1)}, f32[1,1024]{1,0:T(1,128)}, u32[]{:S(2)}) copy-start(f32[1,1024]{1,0:T(1,128)} %get-tuple-element.76) | copy-start | bytes 12292
  483.6 19.6 %copy-start.12 = (bf16[1024,1024]{1,0:T(8,128)(2,1)S(1)}, bf16[1024,1024]{1,0:T(8,128)(2,1)}, u32[]{:S(2)}) copy-start(bf16[1024,1024]{1,0:T(8,128)(2,1)} %get-tuple-element.71) | copy-start | bytes 6291460
  511.9 57.0 %copy-start.2 = (bf16[1024,1024]{1,0:T(8,128)(2,1)S(1)}, bf16[1024,1024]{1,0:T(8,128)(2,1)}, u32[]{:S(2)}) copy-start(bf16[1024,1024]{1,0:T(8,128)(2,1)} %get-tuple-element.58) | copy-start | bytes 6291460
  560.7 9.5 %copy-start.6 = (f32[32,1024]{1,0:T(8,128)S(1)}, f32[32,1024]{1,0:T(8,128)}, u32[]{:S(2)}) copy-start(f32[32,1024]{1,0:T(8,128)} %get-tuple-element.118) | copy-start | bytes 393220
  560.7 10.2 %copy-start.4 = (f32[32,4608]{1,0:T(8,128)S(1)}, f32[32,4608]{1,0:T(8,128)}, u32[]{:S(2)}) copy-start(f32[32,4608]{1,0:T(8,128)} %get-tuple-element.119) | copy-start | bytes 1769476
  560.7 11.0 %copy-start.3 = (f32[32,4608]{1,0:T(8,128)S(1)}, f32[32,4608]{1,0:T(8,128)}, u32[]{:S(2)}) copy-start(f32[32,4608]{1,0:T(8,128)} %get-tuple-element.120) | copy-start | bytes 1769476
Sparse Core Ops, SparseCore 0:
  10.9 87.9 all-gather.1
  396.7 141.7 reduce-scatter.1

commit v5 on v4

--- a/solution.py
+++ b/solution.py
@@ -1,4 +1,5 @@
 import functools
+import itertools
 
 import jax
 import jax.numpy as jnp
@@ -480,30 +481,34 @@
 
 
 class ColumnGather:
-    def __init__(self, me, own, whole, slots, send, recv, keep_sems, load_sems):
+    def __init__(self, me, own, whole, slots, send, recv, keep_sem, load_sems):
         self.me, self.own, self.whole, self.slots = me, own, whole, slots
-        self.sems, self.keep_sems, self.load_sems = (send, recv), keep_sems, load_sems
-
-    def cols(self, k):
+        self.sems, self.keep_sem, self.load_sems = (send, recv), keep_sem, load_sems
+
+    def cols(self, k, j=None):
         width = self.slots.shape[-1]
-        start = k * width
-        return pl.ds(start if isinstance(k, int) else pl.multiple_of(start, width), width)
-
-    def keep(self, j):
+        start = k * width if isinstance(k, int) else pl.multiple_of(k * width, width)
+        if j is None:
+            return pl.ds(start, width)
+        half = width // 2
+        start = start + j * half
+        return pl.ds(start if isinstance(k, int) else pl.multiple_of(start, half), half)
+
+    def keep(self):
         me = self.me
         return pltpu.make_async_copy(
-            self.own[j], self.whole[j].at[me.z, me.y, me.c, me.x], self.keep_sems.at[j]
+            self.own, self.whole.at[me.z, me.y, me.c, me.x], self.keep_sem.at[0]
         )
 
     def hop(self, k, j, s):
         me, every = self.me, slice(None)
-        whole = self.whole[j]
+        whole = self.whole
 
         def mine(z, y, c, x):
-            return whole.at[z, y, c, x, every, self.cols(k)]
+            return whole.at[z, y, c, x, every, self.cols(k, j)]
 
         if s == 0:
-            give = self.own[j].at[:, self.cols(k)]
+            give = self.own.at[:, self.cols(k, j)]
             return [
                 remote(give, mine(me.z, me.y, me.c, me.x), self.sems, (k, j, d - 1), me.peer(z=me.up(d)))
                 for d in (1, 2, 3)
@@ -519,12 +524,12 @@
             give, peer = mine(every, every, me.c, every), me.peer(c=1 - me.c)
         return [remote(give, give, self.sems, (k, j, 2 + s), peer)]
 
-    def load(self, k, j):
+    def load(self, k):
         every = slice(None)
         slot = k % 2 if isinstance(k, int) else lax.rem(k, 2)
         return pltpu.make_async_copy(
-            self.whole[j].at[every, every, every, every, every, self.cols(k)],
-            self.slots.at[slot, j], self.load_sems.at[slot, j],
+            self.whole.at[every, every, every, every, every, self.cols(k)],
+            self.slots.at[slot], self.load_sems.at[slot],
         )
 
     def start(self, k, s):
@@ -538,12 +543,10 @@
                 copy.wait()
 
     def open(self):
-        for j in (0, 1):
-            self.keep(j).start()
+        self.keep().start()
         for k in range(3):
             self.start(k, 0)
-        for j in (0, 1):
-            self.keep(j).wait()
+        self.keep().wait()
         for k, s in ((0, 1), (1, 1), (0, 2), (2, 1), (1, 2), (0, 3), (3, 1), (2, 2), (1, 3), (4, 1), (3, 2), (5, 1)):
             self.wait(k, s - 1)
             self.start(k, s)
@@ -553,12 +556,10 @@
 
     def fetch(self, k):
         self.wait(k, 3)
-        for j in (0, 1):
-            self.load(k, j).start()
+        self.load(k).start()
 
     def ready(self, k):
-        for j in (0, 1):
-            self.load(k, j).wait()
+        self.load(k).wait()
 
     def advance(self, step, steps):
         for s, early in ((1, 6), (2, 4), (3, 2)):
@@ -573,10 +574,6 @@
         def _():
             self.start(step + 9, 0)
 
-        @pl.when(step + 1 < steps)
-        def _():
-            self.fetch(step + 1)
-
 
 class GradSums:
     def __init__(self, me, outs, made, r0, r1, r2, r3, send, recv):
@@ -584,39 +581,49 @@
         self.r0, self.r1, self.r2, self.r3, self.send, self.recv = r0, r1, r2, r3, send, recv
 
     def keep(self, step, i, j, grad):
-        self.made[lax.rem(step, 2), j, i] = grad.astype(BF).reshape(self.made.shape[3:])
+        slot = lax.rem(step, 2)
+        grad = grad.astype(BF)
+        share = self.made.shape[-2]
+        for y, c, x in itertools.product((0, 1), (0, 1), (0, 1)):
+            row = ((y * 2 + c) * 2 + x) * share
+            one, two = (x, y) if j == 0 else (y, x)
+            self.made[slot, j, c, one, two, i] = grad[row : row + share]
+
+    def axes(self, j):
+        me = self.me
+        along_x = (me.x, me.peer(x=1 - me.x))
+        along_y = (me.y, me.peer(y=1 - me.y))
+        return (along_x, along_y) if j == 0 else (along_y, along_x)
 
     def hop(self, k, j, s):
-        me, every = self.me, slice(None)
+        me = self.me
         sems = (self.send, self.recv)
         r0, r1, r2, r3 = (r.at[k, j] for r in (self.r0, self.r1, self.r2, self.r3))
-        to_x, to_y = me.peer(x=1 - me.x), me.peer(y=1 - me.y)
+        (one, to_one), (two, to_two) = self.axes(j)
         if s == 0:
-            give = self.made.at[lax.rem(k, 2), j, every, every, 1 - me.c]
+            give = self.made.at[lax.rem(k, 2), j, 1 - me.c]
             return [remote(give, r0, sems, (k, j, 0), me.peer(c=1 - me.c))]
         if s == 1:
-            if j == 0:
-                return [remote(r0.at[every, every, 1 - me.x], r1, sems, (k, j, 1), to_x)]
-            return [remote(r0.at[every, 1 - me.y], r1, sems, (k, j, 1), to_y)]
+            return [remote(r0.at[1 - one], r1, sems, (k, j, 1), to_one)]
         if s == 2:
-            other, peer = (1 - me.y, to_y) if j == 0 else (1 - me.x, to_x)
-            return [remote(r1.at[every, other], r2, sems, (k, j, 2), peer)]
+            return [remote(r1.at[1 - two], r2, sems, (k, j, 2), to_two)]
         return [
             remote(r2.at[me.up(d)], r3.at[d - 1], sems, (k, j, 2 + d), me.peer(z=me.up(d)))
             for d in (1, 2, 3)
         ]
 
     def settle(self, k, j, s):
-        me, every = self.me, slice(None)
+        me = self.me
         r0, r1, r2, r3 = (r.at[k, j] for r in (self.r0, self.r1, self.r2, self.r3))
+        (one, _), (two, _) = self.axes(j)
         for copy in self.hop(k, j, s):
             copy.wait()
         if s == 0:
-            add_into(r0, self.made.at[lax.rem(k, 2), j, every, every, me.c])
+            add_into(r0, self.made.at[lax.rem(k, 2), j, me.c])
         elif s == 1:
-            add_into(r1, r0.at[every, every, me.x] if j == 0 else r0.at[every, me.y])
+            add_into(r1, r0.at[one])
         elif s == 2:
-            add_into(r2, r1.at[every, me.y if j == 0 else me.x])
+            add_into(r2, r1.at[two])
         else:
             width = r2.shape[-1]
             cols = pl.ds(pl.multiple_of(k * width, width), width)
@@ -625,7 +632,7 @@
             )
 
     def advance(self, step, steps):
-        for s, late in ((3, 6), (2, 5), (1, 3), (0, 1)):
+        for s, late in ((3, 4), (2, 3), (1, 2), (0, 1)):
             k = step - late
 
             @pl.when((k >= 0) & (k < steps))
@@ -639,16 +646,14 @@
 
 def feed_kernel(
     block_t, steps, block_m, head,
-    n_ref, c_ref, wd_ref, own_gate, own_up, h_ref, cot_ref, g_ref, w_ref, o_ref, l_ref, ones_ref,
-    gd_ref, gg_ref, gu_ref, all_gate, all_up, out_ref, dh_ref, low_ref, do_ref, de_ref, gain_ref,
+    n_ref, c_ref, wg_ref, wd_ref, own_up, h_ref, cot_ref, g_ref, w_ref, o_ref, l_ref, ones_ref,
+    gd_ref, gg_ref, gu_ref, all_up, out_ref, dh_ref, low_ref, do_ref, de_ref, gain_ref,
     n_scr, act_scr, dg_scr, du_scr, f_scr, dn_scr, slots, made, r0, r1, r2, r3,
     g_send, g_recv, s_send, s_recv, keep_sems, load_sems,
 ):
     step = pl.program_id(0)
     me = Place()
-    gather = ColumnGather(
-        me, (own_gate, own_up), (all_gate, all_up), slots, g_send, g_recv, keep_sems, load_sems
-    )
+    gather = ColumnGather(me, own_up, all_up, slots, g_send, g_recv, keep_sems, load_sems)
     sums = GradSums(me, (gg_ref, gu_ref), made, r0, r1, r2, r3, s_send, s_recv)
 
     @pl.when(step == 0)
@@ -666,11 +671,16 @@
         width, chunk = n_ref.shape[1], wd_ref.shape[0]
         ffn_block(
             block_t, n_ref, c_ref,
-            lambda: slots[slot, 0].reshape(width, chunk),
-            lambda: slots[slot, 1].reshape(width, chunk),
+            lambda: wg_ref[...],
+            lambda: slots[slot].reshape(width, chunk),
             lambda: wd_ref[...],
             f_scr, dn_scr, act_scr, dg_scr, du_scr,
         )
+
+        @pl.when(step + 1 < steps)
+        def _():
+            gather.fetch(step + 1)
+
         for i in range(width // 256):
             normed = n_scr[256 * i : 256 * i + 256, :]
             sums.keep(step, i, 0, mm(normed, dg_scr[...]))
@@ -700,11 +710,11 @@
 
 
 def feed_call(
-    normed, grad_low, w_down, own_gate, own_up, hidden, cotangent, g, w_o, mixed, totals, ones, head,
+    normed, grad_low, w_gate, w_down, own_up, hidden, cotangent, g, w_o, mixed, totals, ones, head,
     collective,
 ):
     total, width = normed.shape
-    share, units = own_gate.shape
+    share, units = own_up.shape
     q_width = mixed.shape[1]
     chunk = largest_block(units, 512)
     steps = units // chunk
@@ -717,17 +727,18 @@
 
     anywhere = pl.BlockSpec(memory_space=pl.ANY)
     rows = pl.BlockSpec((chunk, width), lambda i: (jnp.minimum(i, last), 0))
+    cols = pl.BlockSpec((width, chunk), lambda i: (0, jnp.minimum(i, last)))
     whole = jax.ShapeDtypeStruct((4, 2, 2, 2, share, units), BF)
     outs = pl.pallas_call(
         functools.partial(feed_kernel, block_t, steps, block_m, head),
         grid=(steps + total // block_m,),
         in_specs=[
-            resident(normed.shape), resident(normed.shape), rows, anywhere, anywhere,
+            resident(normed.shape), resident(normed.shape), cols, rows, anywhere,
             after(width), after(width), resident(g.shape), resident(w_o.shape), after(q_width),
             after(q_width), resident(ones.shape),
         ],
         out_specs=[
-            rows, resident((share, units)), resident((share, units)), anywhere, anywhere,
+            rows, resident((share, units)), resident((share, units)), anywhere,
             after(width), after(width), after(width), after(q_width), after(q_width),
             resident((1, width)),
         ],
@@ -735,7 +746,7 @@
             jax.ShapeDtypeStruct(w_down.shape, BF),
             jax.ShapeDtypeStruct((share, units), F32),
             jax.ShapeDtypeStruct((share, units), F32),
-            whole, whole,
+            whole,
             jax.ShapeDtypeStruct((total, width), BF),
             jax.ShapeDtypeStruct((total, width), F32),
             jax.ShapeDtypeStruct((total, width), BF),
@@ -750,15 +761,15 @@
             pltpu.VMEM((total, chunk), BF),
             pltpu.VMEM((total, width), F32),
             pltpu.VMEM((total, width), F32),
-            pltpu.VMEM((2, 2, 4, 2, 2, 2) + piece, BF),
-            pltpu.VMEM((2, 2, 4, 2, 2, 2) + piece, BF),
-            pltpu.VMEM((steps, 2, 4, 2, 2) + piece, BF),
-            pltpu.VMEM((steps, 2, 4, 2) + piece, BF),
+            pltpu.VMEM((2, 4, 2, 2, 2) + piece, BF),
+            pltpu.VMEM((2, 2, 2, 2, 2, 4) + piece, BF),
+            pltpu.VMEM((steps, 2, 2, 2, 4) + piece, BF),
+            pltpu.VMEM((steps, 2, 2, 4) + piece, BF),
             pltpu.VMEM((steps, 2, 4) + piece, BF),
             pltpu.VMEM((steps, 2, 3) + piece, BF),
         ]
         + [pltpu.SemaphoreType.DMA((steps, 2, 6))] * 4
-        + [pltpu.SemaphoreType.DMA((2,)), pltpu.SemaphoreType.DMA((2, 2))],
+        + [pltpu.SemaphoreType.DMA((1,)), pltpu.SemaphoreType.DMA((2,))],
         compiler_params=pltpu.CompilerParams(
             vmem_limit_bytes=62 * 2**20, collective_id=collective, has_side_effects=True
         ),
@@ -767,9 +778,9 @@
         ),
         name="feed",
     )(
-        normed, grad_low, w_down, own_gate, own_up, hidden, cotangent, g, w_o, mixed, totals, ones
+        normed, grad_low, w_gate, w_down, own_up, hidden, cotangent, g, w_o, mixed, totals, ones
     )
-    return outs[:3] + outs[5:]
+    return outs[:3] + outs[4:]
 
 
 def middle_block(
@@ -1297,7 +1308,7 @@
     cotangent = cotangent.reshape(total, width)
 
     w_qkv = jnp.concatenate([w_q, w_k, w_v], axis=1)
-    w_down = fetch(w_down)
+    w_down, w_gate = fetch(w_down), fetch(w_gate)
     grad_low = cotangent.astype(BF)
     if own_kernels:
         qkv_pieces = col_pieces(0, share, w_qkv.shape[1])
@@ -1305,7 +1316,7 @@
         [w_qkv] = gather_call([w_qkv], qkv_pieces, 0)
     else:
         w_qkv, w_o = fetch(w_qkv), fetch(w_o)
-        w_gate, w_up = fetch(w_gate), fetch(w_up)
+        w_up = fetch(w_up)
 
     tables = (cos, sin, ones, head)
     normed, kv, raw_k = project_call(
@@ -1353,7 +1364,7 @@
     middle_args = (hidden, cotangent, g_ffn[None, :], w_o, mixed, totals, ones, head)
     if own_kernels:
         grad_down, out_gate, out_up, outputs, d_hidden, d_low, d_out, delta, grad_gffn = feed_call(
-            normed_two, grad_low, w_down, w_gate, w_up, *middle_args, 2
+            normed_two, grad_low, w_gate, w_down, w_up, *middle_args, 2
         )
     else:
         ffn, d_normed_two, grad_down, out_gate, out_up = ffn_call(

time: 586 us -> 576 us (0.983)
  Pallas kernels: 477 us -> 433 us
  waiting for transfers between devices: 26.4 us -> 65.7 us
    pallas_call x1, Pallas kernels: 237 us -> 184 us  [feed_call(): pl.pallas_call(functools.partial(feed_kernel, block_t, steps, block_m, he...]
    all_gather x1 -> x2, waiting for transfers between devices: 0.01 us -> 41 us  [fetch(): return lax.all_gather(weight, AXES, axis=0, tiled=True)]
    pallas_call x2, Pallas kernels: 62.9 us -> 69.9 us  [gather_call(): pl.pallas_call(functools.partial(gather_kernel, pieces, count), in_specs=...]
  transfers between devices with their start and end apart: 4 -> 5, of which waited for: 1 -> 2; matrix products, arithmetic and copies ran while one was open for 7% -> 7% of each run, Pallas kernels for 41% -> 44%
where the time goes in v5:
time: 576 us; the launch traced here: 570 us
  Pallas kernels  433 us (75%)
  waiting for transfers between devices  65.7 us (11%)
  other arithmetic  18.6 us (3%)
  local copies, waits for them, and re-layouts  17.5 us (3%)
  between operations  14.4 us (2%)
  matrix products  14.1 us (2%)
  starting transfers between devices  7.16 us (1%)
    pallas_call x1, Pallas kernels, feed_call(): pl.pallas_call(functools.partial(feed_kernel, block_t, steps, block_m, he...  184 us
    pallas_call x2, Pallas kernels, gather_call(): pl.pallas_call(functools.partial(gather_kernel, pieces, count), in_specs=...  69.9 us
    pallas_call x1, Pallas kernels, scatter_call(): pl.pallas_call(functools.partial(scatter_kernel, pieces, count, len(gains...  50.1 us
    pallas_call x2, Pallas kernels, attend_back_call(): pl.pallas_call(functools.partial(attend_back_kernel, block_q, block_k, he...  49.6 us
    all_gather x2, waiting for transfers between devices, fetch(): return lax.all_gather(weight, AXES, axis=0, tiled=True)  41 us
    pallas_call x2, Pallas kernels, attend_call(): pl.pallas_call(functools.partial(attend_kernel, block_q, block_k, heads,...  31.3 us
    ppermute x1, waiting for transfers between devices, per_device(): got = lax.ppermute(jnp.concatenate([dk, dv], axis=2), 'ctx', [(1, 0)])  23.4 us
    pallas_call x2, Pallas kernels, project_call(): pl.pallas_call(functools.partial(project_kernel, rope_width, head, scale)...  21.4 us
  transfers between devices with their start and end apart: 5, of which 2 were waited for; matrix products, arithmetic and copies ran while one was open for 7% of the time, Pallas kernels for 44%

profile of v5, /device:TPU:0, one launch (start us, length us, event | category | flops | bytes accessed | tf_op | source)
XLA Modules:
  0.0 570.0 jit_solution(16800118459680451560)
XLA Ops:
  9.4 1.3 convert_reduce_fusion
  10.7 1.5 pad_maximum_fusion.3.refs_0_
  12.3 42.2 %gather.2 = bf16[4,2,2,2,32,2048]{5,4,3,2,1,0:T(8,128)(2,1)} custom-call(bf16[32,2048]{1,0:T(8,128)(2,1)} %pad_maximum_fusion.3.refs_0_), custom_call_target="tpu_custom_call" | custom-call | tf_op jit(solution)/shard_map/gather/pallas_call | solution.py:1048
  55.2 1.9 fusion
  57.1 1.8 pad_maximum_fusion.1
  59.7 9.1 %project_kv.1 = (bf16[1024,1024]{1,0:T(8,128)(2,1)}, bf16[1024,1024]{1,0:T(8,128)(2,1)}, f32[1024,512]{1,0:T(8,128)}) custom-call(bf16[1024,1024]{1,0:T(8,128)(2,1)} %bitcast.39, bf16[1024,2048]{1,0:T(8,128)(2,1)} %bitcast.36, f32[1,1024]{1,0:T(1,128)} %bitcast.70, f32[1,512]{1,0:T(1,128)} %bitcast.64, f32[1024,128]{1,0:T(8,128)} %get-tuple-element.98.cos_ref, ...), custom_call_target="tpu_custom_call" | custom-call | flops 2147483648 | bytes 12582912 | tf_op jit(solution)/shard_map/project_kv/pallas_call | solution.py:103
  68.8 5.8 %collective-permute-start = (bf16[2,512,1024]{2,1,0:T(8,128)(2,1)}, bf16[2,512,1024]{2,1,0:T(8,128)(2,1)S(1)}, u32[]{:S(2)}, u32[]{:S(2)}) collective-permute-start(bf16[2,512,1024]{2,1,0:T(8,128)(2,1)} %bitcast.77), channel_id=1, source_target_pairs={{0,1},{2,3},{4,5},{6,7},{8,9},{10,11},{12,13},{14,15},{16,17},{18,... | collective-permute-start | bytes 6291464 | tf_op jit(solution)/shard_map/ppermute | solution.py:1327
  75.3 1.0 copy.32.first_ref
  76.3 12.3 %project_q.1 = (bf16[1024,1024]{1,0:T(8,128)(2,1)}, bf16[1024,1024]{1,0:T(8,128)(2,1)}, f32[1024,1024]{1,0:T(8,128)}) custom-call(bf16[1024,1024]{1,0:T(8,128)(2,1)} %bitcast.40, bf16[1024,2048]{1,0:T(8,128)(2,1)} %bitcast.37, f32[1,1024]{1,0:T(1,128)} %bitcast.71, f32[1,1024]{1,0:T(1,128)} %bitcast.62, f32[1024,128]{1,0:T(8,128)} %get-tuple-element.98.cos_ref, ...), custom_call_target="tpu_custom_call" | custom-call | flops 2147483648 | bytes 12582912 | tf_op jit(solution)/shard_map/project_q/pallas_call | solution.py:103
  89.8 19.9 %attend.2 = (f32[2,512,1024]{2,1,0:T(8,128)}, f32[2,512,1024]{2,1,0:T(8,128)}) custom-call(s32[2,2]{1,0:T(2,128)} %get-tuple-element.96.low_ref, s32[2,2]{1,0:T(2,128)} %broadcast_in_dim.15.high_ref, s32[1]{0:T(128)} %constant.83.clone.1.start_ref, bf16[2,512,1024]{2,1,0:T(8,128)(2,1)} %bitcast.50, bf16[2,512,1024]{2,1,0:T(8,128)(2,1)} %bitcast.78, ...), custom_call_target="tpu_custom_call" | custom-call | flops 2147483648 | bytes 16777216 | tf_op jit(solution)/shard_map/attend/pallas_call | solution.py:202
  109.7 27.7 %gather.3 = bf16[4,2,2,2,32,1024]{5,4,3,2,1,0:T(8,128)(2,1)} custom-call(bf16[32,1024]{1,0:T(8,128)(2,1)} %refs_0_), custom_call_target="tpu_custom_call" | custom-call | tf_op jit(solution)/shard_map/gather/pallas_call | solution.py:1048
  137.4 1.0 copy.33.first_ref
  138.4 3.9 bitcast_convert_fusion.c_ref
  143.6 11.4 %attend.3 = (f32[2,512,1024]{2,1,0:T(8,128)}, f32[2,512,1024]{2,1,0:T(8,128)}) custom-call(s32[2,2]{1,0:T(2,128)} %get-tuple-element.97.low_ref, s32[2,2]{1,0:T(2,128)} %broadcast_14_high_ref.2.high_ref, s32[1]{0:T(128)} %constant.76.clone.1.start_ref, bf16[2,512,1024]{2,1,0:T(8,128)(2,1)} %bitcast.51, bf16[2,512,1024]{2,1,0:T(8,128)(2,1)} %copy-done, ...), custom_call_target="tpu_custom_call" | custom-call | flops 2147483648 | bytes 16777216 | tf_op jit(solution)/shard_map/attend/pallas_call | solution.py:202
  155.1 8.3 %hidden.1 = (bf16[1024,1024]{1,0:T(8,128)(2,1)}, f32[1024,1024]{1,0:T(8,128)}, bf16[1024,1024]{1,0:T(8,128)(2,1)}) custom-call(f32[1024,1024]{1,0:T(8,128)} %bitcast.48, bf16[1024,1024]{1,0:T(8,128)(2,1)} %bitcast.43, bf16[1024,1024]{1,0:T(8,128)(2,1)} %bitcast.41, f32[1,1024]{1,0:T(1,128)} %bitcast.68), custom_call_target="tpu_custom_call" | custom-call | tf_op jit(solution)/shard_map/hidden/pallas_call | solution.py:380
  163.4 40.9 %all-gather.5.cloned.1.call-done.wd_ref = bf16[4608,1024]{1,0:T(8,128)(2,1)} async-done(((bf16[144,1024]{1,0:T(8,128)(2,1)}), bf16[4608,1024]{1,0:T(8,128)(2,1)}) %all-gather.5.cloned.1.call-update) | async-done | bytes 9437200 | tf_op jit(solution)/shard_map/all_gather | solution.py:1288
  204.3 183.7 %feed.1 = (bf16[4608,1024]{1,0:T(8,128)(2,1)}, f32[32,4608]{1,0:T(8,128)}, f32[32,4608]{1,0:T(8,128)}, bf16[4,2,2,2,32,4608]{5,4,3,2,1,0:T(8,128)(2,1)}, bf16[10...) custom-call(bf16[1024,1024]{1,0:T(8,128)(2,1)} %get-tuple-element.55, ...), custom_call_target="tpu_custom_call" | custom-call | flops 86973087744 | bytes 56623104 | tf_op jit(solution)/shard_map/feed/pallas_call | solution.py:732
  388.6 13.5 %attend_back.2 = (f32[2,512,1024]{2,1,0:T(8,128)}, bf16[2,512,512]{2,1,0:T(8,128)(2,1)}, bf16[2,512,512]{2,1,0:T(8,128)(2,1)}) custom-call(s32[2,2]{1,0:T(2,128)} %get-tuple-element.97.low_ref, s32[2,2]{1,0:T(2,128)} %broadcast_14_high_ref.2.high_ref, s32[1]{0:T(128)} %constant.76.clone.1.start_ref, bf16[2,512,1024]{2,1,0:T(8,128)(2,1)} %bitcast.52, ...), custom_call_target="tpu_custom_call" | custom-call | flops 5368709120 | bytes 16777216 | tf_op jit(solution)/shard_map/attend_back/pallas_call | solution.py:331
  402.1 1.9 pad_maximum_fusion
  404.1 1.3 collective-permute-start.1
  406.6 36.1 %attend_back.3 = (f32[2,512,1024]{2,1,0:T(8,128)}, bf16[2,512,512]{2,1,0:T(8,128)(2,1)}, bf16[2,512,512]{2,1,0:T(8,128)(2,1)}) custom-call(s32[2,2]{1,0:T(2,128)} %get-tuple-element.96.low_ref, s32[2,2]{1,0:T(2,128)} %broadcast_in_dim.15.high_ref, s32[1]{0:T(128)} %constant.83.clone.1.start_ref, bf16[2,512,1024]{2,1,0:T(8,128)(2,1)} %bitcast.53, ...), custom_call_target="tpu_custom_call" | custom-call | flops 5368709120 | bytes 16777216 | tf_op jit(solution)/shard_map/attend_back/pallas_call | solution.py:331
  442.7 5.3 convolution_convert_fusion.1
  448.0 23.4 %collective-permute-done.1 = bf16[2,512,1024]{2,1,0:T(8,128)(2,1)S(1)} collective-permute-done((bf16[2,512,1024]{2,1,0:T(8,128)(2,1)S(1)}, bf16[2,512,1024]{2,1,0:T(8,128)(2,1)S(1)}, u32[]{:S(2)}, u32[]{:S(2)}) %collective-permute-start.1) | collective-permute-done | bytes 2097184 | tf_op jit(solution)/shard_map/ppermute | solution.py:1383
  471.4 1.3 copy-done.1
  472.7 18.2 %last.1 = (bf16[1024,2048]{1,0:T(8,128)(2,1)}, f32[1024,1024]{1,0:T(8,128)}, f32[1,1024]{1,0:T(1,128)}, f32[1,128]{1,0:T(1,128)}, f32[1,128]{1,0:T(1,128)}) custom-call(f32[1024,1024]{1,0:T(8,128)} %bitcast.45, bf16[1024,512]{1,0:T(8,128)(2,1)} %bitcast.57, bf16[1024,512]{1,0:T(8,128)(2,1)} %bitcast.58, f32[1024,1024]{1,0:T(8,128)} %get-tuple-element.65.rawq_ref, ...), custom_call_target="tpu_custom_call" | custom-call | tf_op jit(solution)/shard_map/last/pallas_call | solution.py:910
  492.3 8.8 %convolution_convert_fusion = bf16[1024,2048]{1,0:T(8,128)(2,1)} fusion(bf16[1024,1024]{1,0:T(8,128)(2,1)S(1)} %copy-done.12, bf16[1024,2048]{1,0:T(8,128)(2,1)} %get-tuple-element.72), kind=kOutput, calls=%fused_computation.1 | convolution fusion | flops 4297064448 | bytes 10485760 | tf_op jit(solution)/shard_map/dot_general | solution.py:26
  501.0 50.1 %scatter.1 = (f32[32,2048]{1,0:T(8,128)}, f32[32,1024]{1,0:T(8,128)}, f32[24,128]{1,0:T(8,128)}) custom-call(bf16[4,2,2,2,32,2048]{5,4,3,2,1,0:T(8,128)(2,1)} %bitcast.47, bf16[4,2,2,2,32,1024]{5,4,3,2,1,0:T(8,128)(2,1)} %bitcast.56, f32[24,128]{1,0:T(8,128)} %pad.4.refs_2_), custom_call_target="tpu_custom_call" | custom-call | tf_op jit(solution)/shard_map/scatter/pallas_call | solution.py:1231
  551.1 1.7 slice.25
  554.7 1.3 fusion.3
  556.0 1.5 fusion.2
  557.6 1.8 convert_element_type.43
  559.4 1.3 copy.39
  (62 shorter events, 14.3 us)
Async XLA Ops:
  7.2 47.3 %copy-start.7 = (f32[64]{0:T(128)S(1)}, f32[64]{0:T(128)}, u32[]{:S(2)}) copy-start(f32[64]{0:T(128)} %param.26) | copy-start | bytes 772
  7.2 156.2 %all-gather.3.cloned.1.call-start = ((), (), s32[]{:S(2)}) async-start(), calls=%async_computation.1 | async-start | bytes 9732096 | tf_op jit(solution)/shard_map/all_gather | solution.py:1288
  7.9 196.4 %all-gather.5.cloned.1.call-start = ((), (), s32[]{:S(2)}) async-start(), calls=%async_computation.2 | async-start | bytes 9732096 | tf_op jit(solution)/shard_map/all_gather | solution.py:1288
  8.7 548.9 %reduce-scatter.2.cloned.1.call-start = ((), (), s32[]{:S(2)}) async-start(), calls=%async_computation.3 | async-start | bytes 9732096 | tf_op jit(solution)/shard_map/reduce_scatter | solution.py:1291
  58.9 15.7 %copy-start.5 = (f32[64]{0:T(128)S(1)}, f32[64]{0:T(128)}, u32[]{:S(2)}) copy-start(f32[64]{0:T(128)} %param.25) | copy-start | bytes 772
  68.8 73.5 %collective-permute-start = (bf16[2,512,1024]{2,1,0:T(8,128)(2,1)}, bf16[2,512,1024]{2,1,0:T(8,128)(2,1)S(1)}, u32[]{:S(2)}, u32[]{:S(2)}) collective-permute-start(bf16[2,512,1024]{2,1,0:T(8,128)(2,1)} %bitcast.77), channel_id=1, source_target_pairs={{0,1},{2,3},{4,5},{6,7},{8,9},{10,11},{12,13},{14,15},{16,17},{18,... | collective-permute-start | bytes 6291464 | tf_op jit(solution)/shard_map/ppermute | solution.py:1327
  142.3 1.3 copy-start
  402.1 3.9 copy-start.8
  402.1 3.9 copy-start.9
  404.1 67.3 %collective-permute-start.1 = (bf16[2,512,1024]{2,1,0:T(8,128)(2,1)S(1)}, bf16[2,512,1024]{2,1,0:T(8,128)(2,1)S(1)}, u32[]{:S(2)}, u32[]{:S(2)}) collective-permute-start(bf16[2,512,1024]{2,1,0:T(8,128)(2,1)S(1)} %pad_maximum_fusion), channel_id=1, source_target_pairs={{1,0},{3,2},{5,4},{7,6},{9,8},{11,10},{13,12},{15,14},{17,16},{19,... | collective-permute-start | bytes 6291464 | tf_op jit(solution)/shard_map/ppermute | solution.py:1383
  406.6 36.1 %copy-start.11 = (bf16[1024,1024]{1,0:T(8,128)(2,1)S(1)}, bf16[1024,1024]{1,0:T(8,128)(2,1)}, u32[]{:S(2)}) copy-start(bf16[1024,1024]{1,0:T(8,128)(2,1)} %get-tuple-element.73) | copy-start | bytes 6291460
  471.4 1.3 copy-start.1
  472.7 18.2 %copy-start.10 = (f32[1,1024]{1,0:T(1,128)S(1)}, f32[1,1024]{1,0:T(1,128)}, u32[]{:S(2)}) copy-start(f32[1,1024]{1,0:T(1,128)} %get-tuple-element.76) | copy-start | bytes 12292
  472.7 19.6 %copy-start.12 = (bf16[1024,1024]{1,0:T(8,128)(2,1)S(1)}, bf16[1024,1024]{1,0:T(8,128)(2,1)}, u32[]{:S(2)}) copy-start(bf16[1024,1024]{1,0:T(8,128)(2,1)} %get-tuple-element.71) | copy-start | bytes 6291460
  501.0 58.4 %copy-start.2 = (bf16[1024,1024]{1,0:T(8,128)(2,1)S(1)}, bf16[1024,1024]{1,0:T(8,128)(2,1)}, u32[]{:S(2)}) copy-start(bf16[1024,1024]{1,0:T(8,128)(2,1)} %get-tuple-element.58) | copy-start | bytes 6291460
  551.1 9.6 %copy-start.6 = (f32[32,1024]{1,0:T(8,128)S(1)}, f32[32,1024]{1,0:T(8,128)}, u32[]{:S(2)}) copy-start(f32[32,1024]{1,0:T(8,128)} %get-tuple-element.118) | copy-start | bytes 393220
  551.1 10.2 %copy-start.4 = (f32[32,4608]{1,0:T(8,128)S(1)}, f32[32,4608]{1,0:T(8,128)}, u32[]{:S(2)}) copy-start(f32[32,4608]{1,0:T(8,128)} %get-tuple-element.119) | copy-start | bytes 1769476
  551.1 11.1 %copy-start.3 = (f32[32,4608]{1,0:T(8,128)S(1)}, f32[32,4608]{1,0:T(8,128)}, u32[]{:S(2)}) copy-start(f32[32,4608]{1,0:T(8,128)} %get-tuple-element.120) | copy-start | bytes 1769476
Sparse Core Ops, SparseCore 0:
  10.9 89.3 all-gather.2
  103.3 100.9 all-gather.4
  388.2 141.1 reduce-scatter.1

commit v6 on v5

--- a/solution.py
+++ b/solution.py
@@ -849,47 +849,70 @@
     )(ffn, d_normed, hidden, cotangent, g, w_o, mixed, totals, ones)
 
 
+def head_back(grad, raw, gains, cos, sin, ones, head):
+    grad = grad * cos + swap_halves(grad * sin, head)
+    inv = lax.rsqrt(head_sum(raw * raw, ones) * (1.0 / head) + epsilon)
+    unit = raw * inv
+    gained = jnp.sum(unit * grad, axis=0, keepdims=True)
+    scaled = grad * gains
+    shared = head_sum(unit * scaled, ones) * (1.0 / head)
+    return inv * (scaled - unit * shared), sum(
+        gained[:, i : i + LANES] for i in range(0, gained.shape[1], LANES)
+    )
+
+
+def last_q_kernel(
+    head, scale, dq_ref, raw_ref, gains_ref, cos_ref, sin_ref, ones_ref, w_ref,
+    d_ref, part_ref, gq_ref,
+):
+    @pl.when(pl.program_id(0) == 0)
+    def _():
+        gq_ref[...] = jnp.zeros_like(gq_ref)
+
+    ones = ones_ref[...]
+    wide = ones.shape[0]
+    cos, sin = spread(cos_ref[...], wide), spread(sin_ref[...], wide)
+    for c in range(0, dq_ref.shape[1], wide):
+        cols = slice(c, c + wide)
+        grad, gained = head_back(
+            dq_ref[:, cols] * scale, raw_ref[:, cols], gains_ref[:, cols], cos, sin, ones, head
+        )
+        gq_ref[...] += gained
+        d_ref[:, cols] = grad.astype(BF)
+    part_ref[...] = mm(d_ref[...], w_ref[...], NT)
+
+
 def last_kernel(
-    q_width, kv_width, head, scale,
-    dq_ref, dk_ref, dv_ref, rawq_ref, rawk_ref, gqk_ref, cos_ref, sin_ref, ones_ref, w_ref, x_ref, g_ref,
+    kv_width, head,
+    dk_ref, dv_ref, raw_ref, gains_ref, cos_ref, sin_ref, ones_ref, w_ref, part_ref, x_ref, g_ref,
     dh_ref, *refs,
 ):
-    got_ref = refs[0] if len(refs) == 6 else None
-    d_ref, in_ref, gain_ref, gq_ref, gk_ref = refs[-5:]
+    got_ref = refs[0] if len(refs) == 5 else None
+    d_ref, in_ref, gain_ref, gk_ref = refs[-4:]
 
     @pl.when(pl.program_id(0) == 0)
     def _():
         gain_ref[...] = jnp.zeros_like(gain_ref)
-        gq_ref[...] = jnp.zeros_like(gq_ref)
         gk_ref[...] = jnp.zeros_like(gk_ref)
 
     ones = ones_ref[...]
     wide = ones.shape[0]
-    cos = spread(cos_ref[...], wide)
-    sin = spread(sin_ref[...], wide)
-    qk = q_width + kv_width
-    for c in range(0, qk, wide):
+    cos, sin = spread(cos_ref[...], wide), spread(sin_ref[...], wide)
+    for c in range(0, kv_width, wide):
         cols = slice(c, c + wide)
-        if c < q_width:
-            grad, total, raw = dq_ref[:, cols] * scale, gq_ref, rawq_ref[:, cols]
-        else:
-            at = slice(c - q_width, c - q_width + wide)
-            grad, total, raw = dk_ref[:, at].astype(F32), gk_ref, rawk_ref[:, at]
-            if got_ref is not None:
-                grad += got_ref[:, at].astype(F32)
-        grad = grad * cos + swap_halves(grad * sin, head)
-        inv = lax.rsqrt(head_sum(raw * raw, ones) * (1.0 / head) + epsilon)
-        unit = raw * inv
-        gained = jnp.sum(unit * grad, axis=0, keepdims=True)
-        total[...] += sum(gained[:, i : i + LANES] for i in range(0, wide, LANES))
-        scaled = grad * gqk_ref[:, cols]
-        shared = head_sum(unit * scaled, ones) * (1.0 / head)
-        d_ref[:, cols] = (inv * (scaled - unit * shared)).astype(BF)
+        grad = dk_ref[:, cols].astype(F32)
+        if got_ref is not None:
+            grad += got_ref[:, cols].astype(F32)
+        grad, gained = head_back(
+            grad, raw_ref[:, cols], gains_ref[:, cols], cos, sin, ones, head
+        )
+        gk_ref[...] += gained
+        d_ref[:, cols] = grad.astype(BF)
     d_values = dv_ref[...].astype(F32)
     if got_ref is not None:
         d_values += got_ref[:, kv_width:].astype(F32)
-    d_ref[:, qk:] = d_values.astype(BF)
-    d_normed = mm(d_ref[...], w_ref[...], NT)
+    d_ref[:, kv_width:] = d_values.astype(BF)
+    d_normed = part_ref[...] + mm(d_ref[...], w_ref[...], NT)
     x = x_ref[...].astype(F32)
     inverse = lax.rsqrt(jnp.mean(x * x, axis=-1, keepdims=True) + epsilon)
     unit = x * inverse
@@ -899,36 +922,63 @@
     in_ref[...] = dh_ref[...] + inverse * (scaled - unit * shared)
 
 
-def last_call(dq, dk, dv, raw_q, raw_k, gqk, cos, sin, ones, w, x, g, d_hidden, head, got=()):
+def row_blocks(total):
+    block = largest_block(total, 256)
+    return total // block, lambda n: pl.BlockSpec((block, n), lambda i: (i, 0))
+
+
+def some_cols(w, first, count):
+    return pl.BlockSpec(
+        (w.shape[0], count), lambda i: (0, first // count), pipeline_mode=pl.Buffered(1)
+    )
+
+
+def last_q_call(dq, raw, gains, cos, sin, ones, w, head):
+    total, q_width = dq.shape
+    width = w.shape[0]
+    blocks, rows = row_blocks(total)
+    return pl.pallas_call(
+        functools.partial(last_q_kernel, head, head ** (-0.5)),
+        grid=(blocks,),
+        in_specs=[
+            rows(q_width), rows(q_width), resident(gains.shape), rows(LANES), rows(LANES),
+            resident(ones.shape), some_cols(w, 0, q_width),
+        ],
+        out_specs=[rows(q_width), rows(width), resident((1, LANES))],
+        out_shape=[
+            jax.ShapeDtypeStruct((total, q_width), BF),
+            jax.ShapeDtypeStruct((total, width), F32),
+            jax.ShapeDtypeStruct((1, LANES), F32),
+        ],
+        compiler_params=params(),
+        name="last_q",
+    )(dq, raw, gains, cos, sin, ones, w)
+
+
+def last_call(dk, dv, raw, gains, cos, sin, ones, w, part, x, g, d_hidden, head, got=()):
     total, width = x.shape
-    q_width, kv_width = dq.shape[1], dk.shape[1]
-    block = largest_block(total, 256)
-
-    def rows(n):
-        return pl.BlockSpec((block, n), lambda i: (i, 0))
-
+    kv_width = dk.shape[1]
+    blocks, rows = row_blocks(total)
     return pl.pallas_call(
-        functools.partial(last_kernel, q_width, kv_width, head, head ** (-0.5)),
-        grid=(total // block,),
+        functools.partial(last_kernel, kv_width, head),
+        grid=(blocks,),
         in_specs=[
-            rows(q_width), rows(kv_width), rows(kv_width), rows(q_width), rows(kv_width),
-            resident(gqk.shape), rows(LANES), rows(LANES), resident(ones.shape),
-            resident(w.shape), rows(width), resident(g.shape), rows(width),
+            rows(kv_width), rows(kv_width), rows(kv_width), resident(gains.shape), rows(LANES),
+            rows(LANES), resident(ones.shape), some_cols(w, w.shape[1] - 2 * kv_width, 2 * kv_width),
+            rows(width), rows(width), resident(g.shape), rows(width),
         ] + [rows(2 * kv_width)] * len(got),
         out_specs=[
-            rows(w.shape[1]), rows(width),
-            resident((1, width)), resident((1, LANES)), resident((1, LANES)),
+            rows(2 * kv_width), rows(width), resident((1, width)), resident((1, LANES)),
         ],
         out_shape=[
-            jax.ShapeDtypeStruct((total, w.shape[1]), BF),
+            jax.ShapeDtypeStruct((total, 2 * kv_width), BF),
             jax.ShapeDtypeStruct((total, width), F32),
             jax.ShapeDtypeStruct((1, width), F32),
             jax.ShapeDtypeStruct((1, LANES), F32),
-            jax.ShapeDtypeStruct((1, LANES), F32),
         ],
         compiler_params=params(),
         name="last",
-    )(dq, dk, dv, raw_q, raw_k, gqk, cos, sin, ones, w, x, g, d_hidden, *got)
+    )(dk, dv, raw, gains, cos, sin, ones, w, part, x, g, d_hidden, *got)
 
 
 class Place:
@@ -1392,23 +1442,30 @@
         ).reshape(total, 2 * kv_width)
         dk, dv, got = dkv[:, :kv_width], dkv[:, kv_width:], ()
     grad_o = mm(attended, d_low, TN).astype(BF)
-    d_qkv, input_grad, grad_gattn, grad_gq, grad_gk = last_call(
-        dq.reshape(total, q_width), dk, dv, raw_q, raw_k,
-        jnp.concatenate([gains_q, gains_k], axis=1), cos, sin, ones,
-        w_qkv, x, g_attn[None, :], d_hidden, head, got,
+    d_q, part, grad_gq = last_q_call(
+        dq.reshape(total, q_width), raw_q, gains_q, cos, sin, ones, w_qkv, head
     )
-    grad_qkv = mm(normed, d_qkv, TN).astype(BF)
+    grad_q = mm(normed, d_q, TN).astype(BF)
+    if own_kernels:
+        got, grad_q, part, grad_o = lax.optimization_barrier((got, grad_q, part, grad_o))
+    d_kv, input_grad, grad_gattn, grad_gk = last_call(
+        dk, dv, raw_k, gains_k, cos, sin, ones, w_qkv, part, x, g_attn[None, :], d_hidden, head, got
+    )
+    grad_kv = mm(normed, d_kv, TN).astype(BF)
     if own_kernels:
         flat = jnp.concatenate([grad_gattn, grad_gffn, grad_gq, grad_gk], axis=1).reshape(-1, LANES)
         flat = jnp.pad(flat, ((0, -flat.shape[0] % 8), (0, 0)))
-        o_pieces = [(1,) + p[1:] for p in o_pieces]
-        out_qkv, out_o, flat = scatter_call([grad_qkv, grad_o], o_pieces + qkv_pieces, 3, (flat,))
+        last_pieces = [
+            (array,) + p[1:] for array, width_of in enumerate((width, q_width, 2 * kv_width))
+            for p in col_pieces(array, share, width_of)
+        ]
+        out_o, out_q, out_kv, flat = scatter_call([grad_o, grad_q, grad_kv], last_pieces, 3, (flat,))
         flat = flat.reshape(1, -1)
         grad_gattn, grad_gffn = flat[:, :width], flat[:, width : 2 * width]
         grad_gq = flat[:, 2 * width : 2 * width + LANES]
         grad_gk = flat[:, 2 * width + LANES : 2 * width + 2 * LANES]
     else:
-        out_qkv, out_o = send(grad_qkv), send(grad_o)
+        out_q, out_kv, out_o = send(grad_q), send(grad_kv), send(grad_o)
         grad_gattn, grad_gffn, grad_gq, grad_gk = lax.psum(
             (grad_gattn, grad_gffn, grad_gq, grad_gk), AXES
         )
@@ -1419,9 +1476,9 @@
     return (
         outputs.reshape(tokens.shape),
         input_grad.reshape(tokens.shape),
-        out_qkv[:, :q_width],
-        out_qkv[:, q_width : q_width + kv_width],
-        out_qkv[:, q_width + kv_width :],
+        out_q,
+        out_kv[:, :kv_width],
+        out_kv[:, kv_width:],
         out_o,
         out_gate,
         out_up,

time: 576 us -> 567 us (0.984)
  waiting for transfers between devices: 65.7 us -> 42.2 us
  Pallas kernels: 433 us -> 448 us
    ppermute x1, waiting for transfers between devices: 23.4 us -> 0.01 us  [per_device(): got = lax.ppermute(jnp.concatenate([dk, dv], axis=2), 'ctx', [(1, 0)])]
    pallas_call x1, Pallas kernels: 50.1 us -> 59.5 us  [scatter_call(): pl.pallas_call(functools.partial(scatter_kernel, pieces, count, len(gains...]
    pallas_call x1 -> x2, Pallas kernels: 18.2 us -> 24.7 us  [the longest x1 13.3 us: last_call(): pl.pallas_call(functools.partial(last_kernel, kv_width, head), grid=(bloc...]
    dot_general x2 -> x3, matrix products: 14.1 us -> 14.6 us  [mm(): return lax.dot_general(a, b, dims, preferred_element_type=F32)]
  transfers between devices with their start and end apart: 5 -> 5, of which waited for: 2 -> 1; matrix products, arithmetic and copies ran while one was open for 7% -> 7% of each run, Pallas kernels for 44% -> 47%
where the time goes in v6:
time: 567 us; the launch traced here: 561 us
  Pallas kernels  448 us (79%)
  waiting for transfers between devices  42.2 us (7%)
  other arithmetic  17.9 us (3%)
  local copies, waits for them, and re-layouts  16.6 us (3%)
  matrix products  14.6 us (3%)
  between operations  14.1 us (2%)
  starting transfers between devices  7.16 us (1%)
    pallas_call x1, Pallas kernels, feed_call(): pl.pallas_call(functools.partial(feed_kernel, block_t, steps, block_m, he...  184 us
    pallas_call x2, Pallas kernels, gather_call(): pl.pallas_call(functools.partial(gather_kernel, pieces, count), in_specs=...  69.9 us
    pallas_call x1, Pallas kernels, scatter_call(): pl.pallas_call(functools.partial(scatter_kernel, pieces, count, len(gains...  59.5 us
    pallas_call x2, Pallas kernels, attend_back_call(): pl.pallas_call(functools.partial(attend_back_kernel, block_q, block_k, he...  49.6 us
    all_gather x2, waiting for transfers between devices, fetch(): return lax.all_gather(weight, AXES, axis=0, tiled=True)  40.8 us
    pallas_call x2, Pallas kernels, attend_call(): pl.pallas_call(functools.partial(attend_kernel, block_q, block_k, heads,...  31.3 us
    pallas_call x2, Pallas kernels, project_call(): pl.pallas_call(functools.partial(project_kernel, rope_width, head, scale)...  21.4 us
    dot_general x3, matrix products, mm(): return lax.dot_general(a, b, dims, preferred_element_type=F32)  14.6 us
  transfers between devices with their start and end apart: 5, of which 1 were waited for; matrix products, arithmetic and copies ran while one was open for 7% of the time, Pallas kernels for 47%

profile of v6, /device:TPU:0, one launch (start us, length us, event | category | flops | bytes accessed | tf_op | source)
XLA Modules:
  0.0 561.1 jit_solution(15065304200390280985)
XLA Ops:
  9.4 1.3 convert_reduce_fusion
  10.7 1.5 pad_maximum_fusion.3.refs_0_
  12.2 42.2 %gather.2 = bf16[4,2,2,2,32,2048]{5,4,3,2,1,0:T(8,128)(2,1)} custom-call(bf16[32,2048]{1,0:T(8,128)(2,1)} %pad_maximum_fusion.3.refs_0_), custom_call_target="tpu_custom_call" | custom-call | tf_op jit(solution)/shard_map/gather/pallas_call | solution.py:1098
  55.2 1.9 fusion
  57.1 1.8 pad_maximum_fusion.1
  59.7 9.1 %project_kv.1 = (bf16[1024,1024]{1,0:T(8,128)(2,1)}, bf16[1024,1024]{1,0:T(8,128)(2,1)}, f32[1024,512]{1,0:T(8,128)}) custom-call(bf16[1024,1024]{1,0:T(8,128)(2,1)} %bitcast.43, bf16[1024,2048]{1,0:T(8,128)(2,1)} %bitcast.39, f32[1,1024]{1,0:T(1,128)} %bitcast.75, f32[1,512]{1,0:T(1,128)} %bitcast.69, f32[1024,128]{1,0:T(8,128)} %get-tuple-element.112.cos_ref, ...), custom_call_target="tpu_custom_call" | custom-call | flops 2147483648 | bytes 12582912 | tf_op jit(solution)/shard_map/project_kv/pallas_call | solution.py:103
  68.8 5.8 %collective-permute-start = (bf16[2,512,1024]{2,1,0:T(8,128)(2,1)}, bf16[2,512,1024]{2,1,0:T(8,128)(2,1)S(1)}, u32[]{:S(2)}, u32[]{:S(2)}) collective-permute-start(bf16[2,512,1024]{2,1,0:T(8,128)(2,1)} %bitcast.82), channel_id=1, source_target_pairs={{0,1},{2,3},{4,5},{6,7},{8,9},{10,11},{12,13},{14,15},{16,17},{18,... | collective-permute-start | bytes 6291464 | tf_op jit(solution)/shard_map/ppermute | solution.py:1377
  75.3 1.0 copy.32.first_ref
  76.3 12.3 %project_q.1 = (bf16[1024,1024]{1,0:T(8,128)(2,1)}, bf16[1024,1024]{1,0:T(8,128)(2,1)}, f32[1024,1024]{1,0:T(8,128)}) custom-call(bf16[1024,1024]{1,0:T(8,128)(2,1)} %bitcast.44, bf16[1024,2048]{1,0:T(8,128)(2,1)} %bitcast.40, f32[1,1024]{1,0:T(1,128)} %bitcast.76, f32[1,1024]{1,0:T(1,128)} %bitcast.66, f32[1024,128]{1,0:T(8,128)} %get-tuple-element.112.cos_ref, ...), custom_call_target="tpu_custom_call" | custom-call | flops 2147483648 | bytes 12582912 | tf_op jit(solution)/shard_map/project_q/pallas_call | solution.py:103
  89.9 19.9 %attend.2 = (f32[2,512,1024]{2,1,0:T(8,128)}, f32[2,512,1024]{2,1,0:T(8,128)}) custom-call(s32[2,2]{1,0:T(2,128)} %get-tuple-element.110.low_ref, s32[2,2]{1,0:T(2,128)} %broadcast_in_dim.15.high_ref, s32[1]{0:T(128)} %constant.83.clone.1.start_ref, bf16[2,512,1024]{2,1,0:T(8,128)(2,1)} %bitcast.53, bf16[2,512,1024]{2,1,0:T(8,128)(2,1)} %bitcast.83, ...), custom_call_target="tpu_custom_call" | custom-call | flops 2147483648 | bytes 16777216 | tf_op jit(solution)/shard_map/attend/pallas_call | solution.py:202
  109.7 27.7 %gather.3 = bf16[4,2,2,2,32,1024]{5,4,3,2,1,0:T(8,128)(2,1)} custom-call(bf16[32,1024]{1,0:T(8,128)(2,1)} %refs_0_), custom_call_target="tpu_custom_call" | custom-call | tf_op jit(solution)/shard_map/gather/pallas_call | solution.py:1098
  137.4 1.0 copy.33.first_ref
  138.5 3.9 bitcast_convert_fusion.c_ref
  143.6 11.5 %attend.3 = (f32[2,512,1024]{2,1,0:T(8,128)}, f32[2,512,1024]{2,1,0:T(8,128)}) custom-call(s32[2,2]{1,0:T(2,128)} %get-tuple-element.111.low_ref, s32[2,2]{1,0:T(2,128)} %broadcast_14_high_ref.2.high_ref, s32[1]{0:T(128)} %constant.76.clone.1.start_ref, bf16[2,512,1024]{2,1,0:T(8,128)(2,1)} %bitcast.54, bf16[2,512,1024]{2,1,0:T(8,128)(2,1)} %copy-done, ...), custom_call_target="tpu_custom_call" | custom-call | flops 2147483648 | bytes 16777216 | tf_op jit(solution)/shard_map/attend/pallas_call | solution.py:202
  155.1 8.3 %hidden.1 = (bf16[1024,1024]{1,0:T(8,128)(2,1)}, f32[1024,1024]{1,0:T(8,128)}, bf16[1024,1024]{1,0:T(8,128)(2,1)}) custom-call(f32[1024,1024]{1,0:T(8,128)} %bitcast.51, bf16[1024,1024]{1,0:T(8,128)(2,1)} %bitcast.47, bf16[1024,1024]{1,0:T(8,128)(2,1)} %bitcast.45, f32[1,1024]{1,0:T(1,128)} %bitcast.73), custom_call_target="tpu_custom_call" | custom-call | tf_op jit(solution)/shard_map/hidden/pallas_call | solution.py:380
  163.4 40.8 %all-gather.5.cloned.1.call-done.wd_ref = bf16[4608,1024]{1,0:T(8,128)(2,1)} async-done(((bf16[144,1024]{1,0:T(8,128)(2,1)}), bf16[4608,1024]{1,0:T(8,128)(2,1)}) %all-gather.5.cloned.1.call-update) | async-done | bytes 9437200 | tf_op jit(solution)/shard_map/all_gather | solution.py:1338
  204.3 183.6 %feed.1 = (bf16[4608,1024]{1,0:T(8,128)(2,1)}, f32[32,4608]{1,0:T(8,128)}, f32[32,4608]{1,0:T(8,128)}, bf16[4,2,2,2,32,4608]{5,4,3,2,1,0:T(8,128)(2,1)}, bf16[10...) custom-call(bf16[1024,1024]{1,0:T(8,128)(2,1)} %get-tuple-element.62, ...), custom_call_target="tpu_custom_call" | custom-call | flops 86973087744 | bytes 56623104 | tf_op jit(solution)/shard_map/feed/pallas_call | solution.py:732
  388.5 13.5 %attend_back.2 = (f32[2,512,1024]{2,1,0:T(8,128)}, bf16[2,512,512]{2,1,0:T(8,128)(2,1)}, bf16[2,512,512]{2,1,0:T(8,128)(2,1)}) custom-call(s32[2,2]{1,0:T(2,128)} %get-tuple-element.111.low_ref, s32[2,2]{1,0:T(2,128)} %broadcast_14_high_ref.2.high_ref, s32[1]{0:T(128)} %constant.76.clone.1.start_ref, bf16[2,512,1024]{2,1,0:T(8,128)(2,1)} %bitcast.55, ...), custom_call_target="tpu_custom_call" | custom-call | flops 5368709120 | bytes 16777216 | tf_op jit(solution)/shard_map/attend_back/pallas_call | solution.py:331
  402.1 1.9 pad_maximum_fusion
  404.0 1.3 collective-permute-start.1
  405.9 36.1 %attend_back.3 = (f32[2,512,1024]{2,1,0:T(8,128)}, bf16[2,512,512]{2,1,0:T(8,128)(2,1)}, bf16[2,512,512]{2,1,0:T(8,128)(2,1)}) custom-call(s32[2,2]{1,0:T(2,128)} %get-tuple-element.110.low_ref, s32[2,2]{1,0:T(2,128)} %broadcast_in_dim.15.high_ref, s32[1]{0:T(128)} %constant.83.clone.1.start_ref, bf16[2,512,1024]{2,1,0:T(8,128)(2,1)} %bitcast.56, ...), custom_call_target="tpu_custom_call" | custom-call | flops 5368709120 | bytes 16777216 | tf_op jit(solution)/shard_map/attend_back/pallas_call | solution.py:331
  442.0 11.5 %last_q.1 = (bf16[1024,1024]{1,0:T(8,128)(2,1)}, f32[1024,1024]{1,0:T(8,128)}, f32[1,128]{1,0:T(1,128)}) custom-call(f32[1024,1024]{1,0:T(8,128)} %bitcast.50, f32[1024,1024]{1,0:T(8,128)} %get-tuple-element.76.raw_ref, f32[1,1024]{1,0:T(1,128)} %bitcast.67, f32[1024,128]{1,0:T(8,128)} %get-tuple-element.112.cos_ref, ...), custom_call_target="tpu_custom_call" | custom-call | tf_op jit(solution)/shard_map/last_q/pallas_call | solution.py:940
  453.5 5.5 convolution_convert_fusion.1
  458.9 3.8 convolution_convert_fusion.2
  462.7 1.3 copy-done.1
  464.0 13.3 %last.1 = (bf16[1024,1024]{1,0:T(8,128)(2,1)}, f32[1024,1024]{1,0:T(8,128)}, f32[1,1024]{1,0:T(1,128)}, f32[1,128]{1,0:T(1,128)}) custom-call(bf16[1024,512]{1,0:T(8,128)(2,1)} %bitcast.62, bf16[1024,512]{1,0:T(8,128)(2,1)} %bitcast.63, f32[1024,512]{1,0:T(8,128)} %get-tuple-element.71.raw_ref, f32[1,512]{1,0:T(1,128)} %bitcast.70, ...), custom_call_target="tpu_custom_call" | custom-call | tf_op jit(solution)/shard_map/last/pallas_call | solution.py:962
  478.6 5.3 convolution_convert_fusion
  484.0 59.5 %scatter.1 = (f32[32,1024]{1,0:T(8,128)}, f32[32,1024]{1,0:T(8,128)}, f32[32,1024]{1,0:T(8,128)}, f32[24,128]{1,0:T(8,128)}) custom-call(bf16[4,2,2,2,32,1024]{5,4,3,2,1,0:T(8,128)(2,1)} %bitcast.59, bf16[4,2,2,2,32,1024]{5,4,3,2,1,0:T(8,128)(2,1)} %bitcast.60, bf16[4,2,2,2,32,1024]{5,4,3,2,1,0:T(8,128)(2,1)} %bitcast.61, f32[24,128]{1,0:T(8,128)} %pad.4.refs_3_), custom_call_target="tpu_custom_call" | custom-call | tf_op jit(solution)/shard_map/scatter/pallas_call | solution.py:1281
  545.4 1.3 fusion.3
  546.7 1.5 fusion.2
  548.2 1.8 convert_element_type.49
  550.1 1.3 copy.40
  (67 shorter events, 14.4 us)
Async XLA Ops:
  7.2 156.3 %all-gather.3.cloned.1.call-start = ((), (), s32[]{:S(2)}) async-start(), calls=%async_computation.1 | async-start | bytes 9732096 | tf_op jit(solution)/shard_map/all_gather | solution.py:1338
  7.9 196.4 %all-gather.5.cloned.1.call-start = ((), (), s32[]{:S(2)}) async-start(), calls=%async_computation.2 | async-start | bytes 9732096 | tf_op jit(solution)/shard_map/all_gather | solution.py:1338
  8.7 539.6 %reduce-scatter.2.cloned.1.call-start = ((), (), s32[]{:S(2)}) async-start(), calls=%async_computation.3 | async-start | bytes 9732096 | tf_op jit(solution)/shard_map/reduce_scatter | solution.py:1341
  12.2 42.2 %copy-start.8 = (f32[64]{0:T(128)S(1)}, f32[64]{0:T(128)}, u32[]{:S(2)}) copy-start(f32[64]{0:T(128)} %param.26) | copy-start | bytes 772
  59.7 15.0 %copy-start.5 = (f32[64]{0:T(128)S(1)}, f32[64]{0:T(128)}, u32[]{:S(2)}) copy-start(f32[64]{0:T(128)} %param.25) | copy-start | bytes 772
  68.8 73.6 %collective-permute-start = (bf16[2,512,1024]{2,1,0:T(8,128)(2,1)}, bf16[2,512,1024]{2,1,0:T(8,128)(2,1)S(1)}, u32[]{:S(2)}, u32[]{:S(2)}) collective-permute-start(bf16[2,512,1024]{2,1,0:T(8,128)(2,1)} %bitcast.82), channel_id=1, source_target_pairs={{0,1},{2,3},{4,5},{6,7},{8,9},{10,11},{12,13},{14,15},{16,17},{18,... | collective-permute-start | bytes 6291464 | tf_op jit(solution)/shard_map/ppermute | solution.py:1377
  142.3 1.3 copy-start
  404.0 58.7 %collective-permute-start.1 = (bf16[2,512,1024]{2,1,0:T(8,128)(2,1)S(1)}, bf16[2,512,1024]{2,1,0:T(8,128)(2,1)S(1)}, u32[]{:S(2)}, u32[]{:S(2)}) collective-permute-start(bf16[2,512,1024]{2,1,0:T(8,128)(2,1)S(1)} %pad_maximum_fusion), channel_id=1, source_target_pairs={{1,0},{3,2},{5,4},{7,6},{9,8},{11,10},{13,12},{15,14},{17,16},{19,... | collective-permute-start | bytes 6291464 | tf_op jit(solution)/shard_map/ppermute | solution.py:1433
  441.9 11.5 %copy-start.11 = (bf16[1024,1024]{1,0:T(8,128)(2,1)S(1)}, bf16[1024,1024]{1,0:T(8,128)(2,1)}, u32[]{:S(2)}) copy-start(bf16[1024,1024]{1,0:T(8,128)(2,1)} %get-tuple-element.79) | copy-start | bytes 6291460
  453.4 5.5 copy-start.12
  453.4 5.5 copy-start.13
  462.7 1.3 copy-start.1
  464.0 13.3 %copy-start.9 = (f32[1,1024]{1,0:T(1,128)S(1)}, f32[1,1024]{1,0:T(1,128)}, u32[]{:S(2)}) copy-start(f32[1,1024]{1,0:T(1,128)} %get-tuple-element.89) | copy-start | bytes 12292
  464.0 13.3 %copy-start.10 = (f32[1,128]{1,0:T(1,128)S(1)}, f32[1,128]{1,0:T(1,128)}, u32[]{:S(2)}) copy-start(f32[1,128]{1,0:T(1,128)} %get-tuple-element.90) | copy-start | bytes 1540
  464.0 14.6 %copy-start.14 = (bf16[1024,1024]{1,0:T(8,128)(2,1)S(1)}, bf16[1024,1024]{1,0:T(8,128)(2,1)}, u32[]{:S(2)}) copy-start(bf16[1024,1024]{1,0:T(8,128)(2,1)} %get-tuple-element.74) | copy-start | bytes 6291460
  484.0 66.1 %copy-start.2 = (bf16[1024,1024]{1,0:T(8,128)(2,1)S(1)}, bf16[1024,1024]{1,0:T(8,128)(2,1)}, u32[]{:S(2)}) copy-start(bf16[1024,1024]{1,0:T(8,128)(2,1)} %get-tuple-element.65) | copy-start | bytes 6291460
  550.1 1.3 copy-start.7
  550.1 2.0 copy-start.6
  550.1 2.7 copy-start.4
  550.1 3.5 copy-start.3
Sparse Core Ops, SparseCore 0:
  10.9 89.3 all-gather.2
  103.3 100.9 all-gather.4
  388.1 143.6 reduce-scatter.1

commit v7 on v6

--- a/solution.py
+++ b/solution.py
@@ -1307,7 +1307,7 @@
     )(*grads, *gains)
 
 
-def col_pieces(array, rows, cols, width=512, high=None):
+def col_pieces(array, rows, cols, width=256, high=None):
     high = high or rows
     return [
         (array, slice(r, r + high), slice(c, c + width), (c // width) % 2 == 0)

time: 567 us -> 566 us (level)
  no operation moved by 1% of the time
where the time goes in v7:
time: 566 us; the launch traced here: 561 us
  Pallas kernels  448 us (79%)
  waiting for transfers between devices  46.4 us (8%)
  other arithmetic  17.9 us (3%)
  local copies, waits for them, and re-layouts  16.6 us (3%)
  matrix products  14.6 us (3%)
  between operations  14.1 us (2%)
    pallas_call x1, Pallas kernels, feed_call(): pl.pallas_call(functools.partial(feed_kernel, block_t, steps, block_m, he...  184 us
    pallas_call x2, Pallas kernels, gather_call(): pl.pallas_call(functools.partial(gather_kernel, pieces, count), in_specs=...  70.8 us
    pallas_call x1, Pallas kernels, scatter_call(): pl.pallas_call(functools.partial(scatter_kernel, pieces, count, len(gains...  57.7 us
    pallas_call x2, Pallas kernels, attend_back_call(): pl.pallas_call(functools.partial(attend_back_kernel, block_q, block_k, he...  49.6 us
    all_gather x2, waiting for transfers between devices, fetch(): return lax.all_gather(weight, AXES, axis=0, tiled=True)  45 us
    pallas_call x2, Pallas kernels, attend_call(): pl.pallas_call(functools.partial(attend_kernel, block_q, block_k, heads,...  31.3 us
    pallas_call x2, Pallas kernels, project_call(): pl.pallas_call(functools.partial(project_kernel, rope_width, head, scale)...  21.4 us
    dot_general x3, matrix products, mm(): return lax.dot_general(a, b, dims, preferred_element_type=F32)  14.6 us
  transfers between devices with their start and end apart: 5, of which 1 were waited for; matrix products, arithmetic and copies ran while one was open for 7% of the time, Pallas kernels for 47%

profile of v7, /device:TPU:0, one launch (start us, length us, event | category | flops | bytes accessed | tf_op | source)
XLA Modules:
  0.0 560.6 jit_solution(17089554906069118519)
XLA Ops:
  9.4 1.3 convert_reduce_fusion
  10.7 1.5 pad_maximum_fusion.3.refs_0_
  12.2 37.4 %gather.2 = bf16[4,2,2,2,32,2048]{5,4,3,2,1,0:T(8,128)(2,1)} custom-call(bf16[32,2048]{1,0:T(8,128)(2,1)} %pad_maximum_fusion.3.refs_0_), custom_call_target="tpu_custom_call" | custom-call | tf_op jit(solution)/shard_map/gather/pallas_call | solution.py:1098
  50.3 1.9 fusion
  52.2 1.8 pad_maximum_fusion.1
  54.8 9.1 %project_kv.1 = (bf16[1024,1024]{1,0:T(8,128)(2,1)}, bf16[1024,1024]{1,0:T(8,128)(2,1)}, f32[1024,512]{1,0:T(8,128)}) custom-call(bf16[1024,1024]{1,0:T(8,128)(2,1)} %bitcast.43, bf16[1024,2048]{1,0:T(8,128)(2,1)} %bitcast.39, f32[1,1024]{1,0:T(1,128)} %bitcast.75, f32[1,512]{1,0:T(1,128)} %bitcast.69, f32[1024,128]{1,0:T(8,128)} %get-tuple-element.112.cos_ref, ...), custom_call_target="tpu_custom_call" | custom-call | flops 2147483648 | bytes 12582912 | tf_op jit(solution)/shard_map/project_kv/pallas_call | solution.py:103
  63.9 1.9 collective-permute-start
  66.7 1.0 copy.32.first_ref
  67.7 12.3 %project_q.1 = (bf16[1024,1024]{1,0:T(8,128)(2,1)}, bf16[1024,1024]{1,0:T(8,128)(2,1)}, f32[1024,1024]{1,0:T(8,128)}) custom-call(bf16[1024,1024]{1,0:T(8,128)(2,1)} %bitcast.44, bf16[1024,2048]{1,0:T(8,128)(2,1)} %bitcast.40, f32[1,1024]{1,0:T(1,128)} %bitcast.76, f32[1,1024]{1,0:T(1,128)} %bitcast.66, f32[1024,128]{1,0:T(8,128)} %get-tuple-element.112.cos_ref, ...), custom_call_target="tpu_custom_call" | custom-call | flops 2147483648 | bytes 12582912 | tf_op jit(solution)/shard_map/project_q/pallas_call | solution.py:103
  81.2 19.9 %attend.2 = (f32[2,512,1024]{2,1,0:T(8,128)}, f32[2,512,1024]{2,1,0:T(8,128)}) custom-call(s32[2,2]{1,0:T(2,128)} %get-tuple-element.110.low_ref, s32[2,2]{1,0:T(2,128)} %broadcast_in_dim.15.high_ref, s32[1]{0:T(128)} %constant.83.clone.1.start_ref, bf16[2,512,1024]{2,1,0:T(8,128)(2,1)} %bitcast.53, bf16[2,512,1024]{2,1,0:T(8,128)(2,1)} %bitcast.83, ...), custom_call_target="tpu_custom_call" | custom-call | flops 2147483648 | bytes 16777216 | tf_op jit(solution)/shard_map/attend/pallas_call | solution.py:202
  101.1 33.4 %gather.3 = bf16[4,2,2,2,32,1024]{5,4,3,2,1,0:T(8,128)(2,1)} custom-call(bf16[32,1024]{1,0:T(8,128)(2,1)} %refs_0_), custom_call_target="tpu_custom_call" | custom-call | tf_op jit(solution)/shard_map/gather/pallas_call | solution.py:1098
  134.5 1.0 copy.33.first_ref
  135.5 3.9 bitcast_convert_fusion.c_ref
  140.7 11.5 %attend.3 = (f32[2,512,1024]{2,1,0:T(8,128)}, f32[2,512,1024]{2,1,0:T(8,128)}) custom-call(s32[2,2]{1,0:T(2,128)} %get-tuple-element.111.low_ref, s32[2,2]{1,0:T(2,128)} %broadcast_14_high_ref.2.high_ref, s32[1]{0:T(128)} %constant.76.clone.1.start_ref, bf16[2,512,1024]{2,1,0:T(8,128)(2,1)} %bitcast.54, bf16[2,512,1024]{2,1,0:T(8,128)(2,1)} %copy-done, ...), custom_call_target="tpu_custom_call" | custom-call | flops 2147483648 | bytes 16777216 | tf_op jit(solution)/shard_map/attend/pallas_call | solution.py:202
  152.2 8.3 %hidden.1 = (bf16[1024,1024]{1,0:T(8,128)(2,1)}, f32[1024,1024]{1,0:T(8,128)}, bf16[1024,1024]{1,0:T(8,128)(2,1)}) custom-call(f32[1024,1024]{1,0:T(8,128)} %bitcast.51, bf16[1024,1024]{1,0:T(8,128)(2,1)} %bitcast.47, bf16[1024,1024]{1,0:T(8,128)(2,1)} %bitcast.45, f32[1,1024]{1,0:T(1,128)} %bitcast.73), custom_call_target="tpu_custom_call" | custom-call | tf_op jit(solution)/shard_map/hidden/pallas_call | solution.py:380
  160.5 45.0 %all-gather.5.cloned.1.call-done.wd_ref = bf16[4608,1024]{1,0:T(8,128)(2,1)} async-done(((bf16[144,1024]{1,0:T(8,128)(2,1)}), bf16[4608,1024]{1,0:T(8,128)(2,1)}) %all-gather.5.cloned.1.call-update) | async-done | bytes 9437200 | tf_op jit(solution)/shard_map/all_gather | solution.py:1338
  205.5 183.6 %feed.1 = (bf16[4608,1024]{1,0:T(8,128)(2,1)}, f32[32,4608]{1,0:T(8,128)}, f32[32,4608]{1,0:T(8,128)}, bf16[4,2,2,2,32,4608]{5,4,3,2,1,0:T(8,128)(2,1)}, bf16[10...) custom-call(bf16[1024,1024]{1,0:T(8,128)(2,1)} %get-tuple-element.62, ...), custom_call_target="tpu_custom_call" | custom-call | flops 86973087744 | bytes 56623104 | tf_op jit(solution)/shard_map/feed/pallas_call | solution.py:732
  389.7 13.5 %attend_back.2 = (f32[2,512,1024]{2,1,0:T(8,128)}, bf16[2,512,512]{2,1,0:T(8,128)(2,1)}, bf16[2,512,512]{2,1,0:T(8,128)(2,1)}) custom-call(s32[2,2]{1,0:T(2,128)} %get-tuple-element.111.low_ref, s32[2,2]{1,0:T(2,128)} %broadcast_14_high_ref.2.high_ref, s32[1]{0:T(128)} %constant.76.clone.1.start_ref, bf16[2,512,1024]{2,1,0:T(8,128)(2,1)} %bitcast.55, ...), custom_call_target="tpu_custom_call" | custom-call | flops 5368709120 | bytes 16777216 | tf_op jit(solution)/shard_map/attend_back/pallas_call | solution.py:331
  403.3 1.9 pad_maximum_fusion
  405.2 1.3 collective-permute-start.1
  407.1 36.1 %attend_back.3 = (f32[2,512,1024]{2,1,0:T(8,128)}, bf16[2,512,512]{2,1,0:T(8,128)(2,1)}, bf16[2,512,512]{2,1,0:T(8,128)(2,1)}) custom-call(s32[2,2]{1,0:T(2,128)} %get-tuple-element.110.low_ref, s32[2,2]{1,0:T(2,128)} %broadcast_in_dim.15.high_ref, s32[1]{0:T(128)} %constant.83.clone.1.start_ref, bf16[2,512,1024]{2,1,0:T(8,128)(2,1)} %bitcast.56, ...), custom_call_target="tpu_custom_call" | custom-call | flops 5368709120 | bytes 16777216 | tf_op jit(solution)/shard_map/attend_back/pallas_call | solution.py:331
  443.1 11.5 %last_q.1 = (bf16[1024,1024]{1,0:T(8,128)(2,1)}, f32[1024,1024]{1,0:T(8,128)}, f32[1,128]{1,0:T(1,128)}) custom-call(f32[1024,1024]{1,0:T(8,128)} %bitcast.50, f32[1024,1024]{1,0:T(8,128)} %get-tuple-element.76.raw_ref, f32[1,1024]{1,0:T(1,128)} %bitcast.67, f32[1024,128]{1,0:T(8,128)} %get-tuple-element.112.cos_ref, ...), custom_call_target="tpu_custom_call" | custom-call | tf_op jit(solution)/shard_map/last_q/pallas_call | solution.py:940
  454.6 5.5 convolution_convert_fusion.1
  460.1 3.8 convolution_convert_fusion.2
  463.9 1.3 copy-done.1
  465.2 13.4 %last.1 = (bf16[1024,1024]{1,0:T(8,128)(2,1)}, f32[1024,1024]{1,0:T(8,128)}, f32[1,1024]{1,0:T(1,128)}, f32[1,128]{1,0:T(1,128)}) custom-call(bf16[1024,512]{1,0:T(8,128)(2,1)} %bitcast.62, bf16[1024,512]{1,0:T(8,128)(2,1)} %bitcast.63, f32[1024,512]{1,0:T(8,128)} %get-tuple-element.71.raw_ref, f32[1,512]{1,0:T(1,128)} %bitcast.70, ...), custom_call_target="tpu_custom_call" | custom-call | tf_op jit(solution)/shard_map/last/pallas_call | solution.py:962
  479.9 5.4 convolution_convert_fusion
  485.3 57.7 %scatter.1 = (f32[32,1024]{1,0:T(8,128)}, f32[32,1024]{1,0:T(8,128)}, f32[32,1024]{1,0:T(8,128)}, f32[24,128]{1,0:T(8,128)}) custom-call(bf16[4,2,2,2,32,1024]{5,4,3,2,1,0:T(8,128)(2,1)} %bitcast.59, bf16[4,2,2,2,32,1024]{5,4,3,2,1,0:T(8,128)(2,1)} %bitcast.60, bf16[4,2,2,2,32,1024]{5,4,3,2,1,0:T(8,128)(2,1)} %bitcast.61, f32[24,128]{1,0:T(8,128)} %pad.4.refs_3_), custom_call_target="tpu_custom_call" | custom-call | tf_op jit(solution)/shard_map/scatter/pallas_call | solution.py:1281
  544.9 1.3 fusion.3
  546.2 1.5 fusion.2
  547.8 1.8 convert_element_type.49
  549.6 1.3 copy.40
  (67 shorter events, 14.4 us)
Async XLA Ops:
  7.2 153.3 %all-gather.3.cloned.1.call-start = ((), (), s32[]{:S(2)}) async-start(), calls=%async_computation.1 | async-start | bytes 9732096 | tf_op jit(solution)/shard_map/all_gather | solution.py:1338
  7.9 197.6 %all-gather.5.cloned.1.call-start = ((), (), s32[]{:S(2)}) async-start(), calls=%async_computation.2 | async-start | bytes 9732096 | tf_op jit(solution)/shard_map/all_gather | solution.py:1338
  8.7 539.1 %reduce-scatter.2.cloned.1.call-start = ((), (), s32[]{:S(2)}) async-start(), calls=%async_computation.3 | async-start | bytes 9732096 | tf_op jit(solution)/shard_map/reduce_scatter | solution.py:1341
  12.2 37.4 %copy-start.8 = (f32[64]{0:T(128)S(1)}, f32[64]{0:T(128)}, u32[]{:S(2)}) copy-start(f32[64]{0:T(128)} %param.26) | copy-start | bytes 772
  54.8 11.1 %copy-start.5 = (f32[64]{0:T(128)S(1)}, f32[64]{0:T(128)}, u32[]{:S(2)}) copy-start(f32[64]{0:T(128)} %param.25) | copy-start | bytes 772
  63.9 75.5 %collective-permute-start = (bf16[2,512,1024]{2,1,0:T(8,128)(2,1)}, bf16[2,512,1024]{2,1,0:T(8,128)(2,1)S(1)}, u32[]{:S(2)}, u32[]{:S(2)}) collective-permute-start(bf16[2,512,1024]{2,1,0:T(8,128)(2,1)} %bitcast.82), channel_id=1, source_target_pairs={{0,1},{2,3},{4,5},{6,7},{8,9},{10,11},{12,13},{14,15},{16,17},{18,... | collective-permute-start | bytes 6291464 | tf_op jit(solution)/shard_map/ppermute | solution.py:1377
  139.4 1.3 copy-start
  405.2 58.7 %collective-permute-start.1 = (bf16[2,512,1024]{2,1,0:T(8,128)(2,1)S(1)}, bf16[2,512,1024]{2,1,0:T(8,128)(2,1)S(1)}, u32[]{:S(2)}, u32[]{:S(2)}) collective-permute-start(bf16[2,512,1024]{2,1,0:T(8,128)(2,1)S(1)} %pad_maximum_fusion), channel_id=1, source_target_pairs={{1,0},{3,2},{5,4},{7,6},{9,8},{11,10},{13,12},{15,14},{17,16},{19,... | collective-permute-start | bytes 6291464 | tf_op jit(solution)/shard_map/ppermute | solution.py:1433
  443.1 11.5 %copy-start.11 = (bf16[1024,1024]{1,0:T(8,128)(2,1)S(1)}, bf16[1024,1024]{1,0:T(8,128)(2,1)}, u32[]{:S(2)}) copy-start(bf16[1024,1024]{1,0:T(8,128)(2,1)} %get-tuple-element.79) | copy-start | bytes 6291460
  454.6 5.5 copy-start.12
  454.6 5.5 copy-start.13
  463.9 1.3 copy-start.1
  465.2 13.4 %copy-start.9 = (f32[1,1024]{1,0:T(1,128)S(1)}, f32[1,1024]{1,0:T(1,128)}, u32[]{:S(2)}) copy-start(f32[1,1024]{1,0:T(1,128)} %get-tuple-element.89) | copy-start | bytes 12292
  465.2 13.4 %copy-start.10 = (f32[1,128]{1,0:T(1,128)S(1)}, f32[1,128]{1,0:T(1,128)}, u32[]{:S(2)}) copy-start(f32[1,128]{1,0:T(1,128)} %get-tuple-element.90) | copy-start | bytes 1540
  465.2 14.7 %copy-start.14 = (bf16[1024,1024]{1,0:T(8,128)(2,1)S(1)}, bf16[1024,1024]{1,0:T(8,128)(2,1)}, u32[]{:S(2)}) copy-start(bf16[1024,1024]{1,0:T(8,128)(2,1)} %get-tuple-element.74) | copy-start | bytes 6291460
  485.3 64.3 %copy-start.2 = (bf16[1024,1024]{1,0:T(8,128)(2,1)S(1)}, bf16[1024,1024]{1,0:T(8,128)(2,1)}, u32[]{:S(2)}) copy-start(bf16[1024,1024]{1,0:T(8,128)(2,1)} %get-tuple-element.65) | copy-start | bytes 6291460
  549.6 1.3 copy-start.7
  549.6 2.0 copy-start.6
  549.6 2.7 copy-start.4
  549.6 3.5 copy-start.3
Sparse Core Ops, SparseCore 0:
  10.9 87.0 all-gather.2
  100.9 104.5 all-gather.4
  389.3 144.9 reduce-scatter.1
